TPU v7x, 256 devices: a whole 4x4x8 slice. The times are simulated.
256 devices in a mesh: src: 64 (over y_hi, z, x), row: 4 (over y_lo, core).
Axes of the slice: x: 4, y: 4 (y_hi: 2, y_lo: 2; y = y_hi * 2 + y_lo), z: 8, core: 2. Of those that a mesh axis runs over, the one named last changes fastest.
Arguments:
- right_side: float32 [2, 8192, 16384], P(None, 'row', 'src'), may hold values from -6 to 6
- pivot_inverse: float32 [2, 2, 512, 512], P(None, None, 'src')
- ancestor_panel: float32 [2, 2, 4096, 512], P(None, None, ('row', 'src')), may hold values from -0.1875 to 0.1875
- ancestors: int32 [2, 4096], P(None, 'row'), may hold values from -1 to 2047, as said below
- pivot_block: int32 [2], replicated, may hold values from 0 to 15, as said below
Outputs:
- forward: float32 [2, 8192, 16384], P(None, 'row', 'src')
Inputs may be any that keep to these rules, and one draw needn't show every extreme that they name: pivot_block holds 2 distinct blocks of 512 rows; one of them is always the last block. `ancestors`: for supernode k and row device r, slots r * 1024 to r * 1024 + 1023 hold distinct rising local rows of that device followed by -1 in the remaining slots; they never touch the pivot rows of supernodes 0 to k, and for k below 1 they include every pivot row of supernode k + 1 that lies on that device; for each supernode some row device fills all 1024 slots.
All inputs are finite; a program needn't handle non-finite values.
Results may differ from a plain program's by a relative error of at most 0.0001.
Values sent between devices are 32-bit elements; how exact they have to be, the bound alone decides.
No kernel may reach another device: no remote copies, remote signals or barrier semaphores. Data moves between devices by JAX's collectives and lax.ppermute only.
A program may use at most 128 MiB of HBM per device.

v0:
```python
import functools

import jax
import jax.numpy as jnp
from jax import lax
from jax.experimental import pallas as pl
from jax.experimental.pallas import tpu as pltpu
from jax.sharding import Mesh, PartitionSpec as P


SIZES = {"yh": 2, "z": 8, "x": 4, "yl": 2, "c": 2}
SRC = ("yh", "z", "x")
ROW = ("yl", "c")
MIB = 1024 * 1024
cat = jnp.concatenate


def send(value, axis, shift):
    size = SIZES[axis]
    return lax.ppermute(value, axis, [(i, (i + shift) % size) for i in range(size)])


def send_apart(value, axis, hops):
    size = SIZES[axis]
    pairs = [
        (i * 2 + core, (i + hops * (1 - 2 * core)) % size * 2 + core) for i in range(size) for core in range(2)
    ]
    return lax.ppermute(value, (axis, "c"), pairs)


def swap(value):
    return send(value, "c", 1)


def step_of(i):
    return ((i + 1) >> 1) * (1 - 2 * (i & 1))


def source(piece, x_outer):
    yh, z, x, sign = lax.axis_index("yh"), lax.axis_index("z"), lax.axis_index("x"), 1 - 2 * lax.axis_index("c")
    if x_outer:
        dx, dz = step_of(piece >> 4) * sign, step_of((piece >> 1) & 7)
    else:
        dz, dx = step_of(piece >> 3) * sign, step_of((piece >> 1) & 3)
    return ((yh + piece) & 1) * 32 + ((z + dz) & 7) * 4 + ((x + dx) & 3)


def owner_of(block):
    row = lax.axis_index("yl") * 2 + lax.axis_index("c")
    return block >> 2 == row, pl.multiple_of((block & 3) * 512, 512)


def prepare_kernel(inverse_ref, panel_ref, panel0_ref, own_b_ref):
    core = lax.axis_index("c")
    for node in range(2):
        own_b_ref[0, node * 8 : node * 8 + 8, :] = inverse_ref[node, core]
    for part in range(2):
        panel0_ref[0, part * 16 : part * 16 + 16, :] = panel_ref[0, part]
        own_b_ref[0, 16 + part * 16 : 32 + part * 16, :] = panel_ref[1, part]


def prepare(inverse, panel):
    depth = panel.shape[3]
    return pl.pallas_call(
        prepare_kernel,
        out_shape=[jax.ShapeDtypeStruct((1, rows, depth), jnp.float32) for rows in (32, 48)],
        compiler_params=pltpu.CompilerParams(vmem_limit_bytes=4 * MIB),
        name="prepare",
    )(inverse, panel)


def take_kernel(block_ref, front_ref, mine_ref, other_ref, rows_ref, sem):
    owned, first = owner_of(block_ref[0])
    core = lax.axis_index("c")

    @pl.when(owned)
    def _():
        copy = pltpu.make_async_copy(front_ref.at[:, pl.ds(first, rows_ref.shape[1]), :], rows_ref, sem)
        copy.start()
        copy.wait()
        mine_ref[...] = rows_ref[core]
        other_ref[...] = rows_ref[1 - core]

    @pl.when(jnp.logical_not(owned))
    def _():
        mine_ref[...] = jnp.zeros_like(mine_ref)
        other_ref[...] = jnp.zeros_like(other_ref)


def take(blocks, front, depth):
    width = front.shape[2]
    shapes = [jax.ShapeDtypeStruct((depth, width), jnp.float32)] * 2
    return pl.pallas_call(
        take_kernel,
        grid_spec=pltpu.PrefetchScalarGridSpec(
            num_scalar_prefetch=1,
            grid=(1,),
            in_specs=[ANYWHERE],
            out_specs=[whole(s) for s in shapes],
            scratch_shapes=[pltpu.VMEM((2, depth, width), jnp.float32), pltpu.SemaphoreType.DMA],
        ),
        out_shape=shapes,
        cost_estimate=pl.CostEstimate(flops=0, bytes_accessed=2 * MIB, transcendentals=0),
        compiler_params=pltpu.CompilerParams(vmem_limit_bytes=8 * MIB),
        name="take",
    )(blocks, front)


def from_owner(mine, other):
    mine = mine + swap(other)
    mine = mine + send(mine, "yl", 1)
    return mine, swap(mine)


def pack_kernel(rows, own_ref, *refs):
    pairs, outs = refs[: -2 * len(rows)], refs[-2 * len(rows) :]
    core = lax.axis_index("c")
    steps = len(pairs) // 2
    first = 0
    for which, height in enumerate(rows):
        part = slice(first, first + height)
        for who in range(2):
            out = outs[2 * which + who]
            out[0] = own_ref[who * 2 : who * 2 + 2, part, :]
            for k in range(1, steps):
                near, far = pairs[2 * k - 2 : 2 * k]
                out[2 * k - 1 + core] = near[who * 2 : who * 2 + 2, part, :]
                out[2 * k - core] = far[2 - who * 2 : 4 - who * 2, part, :]
            out[2 * steps - 1] = pairs[2 * steps - 2 + who][:, part, :]
        first += height


def pack(own, pairs, rows):
    steps, depth = len(pairs), own.shape[2]
    shapes = [jax.ShapeDtypeStruct((steps, 2, h, depth), jnp.float32) for h in rows for _ in range(2)]
    outs = pl.pallas_call(
        functools.partial(pack_kernel, rows),
        grid=(1,),
        in_specs=[whole(a) for a in (own, *pairs)],
        out_specs=[whole(s) for s in shapes],
        out_shape=shapes,
        cost_estimate=pl.CostEstimate(flops=0, bytes_accessed=3 * MIB, transcendentals=0),
        compiler_params=pltpu.CompilerParams(vmem_limit_bytes=12 * MIB),
        name="pack",
    )(own, *pairs)
    return [out.reshape(steps * 2, *out.shape[2:]) for out in outs]


def whole(array):
    return pl.BlockSpec(array.shape, lambda i, *_, n=len(array.shape): (0,) * n, pipeline_mode=pl.Buffered(1))


ANYWHERE = pl.BlockSpec(memory_space=pl.ANY)


def order_kernel(*refs):
    pieces, outs = refs[:-2], refs[-2:]
    done = 0
    for own, other in zip(pieces[::2], pieces[1::2]):
        count = own.shape[0]

        @pl.loop(0, count)
        def _(j, own=own, other=other, done=done):
            row = pl.multiple_of(source(done + j, True) * 8, 8)
            for node, out in enumerate(outs):
                out[0, pl.ds(row, 8), :] = own[j, node * 8 : node * 8 + 8, :]
                out[1, pl.ds(row, 8), :] = other[j, node * 8 : node * 8 + 8, :]

        done += count


def order(pieces):
    depth = pieces[0].shape[2]
    shapes = [jax.ShapeDtypeStruct((2, depth, depth), jnp.float32)] * 2
    return pl.pallas_call(
        order_kernel,
        grid=(1,),
        in_specs=[whole(a) for a in pieces],
        out_specs=[whole(s) for s in shapes],
        out_shape=shapes,
        cost_estimate=pl.CostEstimate(flops=0, bytes_accessed=8 * MIB, transcendentals=0),
        compiler_params=pltpu.CompilerParams(vmem_limit_bytes=12 * MIB),
        name="order",
    )(*pieces)


def split(value):
    high = value.astype(jnp.bfloat16)
    low = (value - high.astype(jnp.float32)).astype(jnp.bfloat16)
    return high, low


def put_operand(real, imag, high_ref, low_ref):
    depth, width = real.shape
    for ref, re, im in zip((high_ref, low_ref), split(real), split(imag)):
        ref[:depth, :width] = re
        ref[:depth, width:] = im
        ref[depth:, :width] = -im
        ref[depth:, width:] = re


def product(real, imag, high_ref, low_ref):
    dot = functools.partial(jnp.dot, preferred_element_type=jnp.float32)
    (re_high, re_low), (im_high, im_low) = split(real), split(imag)
    high = cat([re_high, im_high], axis=1)
    low = cat([re_low, im_low], axis=1)
    return dot(low, high_ref[...]) + dot(high, low_ref[...]) + dot(high, high_ref[...])


def solve_into(inverse_ref, mine_ref, other_ref, out_ref, high_ref, low_ref):
    width = mine_ref.shape[1]
    core = lax.axis_index("c")
    first = core == 0
    mine, other = mine_ref[...], other_ref[...]
    put_operand(jnp.where(first, mine, other), jnp.where(first, other, mine), high_ref, low_ref)

    @pl.loop(0, 2)
    def _(m):
        rows = pl.ds(pl.multiple_of(m * 256, 256), 256)
        both = product(inverse_ref[core, rows, :], inverse_ref[1 - core, rows, :], high_ref, low_ref)
        out_ref[0, rows, :] = both[:, :width]
        out_ref[1, rows, :] = both[:, width:]


def solve(inverse, mine, other):
    depth, width = mine.shape
    shape = jax.ShapeDtypeStruct((2, depth, width), jnp.float32)
    return pl.pallas_call(
        solve_into,
        grid=(1,),
        in_specs=[whole(inverse), whole(mine), whole(other)],
        out_specs=whole(shape),
        scratch_shapes=[pltpu.VMEM((2 * depth, 2 * width), jnp.bfloat16)] * 2,
        out_shape=shape,
        cost_estimate=pl.CostEstimate(flops=6 * 2 * depth * 2 * depth * 2 * width, bytes_accessed=6 * MIB, transcendentals=0),
        compiler_params=pltpu.CompilerParams(vmem_limit_bytes=24 * MIB),
        name="solve",
    )(inverse, mine, other)


def multiply_panel(part, high_ref, low_ref):
    count, depth = part.shape[0], part.shape[2]
    real = part[:, :16, :].reshape(count * 16, depth)
    imag = part[:, 16:, :].reshape(count * 16, depth)
    return product(real, imag, high_ref, low_ref)


def first_slot(slot_ref, row, last):
    low, high = jnp.int32(0), jnp.int32(last)
    for _ in range(10):
        middle = (low + high) >> 1
        slot = slot_ref[middle]
        before = (slot >= 0) & (slot < row)
        low, high = jnp.where(before, jnp.minimum(middle + 1, high), low), jnp.where(before, high, middle)
    return low


def load_pieces(refs, panel_ref, sem):
    copies, done = [], 0
    for i, ref in enumerate(refs):
        count = ref.shape[0]
        copies.append(pltpu.make_async_copy(ref, panel_ref.at[pl.ds(done, count)], sem.at[i]))
        done += count
    return copies


def project_kernel(pieces, done, first, block_ref, slot_ref, *refs):
    panel_refs = refs[:pieces]
    panel_ref, high_ref, low_ref, sem = refs[-4:]
    owned, first_row = owner_of(block_ref[1])
    copies = load_pieces(panel_refs, panel_ref, sem)
    for copy in copies:
        copy.start()
    if first:
        solved_ref, out_ref = refs[pieces : pieces + 2]
    else:
        solved_ref, so_far_ref, front_ref, out_ref, mine_ref, other_ref, sums_ref, pivot_ref, pivot_sem = refs[pieces:-4]
        depth, width = mine_ref.shape
        pivot = pltpu.make_async_copy(front_ref.at[:, pl.ds(first_row, depth), :], pivot_ref, pivot_sem)
        pivot.start()
        sums_ref[:1024, :] = so_far_ref[...]
    target_ref = out_ref if first else sums_ref
    put_operand(solved_ref[0], solved_ref[1], high_ref, low_ref)
    for copy in copies:
        copy.wait()

    @pl.loop(0, panel_ref.shape[0] // 8)
    def _(m):
        result = multiply_panel(panel_ref[pl.ds(m * 8, 8)], high_ref, low_ref)
        for j in range(8):
            row = pl.multiple_of(source(done + m * 8 + j, False) * 16, 16)
            target_ref[pl.ds(row, 16), :] = result[j * 16 : (j + 1) * 16]

    if not first:
        out_ref[...] = sums_ref[:1024, :]
        pivot.wait()

        @pl.when(owned)
        def _():
            start = first_slot(slot_ref, first_row, 1024 - depth)
            past = start & 7
            turn = (8 - past) & 7
            in_first = lax.broadcasted_iota(jnp.int32, (8, 2 * width), 0) < 8 - past
            core_first = lax.axis_index("c") == 0

            @pl.loop(0, depth // 8)
            def _(m):
                rows = pl.ds(pl.multiple_of(m * 8, 8), 8)
                base = pl.multiple_of(start - past + m * 8, 8)
                upper = pltpu.roll(sums_ref[pl.ds(base, 8), :], turn, 0)
                lower = pltpu.roll(sums_ref[pl.ds(base + 8, 8), :], turn, 0)
                taken = jnp.where(in_first, upper, lower)
                real = pivot_ref[0, rows, :] - taken[:, :width]
                imag = pivot_ref[1, rows, :] - taken[:, width:]
                mine_ref[rows, :] = jnp.where(core_first, real, imag)
                other_ref[rows, :] = jnp.where(core_first, imag, real)

        @pl.when(jnp.logical_not(owned))
        def _():
            mine_ref[...] = jnp.zeros_like(mine_ref)
            other_ref[...] = jnp.zeros_like(other_ref)


def project(blocks, slots, panels, done, solved, so_far=None, front=None):
    _, depth, width = solved.shape
    first = so_far is None
    inputs = [solved] if first else [solved, so_far]
    shapes = [jax.ShapeDtypeStruct((1024, 2 * width), jnp.float32)]
    in_specs = [ANYWHERE] * len(panels) + [whole(a) for a in inputs]
    scratch = [
        pltpu.VMEM((sum(a.shape[0] for a in panels), 32, depth), jnp.float32),
        pltpu.VMEM((2 * depth, 2 * width), jnp.bfloat16),
        pltpu.VMEM((2 * depth, 2 * width), jnp.bfloat16),
        pltpu.SemaphoreType.DMA((len(panels),)),
    ]
    if not first:
        inputs.append(front)
        in_specs.append(ANYWHERE)
        shapes += [jax.ShapeDtypeStruct((depth, width), jnp.float32)] * 2
        scratch = [
            pltpu.VMEM((1032, 2 * width), jnp.float32),
            pltpu.VMEM(solved.shape, jnp.float32),
            pltpu.SemaphoreType.DMA,
        ] + scratch
    return pl.pallas_call(
        functools.partial(project_kernel, len(panels), done, first),
        grid_spec=pltpu.PrefetchScalarGridSpec(
            num_scalar_prefetch=2,
            grid=(1,),
            in_specs=in_specs,
            out_specs=[whole(s) for s in shapes],
            scratch_shapes=scratch,
        ),
        out_shape=shapes,
        cost_estimate=pl.CostEstimate(flops=3 * 2 * 1024 * depth * 2 * width, bytes_accessed=6 * MIB, transcendentals=0),
        compiler_params=pltpu.CompilerParams(vmem_limit_bytes=24 * MIB),
        name="project",
    )(blocks, slots, *panels, *inputs)


def subtract_rows(front_ref, update_ref, first, targets):
    width = front_ref.shape[2]
    new = []
    for i, target in enumerate(targets):
        row = update_ref[pl.ds(first + i, 1), :]
        for part in range(2):
            new.append(front_ref[part, pl.ds(target, 1), :] - row[:, part * width : (part + 1) * width])
    for i, target in enumerate(targets):
        for part in range(2):
            front_ref[part, pl.ds(target, 1), :] = new[2 * i + part]


def slot_targets(slot_ref, base, count, rows):
    slots = [slot_ref[base + i] for i in range(count)]
    return [jnp.where(slot >= 0, slot, rows + i % 8) for i, slot in enumerate(slots)]


def load_front(front_ref, held_ref, sem):
    rows = front_ref.shape[1]
    return [
        pltpu.make_async_copy(front_ref.at[part], held_ref.at[part, pl.ds(0, rows), :], sem.at[part])
        for part in range(2)
    ]


def store_front(held_ref, out_ref, sem):
    rows = out_ref.shape[1]
    return [
        pltpu.make_async_copy(held_ref.at[part, pl.ds(0, rows), :], out_ref.at[part], sem.at[part])
        for part in range(2)
    ]


def scatter_kernel(block_ref, slot_ref, front_ref, update_ref, solved_ref, out_ref, held_ref, sem):
    rows, depth = front_ref.shape[1], solved_ref.shape[1]
    copies = load_front(front_ref, held_ref, sem)
    for copy in copies:
        copy.start()
    for copy in copies:
        copy.wait()

    owned, first_row = owner_of(block_ref[0])

    @pl.when(owned)
    def _():
        held_ref[:, pl.ds(first_row, depth), :] = solved_ref[...]

    @pl.loop(0, 64)
    def _(g):
        subtract_rows(held_ref, update_ref, g * 16, slot_targets(slot_ref, g * 16, 16, rows))

    copies = store_front(held_ref, out_ref, sem)
    for copy in copies:
        copy.start()
    for copy in copies:
        copy.wait()


def scatter(blocks, slots, front, update, solved):
    _, rows, width = front.shape
    return pl.pallas_call(
        scatter_kernel,
        grid_spec=pltpu.PrefetchScalarGridSpec(
            num_scalar_prefetch=2,
            grid=(1,),
            in_specs=[ANYWHERE, whole(update), whole(solved)],
            out_specs=ANYWHERE,
            scratch_shapes=[pltpu.VMEM((2, rows + 8, width), jnp.float32), pltpu.SemaphoreType.DMA((2,))],
        ),
        out_shape=jax.ShapeDtypeStruct(front.shape, jnp.float32),
        cost_estimate=pl.CostEstimate(flops=MIB, bytes_accessed=24 * MIB, transcendentals=0),
        compiler_params=pltpu.CompilerParams(vmem_limit_bytes=24 * MIB),
        name="scatter",
    )(blocks, slots, front, update, solved)


def finish_kernel(pieces, block_ref, slot_ref, *refs):
    inverse_ref, mine_ref, other_ref, front_ref, out_ref = refs[pieces : pieces + 5]
    held_ref, solved_ref, panel_ref, even_ref, odd_ref, high_ref, low_ref, front_sem, sem = refs[pieces + 5 :]
    rows = front_ref.shape[1]
    depth, _ = mine_ref.shape
    copies = load_pieces(refs[:pieces], panel_ref, sem) + load_front(front_ref, held_ref, front_sem)
    for copy in copies:
        copy.start()
    solve_into(inverse_ref, mine_ref, other_ref, solved_ref, high_ref, low_ref)
    put_operand(solved_ref[0], solved_ref[1], high_ref, low_ref)
    for copy in copies:
        copy.wait()

    owned, first_row = owner_of(block_ref[1])

    @pl.when(owned)
    def _():
        held_ref[:, pl.ds(first_row, depth), :] = solved_ref[...]

    def put_down(update_ref, m, skip=None):
        for j in range(8):
            base = source(jnp.maximum(m * 8 + j, 0), True) * 16
            targets = slot_targets(slot_ref, base, 16, rows)
            if skip is not None:
                targets = [jnp.where(skip, rows + i % 8, t) for i, t in enumerate(targets)]
            subtract_rows(held_ref, update_ref, j * 16, targets)

    @pl.loop(0, 4)
    def _(m):
        even_ref[...] = multiply_panel(panel_ref[pl.ds(m * 16, 8)], high_ref, low_ref)
        put_down(odd_ref, 2 * m - 1, skip=m == 0)
        odd_ref[...] = multiply_panel(panel_ref[pl.ds(m * 16 + 8, 8)], high_ref, low_ref)
        put_down(even_ref, 2 * m)

    put_down(odd_ref, 7)
    copies = store_front(held_ref, out_ref, front_sem)
    for copy in copies:
        copy.start()
    for copy in copies:
        copy.wait()


def finish(blocks, slots, panels, inverse, mine, other, front):
    _, rows, width = front.shape
    depth = mine.shape[0]
    return pl.pallas_call(
        functools.partial(finish_kernel, len(panels)),
        grid_spec=pltpu.PrefetchScalarGridSpec(
            num_scalar_prefetch=2,
            grid=(1,),
            in_specs=[ANYWHERE] * len(panels) + [whole(a) for a in (inverse, mine, other)] + [ANYWHERE],
            out_specs=ANYWHERE,
            scratch_shapes=[
                pltpu.VMEM((2, rows + 8, width), jnp.float32),
                pltpu.VMEM((2, depth, width), jnp.float32),
                pltpu.VMEM((64, 32, depth), jnp.float32),
                pltpu.VMEM((128, 2 * width), jnp.float32),
                pltpu.VMEM((128, 2 * width), jnp.float32),
                pltpu.VMEM((2 * depth, 2 * width), jnp.bfloat16),
                pltpu.VMEM((2 * depth, 2 * width), jnp.bfloat16),
                pltpu.SemaphoreType.DMA((2,)),
                pltpu.SemaphoreType.DMA((len(panels),)),
            ],
        ),
        out_shape=jax.ShapeDtypeStruct(front.shape, jnp.float32),
        cost_estimate=pl.CostEstimate(flops=9 * 2 * 1024 * depth * 2 * width, bytes_accessed=13 * MIB, transcendentals=0),
        compiler_params=pltpu.CompilerParams(vmem_limit_bytes=32 * MIB),
        name="finish",
    )(blocks, slots, *panels, inverse, mine, other, front)


def program(right_side, pivot_inverse, ancestor_panel, ancestors, pivot_block):
    depth = pivot_inverse.shape[3]
    panel0, own_b = prepare(pivot_inverse, ancestor_panel)

    pair_a = cat([panel0, send(panel0, "yh", 1)])
    pair_b = cat([own_b, send(own_b, "yh", 1)])
    chip_a = cat([pair_a, swap(pair_a)])
    chip_b = cat([pair_b, swap(pair_b)])

    mine0, other0 = take(pivot_block, right_side, depth)
    mine0, other0 = from_owner(mine0, other0)

    x1 = send_apart(chip_a, "x", 1)
    x2 = send_apart(pair_a, "x", 2)
    own_a, other_a = pack(chip_a, [x1, swap(x1), x2, swap(x2)], (32,))

    z2 = send_apart(chip_b, "z", 2)
    z1 = send_apart(chip_b, "z", 1)
    z3 = send_apart(z2, "z", 1)
    z4 = send_apart(z2[:2], "z", 2)
    near = [z1, swap(z1), z2, swap(z2), z3, swap(z3), z4, swap(z4)]
    own_i, other_i, own_p, other_p = pack(chip_b, near, (16, 32))

    t1, o1 = send_apart(other_a, "z", 1), send_apart(own_a, "z", 1)
    t2, o2 = send_apart(t1, "z", 1), send_apart(o1, "z", 1)
    t3, o3 = send_apart(t2, "z", 1), send_apart(o2, "z", 1)
    o4 = send_apart(o3, "z", 1)
    early_a = [own_a, o1, swap(t1), o2, swap(t2)]
    late_a = [o3, swap(t3), o4]

    io1, it1 = send_apart(own_i, "x", 1), send_apart(other_i, "x", 1)
    io2 = send_apart(io1, "x", 1)
    both = [own_i, other_i, io1, it1, swap(it1), swap(io1), io2, swap(io2)]
    inverse0, inverse1 = order(both)

    po1, pt1 = send_apart(own_p, "x", 1), send_apart(other_p, "x", 1)
    po2 = send_apart(po1, "x", 1)
    panels_b = [own_p, po1, swap(pt1), po2]

    solved0 = solve(inverse0, mine0, other0)
    (early,) = project(pivot_block, ancestors[0], early_a, 0, solved0)
    sums, mine1, other1 = project(pivot_block, ancestors[0], late_a, 40, solved0, early, right_side)
    front = scatter(pivot_block, ancestors[0], right_side, sums, solved0)
    mine1, other1 = from_owner(mine1, other1)
    return finish(pivot_block, ancestors[1], panels_b, inverse1, mine1, other1, front)


def solution(mesh):
    torus = Mesh(mesh.devices.reshape(tuple(SIZES.values())), tuple(SIZES))
    in_specs = (
        P(None, ROW, SRC),
        P(None, None, SRC, None),
        P(None, None, ROW + SRC, None),
        P(None, ROW),
        P(),
    )
    return jax.shard_map(program, mesh=torus, in_specs=in_specs, out_specs=P(None, ROW, SRC), check_vma=False)
```

profile of v0, /device:TPU:1, one launch (start us, length us, event | category | flops | bytes accessed | tf_op | source)
XLA Modules:
  0.0 140.1 jit_solution(16549179261320442458)
XLA Ops:
  0.0 0.9 copy-done.2
  0.9 0.8 copy-done.3
  1.8 3.8 %collective-permute-start.20 = (f32[1,32,512]{2,1,0:T(8,128)S(1)}, f32[1,32,512]{2,1,0:T(8,128)S(1)}, u32[]{:S(2)}, u32[]{:S(2)}) collective-permute-start(f32[1,32,512]{2,1,0:T(8,128)S(1)} %get-tuple-element.26), channel_id=1, source_target_pairs={{0,128},{128,0},{1,129},{129,1},{2,130},{130,2},{3,131},{131,3},{4... | collective-permute-start | bytes 196616 | tf_op jit(solution)/shard_map/ppermute | solution.py:20
  5.6 0.1 collective-permute-start
  5.7 6.0 %collective-permute-done = f32[1,48,512]{2,1,0:T(8,128)S(1)} collective-permute-done((f32[1,48,512]{2,1,0:T(8,128)S(1)}, f32[1,48,512]{2,1,0:T(8,128)S(1)}, u32[]{:S(2)}, u32[]{:S(2)}) %collective-permute-start) | collective-permute-done | bytes 98336 | tf_op jit(solution)/shard_map/ppermute | solution.py:20
  11.8 1.3 collective-permute-start.1
  13.1 1.1 collective-permute-done.1
  14.1 5.8 %collective-permute-start.4 = (f32[4,48,512]{2,1,0:T(8,128)S(1)}, f32[4,48,512]{2,1,0:T(8,128)S(1)}, u32[]{:S(2)}, u32[]{:S(2)}) collective-permute-start(f32[4,48,512]{2,1,0:T(8,128)S(1)} %constant_dynamic-update-slice_fusion.own_ref), channel_id=1, source_target_pairs={{0,32},{1,97},{16,48},{17,113},{32,64},{33,1},{48,80},{49,17},{64,... | collective-permute-start | bytes 1179656 | tf_op jit(solution)/shard_map/ppermute | solution.py:28
  20.0 0.1 collective-permute-start.21
  20.1 1.3 collective-permute-done.21
  21.4 2.6 %collective-permute-start.22 = (f32[4,32,512]{2,1,0:T(8,128)S(1)}, f32[4,32,512]{2,1,0:T(8,128)S(1)}, u32[]{:S(2)}, u32[]{:S(2)}) collective-permute-start(f32[4,32,512]{2,1,0:T(8,128)S(1)} %constant_dynamic-update-slice_fusion.5.own_ref), channel_id=1, source_target_pairs={{0,4},{1,13},{4,8},{5,1},{8,12},{9,5},{12,0},{13,9},{2,6},{3,15},{... | collective-permute-start | bytes 786440 | tf_op jit(solution)/shard_map/ppermute | solution.py:28
  24.0 0.7 collective-permute-start.2
  24.7 4.2 %collective-permute-done.4.refs_2_ = f32[4,48,512]{2,1,0:T(8,128)S(1)} collective-permute-done((f32[4,48,512]{2,1,0:T(8,128)S(1)}, f32[4,48,512]{2,1,0:T(8,128)S(1)}, u32[]{:S(2)}, u32[]{:S(2)}) %collective-permute-start.4) | collective-permute-done | bytes 393248 | tf_op jit(solution)/shard_map/ppermute | solution.py:28
  28.9 2.2 %collective-permute-start.6 = (f32[4,48,512]{2,1,0:T(8,128)S(1)}, f32[4,48,512]{2,1,0:T(8,128)S(1)}, u32[]{:S(2)}, u32[]{:S(2)}) collective-permute-start(f32[4,48,512]{2,1,0:T(8,128)S(1)} %collective-permute-done.4.refs_2_), channel_id=1, source_target_pairs={{0,16},{1,113},{16,32},{17,1},{32,48},{33,17},{48,64},{49,33},{64,... | collective-permute-start | bytes 1179656 | tf_op jit(solution)/shard_map/ppermute | solution.py:28
  31.1 2.0 %collective-permute-start.8 = (f32[2,48,512]{2,1,0:T(8,128)S(1)}, f32[2,48,512]{2,1,0:T(8,128)S(1)}, u32[]{:S(2)}, u32[]{:S(2)}) collective-permute-start(f32[2,48,512]{2,1,0:T(8,128)S(1)} %slice.14), channel_id=1, source_target_pairs={{0,32},{1,97},{16,48},{17,113},{32,64},{33,1},{48,80},{49,17},{64,... | collective-permute-start | bytes 589832 | tf_op jit(solution)/shard_map/ppermute | solution.py:28
  33.1 2.7 %collective-permute-start.24 = (f32[2,32,512]{2,1,0:T(8,128)S(1)}, f32[2,32,512]{2,1,0:T(8,128)S(1)}, u32[]{:S(2)}, u32[]{:S(2)}) collective-permute-start(f32[2,32,512]{2,1,0:T(8,128)S(1)} %get-tuple-element.35), channel_id=1, source_target_pairs={{0,8},{1,9},{4,12},{5,13},{8,0},{9,1},{12,4},{13,5},{2,10},{3,11},... | collective-permute-start | bytes 393224 | tf_op jit(solution)/shard_map/ppermute | solution.py:28
  35.9 3.7 %collective-permute-done.24.refs_2_ = f32[2,32,512]{2,1,0:T(8,128)S(1)} collective-permute-done((f32[2,32,512]{2,1,0:T(8,128)S(1)}, f32[2,32,512]{2,1,0:T(8,128)S(1)}, u32[]{:S(2)}, u32[]{:S(2)}) %collective-permute-start.24) | collective-permute-done | bytes 131104 | tf_op jit(solution)/shard_map/ppermute | solution.py:28
  39.5 2.0 %collective-permute-done.8.refs_6_ = f32[2,48,512]{2,1,0:T(8,128)S(1)} collective-permute-done((f32[2,48,512]{2,1,0:T(8,128)S(1)}, f32[2,48,512]{2,1,0:T(8,128)S(1)}, u32[]{:S(2)}, u32[]{:S(2)}) %collective-permute-start.8) | collective-permute-done | bytes 196640 | tf_op jit(solution)/shard_map/ppermute | solution.py:28
  41.5 1.1 collective-permute-start.9
  42.6 0.5 collective-permute-start.3
  43.1 0.1 collective-permute-start.7
  43.3 2.9 %collective-permute-start.29 = (f32[8,32,512]{2,1,0:T(8,128)S(1)}, f32[8,32,512]{2,1,0:T(8,128)S(1)}, u32[]{:S(2)}, u32[]{:S(2)}) collective-permute-start(f32[8,32,512]{2,1,0:T(8,128)S(1)} %bitcast.21), channel_id=1, source_target_pairs={{0,16},{1,113},{16,32},{17,1},{32,48},{33,17},{48,64},{49,33},{64,... | collective-permute-start | bytes 1572872 | tf_op jit(solution)/shard_map/ppermute | solution.py:28
  46.2 0.8 collective-permute-start.26
  47.0 2.2 %copy-done = f32[2,2048,256]{2,1,0:T(8,128)S(1)} copy-done((f32[2,2048,256]{2,1,0:T(8,128)S(1)}, f32[2,2048,256]{2,1,0:T(8,128)}, u32[]{:S(2)}) %copy-start) | copy-done | bytes 4194328
  49.2 0.6 take.1
  49.9 0.3 collective-permute-start.34
  50.2 0.2 pack.2
  50.4 2.6 %collective-permute-start.14 = (f32[16,16,512]{2,1,0:T(8,128)S(1)}, f32[16,16,512]{2,1,0:T(8,128)S(1)}, u32[]{:S(2)}, u32[]{:S(2)}) collective-permute-start(f32[16,16,512]{2,1,0:T(8,128)S(1)} %bitcast.8), channel_id=1, source_target_pairs={{0,4},{1,13},{4,8},{5,1},{8,12},{9,5},{12,0},{13,9},{2,6},{3,15},{... | collective-permute-start | bytes 1572872 | tf_op jit(solution)/shard_map/ppermute | solution.py:28
  52.9 2.8 %collective-permute-start.30 = (f32[8,32,512]{2,1,0:T(8,128)S(1)}, f32[8,32,512]{2,1,0:T(8,128)S(1)}, u32[]{:S(2)}, u32[]{:S(2)}) collective-permute-start(f32[8,32,512]{2,1,0:T(8,128)S(1)} %collective-permute-done.29), channel_id=1, source_target_pairs={{0,16},{1,113},{16,32},{17,1},{32,48},{33,17},{48,64},{49,33},{64,... | collective-permute-start | bytes 1572872 | tf_op jit(solution)/shard_map/ppermute | solution.py:28
  55.8 2.1 %collective-permute-done.26.refs_1_ = f32[8,32,512]{2,1,0:T(8,128)S(1)} collective-permute-done((f32[8,32,512]{2,1,0:T(8,128)S(1)}, f32[8,32,512]{2,1,0:T(8,128)S(1)}, u32[]{:S(2)}, u32[]{:S(2)}) %collective-permute-start.26) | collective-permute-done | bytes 524320 | tf_op jit(solution)/shard_map/ppermute | solution.py:28
  57.9 3.4 %collective-permute-start.27 = (f32[8,32,512]{2,1,0:T(8,128)S(1)}, f32[8,32,512]{2,1,0:T(8,128)S(1)}, u32[]{:S(2)}, u32[]{:S(2)}) collective-permute-start(f32[8,32,512]{2,1,0:T(8,128)S(1)} %collective-permute-done.26.refs_1_), channel_id=1, source_target_pairs={{0,16},{1,113},{16,32},{17,1},{32,48},{33,17},{48,64},{49,33},{64,... | collective-permute-start | bytes 1572872 | tf_op jit(solution)/shard_map/ppermute | solution.py:28
  61.3 0.1 add.12
  61.4 0.5 collective-permute-start.35
  61.9 2.2 %collective-permute-start.15 = (f32[16,16,512]{2,1,0:T(8,128)S(1)}, f32[16,16,512]{2,1,0:T(8,128)S(1)}, u32[]{:S(2)}, u32[]{:S(2)}) collective-permute-start(f32[16,16,512]{2,1,0:T(8,128)S(1)} %bitcast.10), channel_id=1, source_target_pairs={{0,4},{1,13},{4,8},{5,1},{8,12},{9,5},{12,0},{13,9},{2,6},{3,15},{... | collective-permute-start | bytes 1572872 | tf_op jit(solution)/shard_map/ppermute | solution.py:28
  64.1 0.5 collective-permute-start.18
  64.6 2.0 %collective-permute-start.31 = (f32[8,32,512]{2,1,0:T(8,128)S(1)}, f32[8,32,512]{2,1,0:T(8,128)S(1)}, u32[]{:S(2)}, u32[]{:S(2)}) collective-permute-start(f32[8,32,512]{2,1,0:T(8,128)S(1)} %collective-permute-done.30), channel_id=1, source_target_pairs={{0,16},{1,113},{16,32},{17,1},{32,48},{33,17},{48,64},{49,33},{64,... | collective-permute-start | bytes 1572872 | tf_op jit(solution)/shard_map/ppermute | solution.py:28
  66.6 2.5 %collective-permute-done.27.refs_3_ = f32[8,32,512]{2,1,0:T(8,128)S(1)} collective-permute-done((f32[8,32,512]{2,1,0:T(8,128)S(1)}, f32[8,32,512]{2,1,0:T(8,128)S(1)}, u32[]{:S(2)}, u32[]{:S(2)}) %collective-permute-start.27) | collective-permute-done | bytes 524320 | tf_op jit(solution)/shard_map/ppermute | solution.py:28
  69.2 3.4 %collective-permute-start.28 = (f32[8,32,512]{2,1,0:T(8,128)S(1)}, f32[8,32,512]{2,1,0:T(8,128)S(1)}, u32[]{:S(2)}, u32[]{:S(2)}) collective-permute-start(f32[8,32,512]{2,1,0:T(8,128)S(1)} %collective-permute-done.27.refs_3_), channel_id=1, source_target_pairs={{0,16},{1,113},{16,32},{17,1},{32,48},{33,17},{48,64},{49,33},{64,... | collective-permute-start | bytes 1572872 | tf_op jit(solution)/shard_map/ppermute | solution.py:28
  72.6 2.3 %collective-permute-done.35 = f32[512,256]{1,0:T(8,128)S(1)} collective-permute-done((f32[512,256]{1,0:T(8,128)S(1)}, f32[512,256]{1,0:T(8,128)S(1)}, u32[]{:S(2)}, u32[]{:S(2)}) %collective-permute-start.35) | collective-permute-done | bytes 524320 | tf_op jit(solution)/shard_map/ppermute | solution.py:20
  74.8 0.5 collective-permute-start.16
  75.3 0.5 collective-permute-done.18.refs_6_
  75.8 1.3 collective-permute-start.19
  77.2 0.1 collective-permute-start.36
  77.3 3.1 %collective-permute-done.28.refs_0_ = f32[8,32,512]{2,1,0:T(8,128)S(1)} collective-permute-done((f32[8,32,512]{2,1,0:T(8,128)S(1)}, f32[8,32,512]{2,1,0:T(8,128)S(1)}, u32[]{:S(2)}, u32[]{:S(2)}) %collective-permute-start.28) | collective-permute-done | bytes 524320 | tf_op jit(solution)/shard_map/ppermute | solution.py:28
  80.4 1.9 %collective-permute-start.37 = (f32[8,32,512]{2,1,0:T(8,128)S(1)}, f32[8,32,512]{2,1,0:T(8,128)S(1)}, u32[]{:S(2)}, u32[]{:S(2)}) collective-permute-start(f32[8,32,512]{2,1,0:T(8,128)S(1)} %collective-permute-done.29), channel_id=1, source_target_pairs={{0,1},{1,0},{2,3},{3,2},{4,5},{5,4},{6,7},{7,6},{8,9},{9,8},{10,11... | collective-permute-start | bytes 1572872 | tf_op jit(solution)/shard_map/ppermute | solution.py:20
  82.3 0.5 collective-permute-start.32
  82.8 1.6 %collective-permute-start.33 = (f32[8,32,512]{2,1,0:T(8,128)S(1)}, f32[8,32,512]{2,1,0:T(8,128)S(1)}, u32[]{:S(2)}, u32[]{:S(2)}) collective-permute-start(f32[8,32,512]{2,1,0:T(8,128)S(1)} %collective-permute-done.28.refs_0_), channel_id=1, source_target_pairs={{0,16},{1,113},{16,32},{17,1},{32,48},{33,17},{48,64},{49,33},{64,... | collective-permute-start | bytes 1572872 | tf_op jit(solution)/shard_map/ppermute | solution.py:28
  84.4 1.6 %order.1 = (f32[2,512,512]{2,1,0:T(8,128)S(1)}, f32[2,512,512]{2,1,0:T(8,128)S(1)}) custom-call(f32[16,16,512]{2,1,0:T(8,128)S(1)} %bitcast.9, f32[16,16,512]{2,1,0:T(8,128)S(1)} %bitcast.11, f32[16,16,512]{2,1,0:T(8,128)S(1)} %collective-permute-done.14.refs_2_, f32[16,16,512]{2,1,0:T(8,128)S(1)} %collective-permute-done.15.refs_3_, ...), custom_call_target="tpu_custom_call" | custom-call | bytes 8388608 | tf_op jit(solution)/shard_map/order/pallas_call | solution.py:175
  86.0 2.6 %collective-permute-start.11 = (f32[16,32,512]{2,1,0:T(8,128)S(1)}, f32[16,32,512]{2,1,0:T(8,128)S(1)}, u32[]{:S(2)}, u32[]{:S(2)}) collective-permute-start(f32[16,32,512]{2,1,0:T(8,128)S(1)} %bitcast.18), channel_id=1, source_target_pairs={{0,4},{1,13},{4,8},{5,1},{8,12},{9,5},{12,0},{13,9},{2,6},{3,15},{... | collective-permute-start | bytes 3145736 | tf_op jit(solution)/shard_map/ppermute | solution.py:28
  88.6 0.5 collective-permute-start.10
  89.1 2.3 %solve.1.refs_5_.refs_3_.solved_ref = f32[2,512,256]{2,1,0:T(8,128)S(1)} custom-call(f32[2,512,512]{2,1,0:T(8,128)S(1)} %get-tuple-element.29.inverse_ref, f32[512,256]{1,0:T(8,128)S(1)} %add.13.mine_ref, f32[512,256]{1,0:T(8,128)S(1)} %collective-permute-done.36.other_ref), custom_call_target="tpu_custom_call" | custom-call | flops 3221225472 | bytes 6291456 | tf_op jit(solution)/shard_map/solve/pallas_call | solution.py:228
  91.4 4.0 %project.2.refs_4_ = f32[1024,512]{1,0:T(8,128)S(1)} custom-call(s32[2]{0:T(128)S(1)} %copy-done.4, s32[1024]{0:T(1024)S(1)} %bitcast.12, f32[8,32,512]{2,1,0:T(8,128)S(1)} %bitcast.20, f32[8,32,512]{2,1,0:T(8,128)S(1)} %collective-permute-done.26.refs_1_, f32[8,32,512]{2,1,0:T(8,128)S(1)} %collective-permute-done.37.refs_2_, ...), custom_call_target="tpu_custom_call" | custom-call | flops 1610612736 | bytes 6291456 | tf_op jit(solution)/shard_map/project/pallas_call | solution.py:345
  95.4 3.8 %project.3 = (f32[1024,512]{1,0:T(8,128)S(1)}, f32[512,256]{1,0:T(8,128)S(1)}, f32[512,256]{1,0:T(8,128)S(1)}) custom-call(s32[2]{0:T(128)S(1)} %copy-done.4, s32[1024]{0:T(1024)S(1)} %bitcast.13, f32[8,32,512]{2,1,0:T(8,128)S(1)} %collective-permute-done.28.refs_0_, f32[8,32,512]{2,1,0:T(8,128)S(1)} %collective-permute-done.32.refs_1_, ...), custom_call_target="tpu_custom_call" | custom-call | flops 1610612736 | bytes 6291456 | tf_op jit(solution)/shard_map/project/pallas_call | solution.py:345
  99.2 0.1 collective-permute-start.39
  99.3 1.0 collective-permute-done.11
  100.3 0.7 collective-permute-start.12
  101.1 0.1 collective-permute-done.39
  101.3 0.3 collective-permute-start.40
  101.6 9.9 %collective-permute-done.10.refs_1_ = f32[16,32,512]{2,1,0:T(8,128)S(1)} collective-permute-done((f32[16,32,512]{2,1,0:T(8,128)S(1)}, f32[16,32,512]{2,1,0:T(8,128)S(1)}, u32[]{:S(2)}, u32[]{:S(2)}) %collective-permute-start.10) | collective-permute-done | bytes 1048608 | tf_op jit(solution)/shard_map/ppermute | solution.py:28
  111.6 3.1 %collective-permute-start.13 = (f32[16,32,512]{2,1,0:T(8,128)S(1)}, f32[16,32,512]{2,1,0:T(8,128)S(1)}, u32[]{:S(2)}, u32[]{:S(2)}) collective-permute-start(f32[16,32,512]{2,1,0:T(8,128)S(1)} %collective-permute-done.10.refs_1_), channel_id=1, source_target_pairs={{0,4},{1,13},{4,8},{5,1},{8,12},{9,5},{12,0},{13,9},{2,6},{3,15},{... | collective-permute-start | bytes 3145736 | tf_op jit(solution)/shard_map/ppermute | solution.py:28
  114.8 1.1 collective-permute-start.41
  115.9 7.5 %scatter.1.refs_7_ = f32[2,2048,256]{2,1,0:T(8,128)S(1)} custom-call(s32[2]{0:T(128)S(1)} %copy-done.4, s32[1024]{0:T(1024)S(1)} %bitcast.14, f32[2,2048,256]{2,1,0:T(8,128)S(1)} %copy-done.1, f32[1024,512]{1,0:T(8,128)S(1)} %get-tuple-element.34.update_ref, f32[2,512,256]{2,1,0:T(8,128)S(1)} %solve.1.refs_5_.refs_3_.solved_ref), custom_call_target="tpu_custom_call" | custom-call | flops 1048576 | bytes 25165824 | tf_op jit(solution)/shard_map/scatter/pallas_call | solution.py:421
  123.4 3.1 %collective-permute-done.13.refs_3_ = f32[16,32,512]{2,1,0:T(8,128)S(1)} collective-permute-done((f32[16,32,512]{2,1,0:T(8,128)S(1)}, f32[16,32,512]{2,1,0:T(8,128)S(1)}, u32[]{:S(2)}, u32[]{:S(2)}) %collective-permute-start.13) | collective-permute-done | bytes 1048608 | tf_op jit(solution)/shard_map/ppermute | solution.py:28
  126.4 13.5 %finish.1 = f32[2,2048,256]{2,1,0:T(8,128)} custom-call(s32[2]{0:T(128)S(1)} %copy-done.4, s32[1024]{0:T(1024)S(1)} %bitcast.15, f32[16,32,512]{2,1,0:T(8,128)S(1)} %bitcast.17, f32[16,32,512]{2,1,0:T(8,128)S(1)} %collective-permute-done.10.refs_1_, f32[16,32,512]{2,1,0:T(8,128)S(1)} %collective-permute-done.12.refs_2_, ...), custom_call_target="tpu_custom_call" | custom-call | flops 4831838208 | bytes 13631488 | tf_op jit(solution)/shard_map/finish/pallas_call | solution.py:482
  (55 shorter events, 0.5 us)
Async XLA Ops:
  0.0 0.9 copy-start.2
  0.9 0.8 copy-start.3
  1.7 45.3 %copy-start.4 = (s32[2]{0:T(128)S(1)}, s32[2]{0:T(128)}, u32[]{:S(2)}) copy-start(s32[2]{0:T(128)} %block_ref.9) | copy-start | bytes 28
  1.8 18.2 %collective-permute-start.20 = (f32[1,32,512]{2,1,0:T(8,128)S(1)}, f32[1,32,512]{2,1,0:T(8,128)S(1)}, u32[]{:S(2)}, u32[]{:S(2)}) collective-permute-start(f32[1,32,512]{2,1,0:T(8,128)S(1)} %get-tuple-element.26), channel_id=1, source_target_pairs={{0,128},{128,0},{1,129},{129,1},{2,130},{130,2},{3,131},{131,3},{4... | collective-permute-start | bytes 196616 | tf_op jit(solution)/shard_map/ppermute | solution.py:20
  5.6 6.2 %collective-permute-start = (f32[1,48,512]{2,1,0:T(8,128)S(1)}, f32[1,48,512]{2,1,0:T(8,128)S(1)}, u32[]{:S(2)}, u32[]{:S(2)}) collective-permute-start(f32[1,48,512]{2,1,0:T(8,128)S(1)} %get-tuple-element.20), channel_id=1, source_target_pairs={{0,128},{128,0},{1,129},{129,1},{2,130},{130,2},{3,131},{131,3},{4... | collective-permute-start | bytes 294920 | tf_op jit(solution)/shard_map/ppermute | solution.py:20
  11.8 2.3 %collective-permute-start.1 = (f32[2,48,512]{2,1,0:T(8,128)S(1)}, f32[2,48,512]{2,1,0:T(8,128)S(1)}, u32[]{:S(2)}, u32[]{:S(2)}) collective-permute-start(f32[2,48,512]{2,1,0:T(8,128)S(1)} %pad_maximum_fusion), channel_id=1, source_target_pairs={{0,1},{1,0},{2,3},{3,2},{4,5},{5,4},{6,7},{7,6},{8,9},{9,8},{10,11... | collective-permute-start | bytes 589832 | tf_op jit(solution)/shard_map/ppermute | solution.py:20
  14.1 14.8 %collective-permute-start.4 = (f32[4,48,512]{2,1,0:T(8,128)S(1)}, f32[4,48,512]{2,1,0:T(8,128)S(1)}, u32[]{:S(2)}, u32[]{:S(2)}) collective-permute-start(f32[4,48,512]{2,1,0:T(8,128)S(1)} %constant_dynamic-update-slice_fusion.own_ref), channel_id=1, source_target_pairs={{0,32},{1,97},{16,48},{17,113},{32,64},{33,1},{48,80},{49,17},{64,... | collective-permute-start | bytes 1179656 | tf_op jit(solution)/shard_map/ppermute | solution.py:28
  20.0 1.4 %collective-permute-start.21 = (f32[2,32,512]{2,1,0:T(8,128)S(1)}, f32[2,32,512]{2,1,0:T(8,128)S(1)}, u32[]{:S(2)}, u32[]{:S(2)}) collective-permute-start(f32[2,32,512]{2,1,0:T(8,128)S(1)} %get-tuple-element.35), channel_id=1, source_target_pairs={{0,1},{1,0},{2,3},{3,2},{4,5},{5,4},{6,7},{7,6},{8,9},{9,8},{10,11... | collective-permute-start | bytes 393224 | tf_op jit(solution)/shard_map/ppermute | solution.py:20
  21.4 14.4 %collective-permute-start.22 = (f32[4,32,512]{2,1,0:T(8,128)S(1)}, f32[4,32,512]{2,1,0:T(8,128)S(1)}, u32[]{:S(2)}, u32[]{:S(2)}) collective-permute-start(f32[4,32,512]{2,1,0:T(8,128)S(1)} %constant_dynamic-update-slice_fusion.5.own_ref), channel_id=1, source_target_pairs={{0,4},{1,13},{4,8},{5,1},{8,12},{9,5},{12,0},{13,9},{2,6},{3,15},{... | collective-permute-start | bytes 786440 | tf_op jit(solution)/shard_map/ppermute | solution.py:28
  24.0 18.6 %collective-permute-start.2 = (f32[4,48,512]{2,1,0:T(8,128)S(1)}, f32[4,48,512]{2,1,0:T(8,128)S(1)}, u32[]{:S(2)}, u32[]{:S(2)}) collective-permute-start(f32[4,48,512]{2,1,0:T(8,128)S(1)} %constant_dynamic-update-slice_fusion.own_ref), channel_id=1, source_target_pairs={{0,16},{1,113},{16,32},{17,1},{32,48},{33,17},{48,64},{49,33},{64,... | collective-permute-start | bytes 1179656 | tf_op jit(solution)/shard_map/ppermute | solution.py:28
  28.9 14.2 %collective-permute-start.6 = (f32[4,48,512]{2,1,0:T(8,128)S(1)}, f32[4,48,512]{2,1,0:T(8,128)S(1)}, u32[]{:S(2)}, u32[]{:S(2)}) collective-permute-start(f32[4,48,512]{2,1,0:T(8,128)S(1)} %collective-permute-done.4.refs_2_), channel_id=1, source_target_pairs={{0,16},{1,113},{16,32},{17,1},{32,48},{33,17},{48,64},{49,33},{64,... | collective-permute-start | bytes 1179656 | tf_op jit(solution)/shard_map/ppermute | solution.py:28
  31.1 10.4 %collective-permute-start.8 = (f32[2,48,512]{2,1,0:T(8,128)S(1)}, f32[2,48,512]{2,1,0:T(8,128)S(1)}, u32[]{:S(2)}, u32[]{:S(2)}) collective-permute-start(f32[2,48,512]{2,1,0:T(8,128)S(1)} %slice.14), channel_id=1, source_target_pairs={{0,32},{1,97},{16,48},{17,113},{32,64},{33,1},{48,80},{49,17},{64,... | collective-permute-start | bytes 589832 | tf_op jit(solution)/shard_map/ppermute | solution.py:28
  33.1 6.4 %collective-permute-start.24 = (f32[2,32,512]{2,1,0:T(8,128)S(1)}, f32[2,32,512]{2,1,0:T(8,128)S(1)}, u32[]{:S(2)}, u32[]{:S(2)}) collective-permute-start(f32[2,32,512]{2,1,0:T(8,128)S(1)} %get-tuple-element.35), channel_id=1, source_target_pairs={{0,8},{1,9},{4,12},{5,13},{8,0},{9,1},{12,4},{13,5},{2,10},{3,11},... | collective-permute-start | bytes 393224 | tf_op jit(solution)/shard_map/ppermute | solution.py:28
  35.8 7.4 %collective-permute-start.23 = (f32[4,32,512]{2,1,0:T(8,128)S(1)}, f32[4,32,512]{2,1,0:T(8,128)S(1)}, u32[]{:S(2)}, u32[]{:S(2)}) collective-permute-start(f32[4,32,512]{2,1,0:T(8,128)S(1)} %collective-permute-done.22.refs_0_), channel_id=1, source_target_pairs={{0,1},{1,0},{2,3},{3,2},{4,5},{5,4},{6,7},{7,6},{8,9},{9,8},{10,11... | collective-permute-start | bytes 786440 | tf_op jit(solution)/shard_map/ppermute | solution.py:20
  39.5 3.1 %collective-permute-start.25 = (f32[2,32,512]{2,1,0:T(8,128)S(1)}, f32[2,32,512]{2,1,0:T(8,128)S(1)}, u32[]{:S(2)}, u32[]{:S(2)}) collective-permute-start(f32[2,32,512]{2,1,0:T(8,128)S(1)} %collective-permute-done.24.refs_2_), channel_id=1, source_target_pairs={{0,1},{1,0},{2,3},{3,2},{4,5},{5,4},{6,7},{7,6},{8,9},{9,8},{10,11... | collective-permute-start | bytes 393224 | tf_op jit(solution)/shard_map/ppermute | solution.py:20
  41.5 4.6 %collective-permute-start.9 = (f32[2,48,512]{2,1,0:T(8,128)S(1)}, f32[2,48,512]{2,1,0:T(8,128)S(1)}, u32[]{:S(2)}, u32[]{:S(2)}) collective-permute-start(f32[2,48,512]{2,1,0:T(8,128)S(1)} %collective-permute-done.8.refs_6_), channel_id=1, source_target_pairs={{0,1},{1,0},{2,3},{3,2},{4,5},{5,4},{6,7},{7,6},{8,9},{9,8},{10,11... | collective-permute-start | bytes 589832 | tf_op jit(solution)/shard_map/ppermute | solution.py:20
  42.6 7.2 %collective-permute-start.5 = (f32[4,48,512]{2,1,0:T(8,128)S(1)}, f32[4,48,512]{2,1,0:T(8,128)S(1)}, u32[]{:S(2)}, u32[]{:S(2)}) collective-permute-start(f32[4,48,512]{2,1,0:T(8,128)S(1)} %collective-permute-done.4.refs_2_), channel_id=1, source_target_pairs={{0,1},{1,0},{2,3},{3,2},{4,5},{5,4},{6,7},{7,6},{8,9},{9,8},{10,11... | collective-permute-start | bytes 1179656 | tf_op jit(solution)/shard_map/ppermute | solution.py:20
  42.6 7.5 %collective-permute-start.3 = (f32[4,48,512]{2,1,0:T(8,128)S(1)}, f32[4,48,512]{2,1,0:T(8,128)S(1)}, u32[]{:S(2)}, u32[]{:S(2)}) collective-permute-start(f32[4,48,512]{2,1,0:T(8,128)S(1)} %collective-permute-done.2.refs_0_), channel_id=1, source_target_pairs={{0,1},{1,0},{2,3},{3,2},{4,5},{5,4},{6,7},{7,6},{8,9},{9,8},{10,11... | collective-permute-start | bytes 1179656 | tf_op jit(solution)/shard_map/ppermute | solution.py:20
  43.1 7.0 %collective-permute-start.7 = (f32[4,48,512]{2,1,0:T(8,128)S(1)}, f32[4,48,512]{2,1,0:T(8,128)S(1)}, u32[]{:S(2)}, u32[]{:S(2)}) collective-permute-start(f32[4,48,512]{2,1,0:T(8,128)S(1)} %collective-permute-done.6.refs_4_), channel_id=1, source_target_pairs={{0,1},{1,0},{2,3},{3,2},{4,5},{5,4},{6,7},{7,6},{8,9},{9,8},{10,11... | collective-permute-start | bytes 1179656 | tf_op jit(solution)/shard_map/ppermute | solution.py:20
  43.3 9.7 %collective-permute-start.29 = (f32[8,32,512]{2,1,0:T(8,128)S(1)}, f32[8,32,512]{2,1,0:T(8,128)S(1)}, u32[]{:S(2)}, u32[]{:S(2)}) collective-permute-start(f32[8,32,512]{2,1,0:T(8,128)S(1)} %bitcast.21), channel_id=1, source_target_pairs={{0,16},{1,113},{16,32},{17,1},{32,48},{33,17},{48,64},{49,33},{64,... | collective-permute-start | bytes 1572872 | tf_op jit(solution)/shard_map/ppermute | solution.py:28
  46.2 11.7 %collective-permute-start.26 = (f32[8,32,512]{2,1,0:T(8,128)S(1)}, f32[8,32,512]{2,1,0:T(8,128)S(1)}, u32[]{:S(2)}, u32[]{:S(2)}) collective-permute-start(f32[8,32,512]{2,1,0:T(8,128)S(1)} %bitcast.19), channel_id=1, source_target_pairs={{0,16},{1,113},{16,32},{17,1},{32,48},{33,17},{48,64},{49,33},{64,... | collective-permute-start | bytes 1572872 | tf_op jit(solution)/shard_map/ppermute | solution.py:28
  47.0 2.2 %copy-start = (f32[2,2048,256]{2,1,0:T(8,128)S(1)}, f32[2,2048,256]{2,1,0:T(8,128)}, u32[]{:S(2)}) copy-start(f32[2,2048,256]{2,1,0:T(8,128)} %front_ref.3) | copy-start | bytes 12582916
  49.9 11.5 %collective-permute-start.34 = (f32[512,256]{1,0:T(8,128)S(1)}, f32[512,256]{1,0:T(8,128)S(1)}, u32[]{:S(2)}, u32[]{:S(2)}) collective-permute-start(f32[512,256]{1,0:T(8,128)S(1)} %get-tuple-element.31), channel_id=1, source_target_pairs={{0,1},{1,0},{2,3},{3,2},{4,5},{5,4},{6,7},{7,6},{8,9},{9,8},{10,11... | collective-permute-start | bytes 1572872 | tf_op jit(solution)/shard_map/ppermute | solution.py:20
  50.4 34.0 %copy-start.5 = (s32[2,1024]{1,0:T(2,128)S(1)}, s32[2,1024]{1,0:T(2,128)}, u32[]{:S(2)}) copy-start(s32[2,1024]{1,0:T(2,128)} %param.8) | copy-start | bytes 24580
  50.4 13.7 %collective-permute-start.14 = (f32[16,16,512]{2,1,0:T(8,128)S(1)}, f32[16,16,512]{2,1,0:T(8,128)S(1)}, u32[]{:S(2)}, u32[]{:S(2)}) collective-permute-start(f32[16,16,512]{2,1,0:T(8,128)S(1)} %bitcast.8), channel_id=1, source_target_pairs={{0,4},{1,13},{4,8},{5,1},{8,12},{9,5},{12,0},{13,9},{2,6},{3,15},{... | collective-permute-start | bytes 1572872 | tf_op jit(solution)/shard_map/ppermute | solution.py:28
  52.9 11.7 %collective-permute-start.30 = (f32[8,32,512]{2,1,0:T(8,128)S(1)}, f32[8,32,512]{2,1,0:T(8,128)S(1)}, u32[]{:S(2)}, u32[]{:S(2)}) collective-permute-start(f32[8,32,512]{2,1,0:T(8,128)S(1)} %collective-permute-done.29), channel_id=1, source_target_pairs={{0,16},{1,113},{16,32},{17,1},{32,48},{33,17},{48,64},{49,33},{64,... | collective-permute-start | bytes 1572872 | tf_op jit(solution)/shard_map/ppermute | solution.py:28
  57.9 11.2 %collective-permute-start.27 = (f32[8,32,512]{2,1,0:T(8,128)S(1)}, f32[8,32,512]{2,1,0:T(8,128)S(1)}, u32[]{:S(2)}, u32[]{:S(2)}) collective-permute-start(f32[8,32,512]{2,1,0:T(8,128)S(1)} %collective-permute-done.26.refs_1_), channel_id=1, source_target_pairs={{0,16},{1,113},{16,32},{17,1},{32,48},{33,17},{48,64},{49,33},{64,... | collective-permute-start | bytes 1572872 | tf_op jit(solution)/shard_map/ppermute | solution.py:28
  61.4 13.4 %collective-permute-start.35 = (f32[512,256]{1,0:T(8,128)S(1)}, f32[512,256]{1,0:T(8,128)S(1)}, u32[]{:S(2)}, u32[]{:S(2)}) collective-permute-start(f32[512,256]{1,0:T(8,128)S(1)} %add.12), channel_id=1, source_target_pairs={{0,2},{2,0},{1,3},{3,1},{4,6},{6,4},{5,7},{7,5},{8,10},{10,8},{9,1... | collective-permute-start | bytes 1572872 | tf_op jit(solution)/shard_map/ppermute | solution.py:20
  61.9 12.9 %collective-permute-start.15 = (f32[16,16,512]{2,1,0:T(8,128)S(1)}, f32[16,16,512]{2,1,0:T(8,128)S(1)}, u32[]{:S(2)}, u32[]{:S(2)}) collective-permute-start(f32[16,16,512]{2,1,0:T(8,128)S(1)} %bitcast.10), channel_id=1, source_target_pairs={{0,4},{1,13},{4,8},{5,1},{8,12},{9,5},{12,0},{13,9},{2,6},{3,15},{... | collective-permute-start | bytes 1572872 | tf_op jit(solution)/shard_map/ppermute | solution.py:28
  64.1 11.8 %collective-permute-start.18 = (f32[16,16,512]{2,1,0:T(8,128)S(1)}, f32[16,16,512]{2,1,0:T(8,128)S(1)}, u32[]{:S(2)}, u32[]{:S(2)}) collective-permute-start(f32[16,16,512]{2,1,0:T(8,128)S(1)} %collective-permute-done.14.refs_2_), channel_id=1, source_target_pairs={{0,4},{1,13},{4,8},{5,1},{8,12},{9,5},{12,0},{13,9},{2,6},{3,15},{... | collective-permute-start | bytes 1572872 | tf_op jit(solution)/shard_map/ppermute | solution.py:28
  64.6 12.6 %collective-permute-start.31 = (f32[8,32,512]{2,1,0:T(8,128)S(1)}, f32[8,32,512]{2,1,0:T(8,128)S(1)}, u32[]{:S(2)}, u32[]{:S(2)}) collective-permute-start(f32[8,32,512]{2,1,0:T(8,128)S(1)} %collective-permute-done.30), channel_id=1, source_target_pairs={{0,16},{1,113},{16,32},{17,1},{32,48},{33,17},{48,64},{49,33},{64,... | collective-permute-start | bytes 1572872 | tf_op jit(solution)/shard_map/ppermute | solution.py:28
  69.2 11.2 %collective-permute-start.28 = (f32[8,32,512]{2,1,0:T(8,128)S(1)}, f32[8,32,512]{2,1,0:T(8,128)S(1)}, u32[]{:S(2)}, u32[]{:S(2)}) collective-permute-start(f32[8,32,512]{2,1,0:T(8,128)S(1)} %collective-permute-done.27.refs_3_), channel_id=1, source_target_pairs={{0,16},{1,113},{16,32},{17,1},{32,48},{33,17},{48,64},{49,33},{64,... | collective-permute-start | bytes 1572872 | tf_op jit(solution)/shard_map/ppermute | solution.py:28
  74.8 7.4 %collective-permute-start.17 = (f32[16,16,512]{2,1,0:T(8,128)S(1)}, f32[16,16,512]{2,1,0:T(8,128)S(1)}, u32[]{:S(2)}, u32[]{:S(2)}) collective-permute-start(f32[16,16,512]{2,1,0:T(8,128)S(1)} %collective-permute-done.14.refs_2_), channel_id=1, source_target_pairs={{0,1},{1,0},{2,3},{3,2},{4,5},{5,4},{6,7},{7,6},{8,9},{9,8},{10,11... | collective-permute-start | bytes 1572872 | tf_op jit(solution)/shard_map/ppermute | solution.py:20
  74.8 7.4 %collective-permute-start.16 = (f32[16,16,512]{2,1,0:T(8,128)S(1)}, f32[16,16,512]{2,1,0:T(8,128)S(1)}, u32[]{:S(2)}, u32[]{:S(2)}) collective-permute-start(f32[16,16,512]{2,1,0:T(8,128)S(1)} %collective-permute-done.15.refs_3_), channel_id=1, source_target_pairs={{0,1},{1,0},{2,3},{3,2},{4,5},{5,4},{6,7},{7,6},{8,9},{9,8},{10,11... | collective-permute-start | bytes 1572872 | tf_op jit(solution)/shard_map/ppermute | solution.py:20
  75.8 7.0 %collective-permute-start.19 = (f32[16,16,512]{2,1,0:T(8,128)S(1)}, f32[16,16,512]{2,1,0:T(8,128)S(1)}, u32[]{:S(2)}, u32[]{:S(2)}) collective-permute-start(f32[16,16,512]{2,1,0:T(8,128)S(1)} %collective-permute-done.18.refs_6_), channel_id=1, source_target_pairs={{0,1},{1,0},{2,3},{3,2},{4,5},{5,4},{6,7},{7,6},{8,9},{9,8},{10,11... | collective-permute-start | bytes 1572872 | tf_op jit(solution)/shard_map/ppermute | solution.py:20
  77.2 8.8 %collective-permute-start.36 = (f32[512,256]{1,0:T(8,128)S(1)}, f32[512,256]{1,0:T(8,128)S(1)}, u32[]{:S(2)}, u32[]{:S(2)}) collective-permute-start(f32[512,256]{1,0:T(8,128)S(1)} %add.13.mine_ref), channel_id=1, source_target_pairs={{0,1},{1,0},{2,3},{3,2},{4,5},{5,4},{6,7},{7,6},{8,9},{9,8},{10,11... | collective-permute-start | bytes 1572872 | tf_op jit(solution)/shard_map/ppermute | solution.py:20
  80.4 8.2 %collective-permute-start.37 = (f32[8,32,512]{2,1,0:T(8,128)S(1)}, f32[8,32,512]{2,1,0:T(8,128)S(1)}, u32[]{:S(2)}, u32[]{:S(2)}) collective-permute-start(f32[8,32,512]{2,1,0:T(8,128)S(1)} %collective-permute-done.29), channel_id=1, source_target_pairs={{0,1},{1,0},{2,3},{3,2},{4,5},{5,4},{6,7},{7,6},{8,9},{9,8},{10,11... | collective-permute-start | bytes 1572872 | tf_op jit(solution)/shard_map/ppermute | solution.py:20
  82.3 9.1 %collective-permute-start.38 = (f32[8,32,512]{2,1,0:T(8,128)S(1)}, f32[8,32,512]{2,1,0:T(8,128)S(1)}, u32[]{:S(2)}, u32[]{:S(2)}) collective-permute-start(f32[8,32,512]{2,1,0:T(8,128)S(1)} %collective-permute-done.30), channel_id=1, source_target_pairs={{0,1},{1,0},{2,3},{3,2},{4,5},{5,4},{6,7},{7,6},{8,9},{9,8},{10,11... | collective-permute-start | bytes 1572872 | tf_op jit(solution)/shard_map/ppermute | solution.py:20
  82.3 13.1 %collective-permute-start.32 = (f32[8,32,512]{2,1,0:T(8,128)S(1)}, f32[8,32,512]{2,1,0:T(8,128)S(1)}, u32[]{:S(2)}, u32[]{:S(2)}) collective-permute-start(f32[8,32,512]{2,1,0:T(8,128)S(1)} %collective-permute-done.31), channel_id=1, source_target_pairs={{0,1},{1,0},{2,3},{3,2},{4,5},{5,4},{6,7},{7,6},{8,9},{9,8},{10,11... | collective-permute-start | bytes 1572872 | tf_op jit(solution)/shard_map/ppermute | solution.py:20
  82.8 12.6 %collective-permute-start.33 = (f32[8,32,512]{2,1,0:T(8,128)S(1)}, f32[8,32,512]{2,1,0:T(8,128)S(1)}, u32[]{:S(2)}, u32[]{:S(2)}) collective-permute-start(f32[8,32,512]{2,1,0:T(8,128)S(1)} %collective-permute-done.28.refs_0_), channel_id=1, source_target_pairs={{0,16},{1,113},{16,32},{17,1},{32,48},{33,17},{48,64},{49,33},{64,... | collective-permute-start | bytes 1572872 | tf_op jit(solution)/shard_map/ppermute | solution.py:28
  86.0 14.3 %collective-permute-start.11 = (f32[16,32,512]{2,1,0:T(8,128)S(1)}, f32[16,32,512]{2,1,0:T(8,128)S(1)}, u32[]{:S(2)}, u32[]{:S(2)}) collective-permute-start(f32[16,32,512]{2,1,0:T(8,128)S(1)} %bitcast.18), channel_id=1, source_target_pairs={{0,4},{1,13},{4,8},{5,1},{8,12},{9,5},{12,0},{13,9},{2,6},{3,15},{... | collective-permute-start | bytes 3145736 | tf_op jit(solution)/shard_map/ppermute | solution.py:28
  88.6 23.0 %collective-permute-start.10 = (f32[16,32,512]{2,1,0:T(8,128)S(1)}, f32[16,32,512]{2,1,0:T(8,128)S(1)}, u32[]{:S(2)}, u32[]{:S(2)}) collective-permute-start(f32[16,32,512]{2,1,0:T(8,128)S(1)} %bitcast.16), channel_id=1, source_target_pairs={{0,4},{1,13},{4,8},{5,1},{8,12},{9,5},{12,0},{13,9},{2,6},{3,15},{... | collective-permute-start | bytes 3145736 | tf_op jit(solution)/shard_map/ppermute | solution.py:28
  91.4 4.0 %copy-start.1 = (f32[2,2048,256]{2,1,0:T(8,128)S(1)}, f32[2,2048,256]{2,1,0:T(8,128)}, u32[]{:S(2)}) copy-start(f32[2,2048,256]{2,1,0:T(8,128)} %front_ref.3) | copy-start | bytes 12582916
  99.2 2.0 %collective-permute-start.39 = (f32[512,256]{1,0:T(8,128)S(1)}, f32[512,256]{1,0:T(8,128)S(1)}, u32[]{:S(2)}, u32[]{:S(2)}) collective-permute-start(f32[512,256]{1,0:T(8,128)S(1)} %get-tuple-element.33), channel_id=1, source_target_pairs={{0,1},{1,0},{2,3},{3,2},{4,5},{5,4},{6,7},{7,6},{8,9},{9,8},{10,11... | collective-permute-start | bytes 1572872 | tf_op jit(solution)/shard_map/ppermute | solution.py:20
  100.3 23.0 %collective-permute-start.12 = (f32[16,32,512]{2,1,0:T(8,128)S(1)}, f32[16,32,512]{2,1,0:T(8,128)S(1)}, u32[]{:S(2)}, u32[]{:S(2)}) collective-permute-start(f32[16,32,512]{2,1,0:T(8,128)S(1)} %collective-permute-done.11), channel_id=1, source_target_pairs={{0,1},{1,0},{2,3},{3,2},{4,5},{5,4},{6,7},{7,6},{8,9},{9,8},{10,11... | collective-permute-start | bytes 3145736 | tf_op jit(solution)/shard_map/ppermute | solution.py:20
  101.3 13.4 %collective-permute-start.40 = (f32[512,256]{1,0:T(8,128)S(1)}, f32[512,256]{1,0:T(8,128)S(1)}, u32[]{:S(2)}, u32[]{:S(2)}) collective-permute-start(f32[512,256]{1,0:T(8,128)S(1)} %add.14), channel_id=1, source_target_pairs={{0,2},{2,0},{1,3},{3,1},{4,6},{6,4},{5,7},{7,5},{8,10},{10,8},{9,1... | collective-permute-start | bytes 1572872 | tf_op jit(solution)/shard_map/ppermute | solution.py:20
  111.6 14.9 %collective-permute-start.13 = (f32[16,32,512]{2,1,0:T(8,128)S(1)}, f32[16,32,512]{2,1,0:T(8,128)S(1)}, u32[]{:S(2)}, u32[]{:S(2)}) collective-permute-start(f32[16,32,512]{2,1,0:T(8,128)S(1)} %collective-permute-done.10.refs_1_), channel_id=1, source_target_pairs={{0,4},{1,13},{4,8},{5,1},{8,12},{9,5},{12,0},{13,9},{2,6},{3,15},{... | collective-permute-start | bytes 3145736 | tf_op jit(solution)/shard_map/ppermute | solution.py:28
  114.8 11.6 %collective-permute-start.41 = (f32[512,256]{1,0:T(8,128)S(1)}, f32[512,256]{1,0:T(8,128)S(1)}, u32[]{:S(2)}, u32[]{:S(2)}) collective-permute-start(f32[512,256]{1,0:T(8,128)S(1)} %add.15.refs_5_), channel_id=1, source_target_pairs={{0,1},{1,0},{2,3},{3,2},{4,5},{5,4},{6,7},{7,6},{8,9},{9,8},{10,11... | collective-permute-start | bytes 1572872 | tf_op jit(solution)/shard_map/ppermute | solution.py:20
where the time goes:
time: 142 us; the launch traced here: 140 us
  starting transfers between devices  58.8 us (41%)
  waiting for transfers between devices  43 us (30%)
  Pallas kernels  33.5 us (24%)
  local copies, waits for them, and re-layouts  4.03 us (3%)
    ppermute x19, starting transfers between devices, send_apart(): return lax.ppermute(value, (axis, 'c'), pairs)  44.6 us
    ppermute x19, waiting for transfers between devices, send_apart(): return lax.ppermute(value, (axis, 'c'), pairs)  32.1 us
    ppermute x23, starting transfers between devices, send(): lax.ppermute(value, axis, [(i, (i + shift) % size) for i in range(size)])  14.3 us
    pallas_call x1, Pallas kernels, finish(): pl.pallas_call(functools.partial(finish_kernel, len(panels)), grid_spec=p...  13.5 us
    ppermute x23, waiting for transfers between devices, send(): lax.ppermute(value, axis, [(i, (i + shift) % size) for i in range(size)])  10.9 us
    pallas_call x2, Pallas kernels, project(): pl.pallas_call(functools.partial(project_kernel, len(panels), done, first...  7.75 us
    pallas_call x1, Pallas kernels, scatter(): pl.pallas_call(scatter_kernel, grid_spec=pltpu.PrefetchScalarGridSpec(num...  7.46 us
    unnamed x15, local copies, waits for them, and re-layouts  3.97 us
  transfers between devices with their start and end apart: 42, of which 15 were waited for; matrix products, arithmetic and copies ran while one was open for 0% of the time, Pallas kernels for 14%

commit v1 on v0

--- a/solution.py
+++ b/solution.py
@@ -39,10 +39,10 @@
 def source(piece, x_outer):
     yh, z, x, sign = lax.axis_index("yh"), lax.axis_index("z"), lax.axis_index("x"), 1 - 2 * lax.axis_index("c")
     if x_outer:
-        dx, dz = step_of(piece >> 4) * sign, step_of((piece >> 1) & 7)
+        dx, dy, dz = step_of(piece >> 4) * sign, piece >> 3, step_of(piece & 7)
     else:
-        dz, dx = step_of(piece >> 3) * sign, step_of((piece >> 1) & 3)
-    return ((yh + piece) & 1) * 32 + ((z + dz) & 7) * 4 + ((x + dx) & 3)
+        dz, dx, dy = step_of(piece >> 3) * sign, step_of((piece >> 1) & 3), piece
+    return ((yh + dy) & 1) * 32 + ((z + dz) & 7) * 4 + ((x + dx) & 3)
 
 
 def owner_of(block):
@@ -115,24 +115,25 @@
 def pack_kernel(rows, own_ref, *refs):
     pairs, outs = refs[: -2 * len(rows)], refs[-2 * len(rows) :]
     core = lax.axis_index("c")
-    steps = len(pairs) // 2
+    steps, count = len(pairs) // 2, own_ref.shape[0] // 2
     first = 0
     for which, height in enumerate(rows):
         part = slice(first, first + height)
         for who in range(2):
             out = outs[2 * which + who]
-            out[0] = own_ref[who * 2 : who * 2 + 2, part, :]
+            here, there = (slice(w * count, (w + 1) * count) for w in (who, 1 - who))
+            out[0] = own_ref[here, part, :]
             for k in range(1, steps):
                 near, far = pairs[2 * k - 2 : 2 * k]
-                out[2 * k - 1 + core] = near[who * 2 : who * 2 + 2, part, :]
-                out[2 * k - core] = far[2 - who * 2 : 4 - who * 2, part, :]
+                out[2 * k - 1 + core] = near[here, part, :]
+                out[2 * k - core] = far[there, part, :]
             out[2 * steps - 1] = pairs[2 * steps - 2 + who][:, part, :]
         first += height
 
 
 def pack(own, pairs, rows):
-    steps, depth = len(pairs), own.shape[2]
-    shapes = [jax.ShapeDtypeStruct((steps, 2, h, depth), jnp.float32) for h in rows for _ in range(2)]
+    steps, count, depth = len(pairs), own.shape[0] // 2, own.shape[2]
+    shapes = [jax.ShapeDtypeStruct((steps, count, h, depth), jnp.float32) for h in rows for _ in range(2)]
     outs = pl.pallas_call(
         functools.partial(pack_kernel, rows),
         grid=(1,),
@@ -143,7 +144,7 @@
         compiler_params=pltpu.CompilerParams(vmem_limit_bytes=12 * MIB),
         name="pack",
     )(own, *pairs)
-    return [out.reshape(steps * 2, *out.shape[2:]) for out in outs]
+    return [out.reshape(steps * count, *out.shape[2:]) for out in outs]
 
 
 def whole(array):
@@ -510,9 +511,8 @@
     panel0, own_b = prepare(pivot_inverse, ancestor_panel)
 
     pair_a = cat([panel0, send(panel0, "yh", 1)])
-    pair_b = cat([own_b, send(own_b, "yh", 1)])
     chip_a = cat([pair_a, swap(pair_a)])
-    chip_b = cat([pair_b, swap(pair_b)])
+    chip_b = cat([own_b, swap(own_b)])
 
     mine0, other0 = take(pivot_block, right_side, depth)
     mine0, other0 = from_owner(mine0, other0)
@@ -524,9 +524,12 @@
     z2 = send_apart(chip_b, "z", 2)
     z1 = send_apart(chip_b, "z", 1)
     z3 = send_apart(z2, "z", 1)
-    z4 = send_apart(z2[:2], "z", 2)
+    z4 = send_apart(z2[:1], "z", 2)
     near = [z1, swap(z1), z2, swap(z2), z3, swap(z3), z4, swap(z4)]
     own_i, other_i, own_p, other_p = pack(chip_b, near, (16, 32))
+    across_i, across_p = send(own_i, "yh", 1), send(own_p, "yh", 1)
+    own_i, other_i = cat([own_i, across_i]), cat([other_i, swap(across_i)])
+    own_p, other_p = cat([own_p, across_p]), cat([other_p, swap(across_p)])
 
     t1, o1 = send_apart(other_a, "z", 1), send_apart(own_a, "z", 1)
     t2, o2 = send_apart(t1, "z", 1), send_apart(o1, "z", 1)

time: 142 us -> 149 us (1.049); the launches traced: 140 us -> 149 us
  starting transfers between devices: 58.8 us -> 64 us
  waiting for transfers between devices: 43 us -> 45.7 us
    ppermute x23 -> x26, starting transfers between devices: 14.3 us -> 29.3 us  [send(): lax.ppermute(value, axis, [(i, (i + shift) % size) for i in range(size)])]
    ppermute x23 -> x26, waiting for transfers between devices: 10.9 us -> 21.2 us  [send(): lax.ppermute(value, axis, [(i, (i + shift) % size) for i in range(size)])]
    ppermute x19, starting transfers between devices: 44.6 us -> 34.7 us  [send_apart(): return lax.ppermute(value, (axis, 'c'), pairs)]
    ppermute x19, waiting for transfers between devices: 32.1 us -> 24.5 us  [send_apart(): return lax.ppermute(value, (axis, 'c'), pairs)]
    unnamed x15 -> x16, local copies, waits for them, and re-layouts: 3.97 us -> 4.61 us
  transfers between devices with their start and end apart: 42 -> 45, of which waited for: 15 -> 13; matrix products, arithmetic and copies ran while one was open for 0% -> 0% of each run, Pallas kernels for 14% -> 13%
where the time goes in v1:
time: 149 us
  starting transfers between devices  64 us (43%)
  waiting for transfers between devices  45.7 us (31%)
  Pallas kernels  33.3 us (22%)
  local copies, waits for them, and re-layouts  4.66 us (3%)
    ppermute x19, starting transfers between devices, send_apart(): return lax.ppermute(value, (axis, 'c'), pairs)  34.7 us
    ppermute x26, starting transfers between devices, send(): lax.ppermute(value, axis, [(i, (i + shift) % size) for i in range(size)])  29.3 us
    ppermute x19, waiting for transfers between devices, send_apart(): return lax.ppermute(value, (axis, 'c'), pairs)  24.5 us
    ppermute x26, waiting for transfers between devices, send(): lax.ppermute(value, axis, [(i, (i + shift) % size) for i in range(size)])  21.2 us
    pallas_call x1, Pallas kernels, finish(): pl.pallas_call(functools.partial(finish_kernel, len(panels)), grid_spec=p...  13.4 us
    pallas_call x2, Pallas kernels, project(): pl.pallas_call(functools.partial(project_kernel, len(panels), done, first...  7.73 us
    pallas_call x1, Pallas kernels, scatter(): pl.pallas_call(scatter_kernel, grid_spec=pltpu.PrefetchScalarGridSpec(num...  7.47 us
    unnamed x16, local copies, waits for them, and re-layouts  4.61 us
  transfers between devices with their start and end apart: 45, of which 13 were waited for; matrix products, arithmetic and copies ran while one was open for 0% of the time, Pallas kernels for 13%

profile of v1, /device:TPU:1, one launch (start us, length us, event | category | flops | bytes accessed | tf_op | source)
XLA Modules:
  0.0 148.8 jit_solution(3281248106532520348)
XLA Ops:
  0.0 0.9 copy-done.2
  0.9 0.8 copy-done.3
  1.8 3.3 %collective-permute-start = (f32[1,48,512]{2,1,0:T(8,128)S(1)}, f32[1,48,512]{2,1,0:T(8,128)S(1)}, u32[]{:S(2)}, u32[]{:S(2)}) collective-permute-start(f32[1,48,512]{2,1,0:T(8,128)S(1)} %get-tuple-element.20), channel_id=1, source_target_pairs={{0,1},{1,0},{2,3},{3,2},{4,5},{5,4},{6,7},{7,6},{8,9},{9,8},{10,11... | collective-permute-start | bytes 294920 | tf_op jit(solution)/shard_map/ppermute | solution.py:20
  5.1 0.9 collective-permute-done
  6.0 4.4 %collective-permute-start.3 = (f32[2,48,512]{2,1,0:T(8,128)S(1)}, f32[2,48,512]{2,1,0:T(8,128)S(1)}, u32[]{:S(2)}, u32[]{:S(2)}) collective-permute-start(f32[2,48,512]{2,1,0:T(8,128)S(1)} %constant_dynamic-update-slice_fusion.own_ref), channel_id=1, source_target_pairs={{0,32},{1,97},{16,48},{17,113},{32,64},{33,1},{48,80},{49,17},{64,... | collective-permute-start | bytes 589832 | tf_op jit(solution)/shard_map/ppermute | solution.py:28
  10.4 2.9 %collective-permute-start.23 = (f32[1,32,512]{2,1,0:T(8,128)S(1)}, f32[1,32,512]{2,1,0:T(8,128)S(1)}, u32[]{:S(2)}, u32[]{:S(2)}) collective-permute-start(f32[1,32,512]{2,1,0:T(8,128)S(1)} %get-tuple-element.26), channel_id=1, source_target_pairs={{0,128},{128,0},{1,129},{129,1},{2,130},{130,2},{3,131},{131,3},{4... | collective-permute-start | bytes 196616 | tf_op jit(solution)/shard_map/ppermute | solution.py:20
  13.3 0.8 collective-permute-start.1
  14.1 4.1 %collective-permute-start.5 = (f32[2,48,512]{2,1,0:T(8,128)S(1)}, f32[2,48,512]{2,1,0:T(8,128)S(1)}, u32[]{:S(2)}, u32[]{:S(2)}) collective-permute-start(f32[2,48,512]{2,1,0:T(8,128)S(1)} %collective-permute-done.3.refs_2_), channel_id=1, source_target_pairs={{0,16},{1,113},{16,32},{17,1},{32,48},{33,17},{48,64},{49,33},{64,... | collective-permute-start | bytes 589832 | tf_op jit(solution)/shard_map/ppermute | solution.py:28
  18.2 0.1 collective-permute-start.24
  18.3 2.2 %copy-done = f32[2,2048,256]{2,1,0:T(8,128)S(1)} copy-done((f32[2,2048,256]{2,1,0:T(8,128)S(1)}, f32[2,2048,256]{2,1,0:T(8,128)}, u32[]{:S(2)}) %copy-start) | copy-done | bytes 4194328
  20.5 0.7 copy-done.4
  21.2 0.6 take.1
  21.8 0.6 collective-permute-start.37
  22.4 1.5 %collective-permute-start.7 = (f32[1,48,512]{2,1,0:T(8,128)S(1)}, f32[1,48,512]{2,1,0:T(8,128)S(1)}, u32[]{:S(2)}, u32[]{:S(2)}) collective-permute-start(f32[1,48,512]{2,1,0:T(8,128)S(1)} %slice.14), channel_id=1, source_target_pairs={{0,32},{1,97},{16,48},{17,113},{32,64},{33,1},{48,80},{49,17},{64,... | collective-permute-start | bytes 294920 | tf_op jit(solution)/shard_map/ppermute | solution.py:28
  23.9 0.5 collective-permute-start.2
  24.4 2.5 %collective-permute-done.7.refs_6_ = f32[1,48,512]{2,1,0:T(8,128)S(1)} collective-permute-done((f32[1,48,512]{2,1,0:T(8,128)S(1)}, f32[1,48,512]{2,1,0:T(8,128)S(1)}, u32[]{:S(2)}, u32[]{:S(2)}) %collective-permute-start.7) | collective-permute-done | bytes 98336 | tf_op jit(solution)/shard_map/ppermute | solution.py:28
  26.9 2.8 %collective-permute-start.8 = (f32[1,48,512]{2,1,0:T(8,128)S(1)}, f32[1,48,512]{2,1,0:T(8,128)S(1)}, u32[]{:S(2)}, u32[]{:S(2)}) collective-permute-start(f32[1,48,512]{2,1,0:T(8,128)S(1)} %collective-permute-done.7.refs_6_), channel_id=1, source_target_pairs={{0,1},{1,0},{2,3},{3,2},{4,5},{5,4},{6,7},{7,6},{8,9},{9,8},{10,11... | collective-permute-start | bytes 294920 | tf_op jit(solution)/shard_map/ppermute | solution.py:20
  29.8 0.9 collective-permute-done.8.refs_7_
  30.7 2.3 %collective-permute-start.25 = (f32[4,32,512]{2,1,0:T(8,128)S(1)}, f32[4,32,512]{2,1,0:T(8,128)S(1)}, u32[]{:S(2)}, u32[]{:S(2)}) collective-permute-start(f32[4,32,512]{2,1,0:T(8,128)S(1)} %constant_dynamic-update-slice_fusion.4.own_ref), channel_id=1, source_target_pairs={{0,4},{1,13},{4,8},{5,1},{8,12},{9,5},{12,0},{13,9},{2,6},{3,15},{... | collective-permute-start | bytes 786440 | tf_op jit(solution)/shard_map/ppermute | solution.py:28
  33.0 0.1 pack.2
  33.2 2.9 %collective-permute-start.15 = (f32[8,16,512]{2,1,0:T(8,128)S(1)}, f32[8,16,512]{2,1,0:T(8,128)S(1)}, u32[]{:S(2)}, u32[]{:S(2)}) collective-permute-start(f32[8,16,512]{2,1,0:T(8,128)S(1)} %bitcast.12), channel_id=1, source_target_pairs={{0,128},{128,0},{1,129},{129,1},{2,130},{130,2},{3,131},{131,3},{4... | collective-permute-start | bytes 786440 | tf_op jit(solution)/shard_map/ppermute | solution.py:20
  36.1 0.7 collective-permute-start.27
  36.8 1.8 %collective-permute-start.26 = (f32[4,32,512]{2,1,0:T(8,128)S(1)}, f32[4,32,512]{2,1,0:T(8,128)S(1)}, u32[]{:S(2)}, u32[]{:S(2)}) collective-permute-start(f32[4,32,512]{2,1,0:T(8,128)S(1)} %collective-permute-done.25.refs_0_), channel_id=1, source_target_pairs={{0,1},{1,0},{2,3},{3,2},{4,5},{5,4},{6,7},{7,6},{8,9},{9,8},{10,11... | collective-permute-start | bytes 786440 | tf_op jit(solution)/shard_map/ppermute | solution.py:20
  38.7 1.2 collective-permute-start.38
  39.9 3.3 %collective-permute-start.9 = (f32[8,32,512]{2,1,0:T(8,128)S(1)}, f32[8,32,512]{2,1,0:T(8,128)S(1)}, u32[]{:S(2)}, u32[]{:S(2)}) collective-permute-start(f32[8,32,512]{2,1,0:T(8,128)S(1)} %bitcast.9), channel_id=1, source_target_pairs={{0,128},{128,0},{1,129},{129,1},{2,130},{130,2},{3,131},{131,3},{4... | collective-permute-start | bytes 1572872 | tf_op jit(solution)/shard_map/ppermute | solution.py:20
  43.2 1.1 collective-permute-start.28
  44.3 0.3 collective-permute-start.16
  44.6 0.7 collective-permute-done.28.refs_3_
  45.4 0.9 collective-permute-start.32
  46.3 0.8 collective-permute-start.29
  47.2 3.5 %collective-permute-start.17 = (f32[16,16,512]{2,1,0:T(8,128)S(1)}, f32[16,16,512]{2,1,0:T(8,128)S(1)}, u32[]{:S(2)}, u32[]{:S(2)}) collective-permute-start(f32[16,16,512]{2,1,0:T(8,128)S(1)} %pad_maximum_fusion.2.refs_0_), channel_id=1, source_target_pairs={{0,4},{1,13},{4,8},{5,1},{8,12},{9,5},{12,0},{13,9},{2,6},{3,15},{... | collective-permute-start | bytes 1572872 | tf_op jit(solution)/shard_map/ppermute | solution.py:28
  50.7 3.9 %collective-permute-done.38 = f32[512,256]{1,0:T(8,128)S(1)} collective-permute-done((f32[512,256]{1,0:T(8,128)S(1)}, f32[512,256]{1,0:T(8,128)S(1)}, u32[]{:S(2)}, u32[]{:S(2)}) %collective-permute-start.38) | collective-permute-done | bytes 524320 | tf_op jit(solution)/shard_map/ppermute | solution.py:20
  54.6 11.3 %collective-permute-done.9 = f32[8,32,512]{2,1,0:T(8,128)S(1)} collective-permute-done((f32[8,32,512]{2,1,0:T(8,128)S(1)}, f32[8,32,512]{2,1,0:T(8,128)S(1)}, u32[]{:S(2)}, u32[]{:S(2)}) %collective-permute-start.9) | collective-permute-done | bytes 524320 | tf_op jit(solution)/shard_map/ppermute | solution.py:20
  66.0 1.4 collective-permute-start.11
  67.3 0.8 collective-permute-start.33
  68.2 0.8 collective-permute-start.30
  69.0 3.4 %collective-permute-start.21 = (f32[16,16,512]{2,1,0:T(8,128)S(1)}, f32[16,16,512]{2,1,0:T(8,128)S(1)}, u32[]{:S(2)}, u32[]{:S(2)}) collective-permute-start(f32[16,16,512]{2,1,0:T(8,128)S(1)} %collective-permute-done.17.refs_2_), channel_id=1, source_target_pairs={{0,4},{1,13},{4,8},{5,1},{8,12},{9,5},{12,0},{13,9},{2,6},{3,15},{... | collective-permute-start | bytes 1572872 | tf_op jit(solution)/shard_map/ppermute | solution.py:28
  72.5 0.5 collective-permute-start.19
  73.0 2.7 %collective-permute-done.33 = f32[8,32,512]{2,1,0:T(8,128)S(1)} collective-permute-done((f32[8,32,512]{2,1,0:T(8,128)S(1)}, f32[8,32,512]{2,1,0:T(8,128)S(1)}, u32[]{:S(2)}, u32[]{:S(2)}) %collective-permute-start.33) | collective-permute-done | bytes 524320 | tf_op jit(solution)/shard_map/ppermute | solution.py:28
  75.7 2.0 %collective-permute-start.34 = (f32[8,32,512]{2,1,0:T(8,128)S(1)}, f32[8,32,512]{2,1,0:T(8,128)S(1)}, u32[]{:S(2)}, u32[]{:S(2)}) collective-permute-start(f32[8,32,512]{2,1,0:T(8,128)S(1)} %collective-permute-done.33), channel_id=1, source_target_pairs={{0,16},{1,113},{16,32},{17,1},{32,48},{33,17},{48,64},{49,33},{64,... | collective-permute-start | bytes 1572872 | tf_op jit(solution)/shard_map/ppermute | solution.py:28
  77.7 3.6 %collective-permute-done.30.refs_3_ = f32[8,32,512]{2,1,0:T(8,128)S(1)} collective-permute-done((f32[8,32,512]{2,1,0:T(8,128)S(1)}, f32[8,32,512]{2,1,0:T(8,128)S(1)}, u32[]{:S(2)}, u32[]{:S(2)}) %collective-permute-start.30) | collective-permute-done | bytes 524320 | tf_op jit(solution)/shard_map/ppermute | solution.py:28
  81.3 1.7 %collective-permute-start.31 = (f32[8,32,512]{2,1,0:T(8,128)S(1)}, f32[8,32,512]{2,1,0:T(8,128)S(1)}, u32[]{:S(2)}, u32[]{:S(2)}) collective-permute-start(f32[8,32,512]{2,1,0:T(8,128)S(1)} %collective-permute-done.30.refs_3_), channel_id=1, source_target_pairs={{0,16},{1,113},{16,32},{17,1},{32,48},{33,17},{48,64},{49,33},{64,... | collective-permute-start | bytes 1572872 | tf_op jit(solution)/shard_map/ppermute | solution.py:28
  83.0 0.3 collective-permute-start.22
  83.4 0.3 collective-permute-start.39
  83.7 0.3 collective-permute-start.40
  84.1 2.8 %collective-permute-done.34 = f32[8,32,512]{2,1,0:T(8,128)S(1)} collective-permute-done((f32[8,32,512]{2,1,0:T(8,128)S(1)}, f32[8,32,512]{2,1,0:T(8,128)S(1)}, u32[]{:S(2)}, u32[]{:S(2)}) %collective-permute-start.34) | collective-permute-done | bytes 524320 | tf_op jit(solution)/shard_map/ppermute | solution.py:28
  86.9 2.1 %collective-permute-start.41 = (f32[8,32,512]{2,1,0:T(8,128)S(1)}, f32[8,32,512]{2,1,0:T(8,128)S(1)}, u32[]{:S(2)}, u32[]{:S(2)}) collective-permute-start(f32[8,32,512]{2,1,0:T(8,128)S(1)} %collective-permute-done.33), channel_id=1, source_target_pairs={{0,1},{1,0},{2,3},{3,2},{4,5},{5,4},{6,7},{7,6},{8,9},{9,8},{10,11... | collective-permute-start | bytes 1572872 | tf_op jit(solution)/shard_map/ppermute | solution.py:20
  89.1 3.5 %collective-permute-done.31.refs_0_ = f32[8,32,512]{2,1,0:T(8,128)S(1)} collective-permute-done((f32[8,32,512]{2,1,0:T(8,128)S(1)}, f32[8,32,512]{2,1,0:T(8,128)S(1)}, u32[]{:S(2)}, u32[]{:S(2)}) %collective-permute-start.31) | collective-permute-done | bytes 524320 | tf_op jit(solution)/shard_map/ppermute | solution.py:28
  92.5 2.1 %collective-permute-start.35 = (f32[8,32,512]{2,1,0:T(8,128)S(1)}, f32[8,32,512]{2,1,0:T(8,128)S(1)}, u32[]{:S(2)}, u32[]{:S(2)}) collective-permute-start(f32[8,32,512]{2,1,0:T(8,128)S(1)} %collective-permute-done.34), channel_id=1, source_target_pairs={{0,1},{1,0},{2,3},{3,2},{4,5},{5,4},{6,7},{7,6},{8,9},{9,8},{10,11... | collective-permute-start | bytes 1572872 | tf_op jit(solution)/shard_map/ppermute | solution.py:20
  94.7 1.6 %order.1 = (f32[2,512,512]{2,1,0:T(8,128)S(1)}, f32[2,512,512]{2,1,0:T(8,128)S(1)}) custom-call(f32[16,16,512]{2,1,0:T(8,128)S(1)} %pad_maximum_fusion.2.refs_0_, f32[16,16,512]{2,1,0:T(8,128)S(1)} %pad_maximum_fusion.3.refs_1_, f32[16,16,512]{2,1,0:T(8,128)S(1)} %collective-permute-done.17.refs_2_, f32[16,16,512]{2,1,0:T(8,128)S(1)} %collective-permute-done.18.refs_3_, ...), custom_call_target="tpu_custom_call" | custom-call | bytes 8388608 | tf_op jit(solution)/shard_map/order/pallas_call | solution.py:176
  96.3 3.5 %collective-permute-start.10 = (f32[16,32,512]{2,1,0:T(8,128)S(1)}, f32[16,32,512]{2,1,0:T(8,128)S(1)}, u32[]{:S(2)}, u32[]{:S(2)}) collective-permute-start(f32[16,32,512]{2,1,0:T(8,128)S(1)} %pad_maximum_fusion.refs_0_), channel_id=1, source_target_pairs={{0,4},{1,13},{4,8},{5,1},{8,12},{9,5},{12,0},{13,9},{2,6},{3,15},{... | collective-permute-start | bytes 3145736 | tf_op jit(solution)/shard_map/ppermute | solution.py:28
  99.8 0.1 collective-permute-start.12
  99.9 2.3 %solve.1.refs_5_.refs_3_.solved_ref = f32[2,512,256]{2,1,0:T(8,128)S(1)} custom-call(f32[2,512,512]{2,1,0:T(8,128)S(1)} %get-tuple-element.29.inverse_ref, f32[512,256]{1,0:T(8,128)S(1)} %add.13.mine_ref, f32[512,256]{1,0:T(8,128)S(1)} %collective-permute-done.39.other_ref), custom_call_target="tpu_custom_call" | custom-call | flops 3221225472 | bytes 6291456 | tf_op jit(solution)/shard_map/solve/pallas_call | solution.py:229
  102.2 4.0 %project.2.refs_4_ = f32[1024,512]{1,0:T(8,128)S(1)} custom-call(s32[2]{0:T(128)S(1)} %copy-done.5, s32[1024]{0:T(1024)S(1)} %bitcast.14, f32[8,32,512]{2,1,0:T(8,128)S(1)} %bitcast.19, f32[8,32,512]{2,1,0:T(8,128)S(1)} %collective-permute-done.29.refs_1_, f32[8,32,512]{2,1,0:T(8,128)S(1)} %collective-permute-done.40.refs_2_, ...), custom_call_target="tpu_custom_call" | custom-call | flops 1610612736 | bytes 6291456 | tf_op jit(solution)/shard_map/project/pallas_call | solution.py:346
  106.2 3.8 %project.3 = (f32[1024,512]{1,0:T(8,128)S(1)}, f32[512,256]{1,0:T(8,128)S(1)}, f32[512,256]{1,0:T(8,128)S(1)}) custom-call(s32[2]{0:T(128)S(1)} %copy-done.5, s32[1024]{0:T(1024)S(1)} %bitcast.15, f32[8,32,512]{2,1,0:T(8,128)S(1)} %collective-permute-done.31.refs_0_, f32[8,32,512]{2,1,0:T(8,128)S(1)} %collective-permute-done.35.refs_1_, ...), custom_call_target="tpu_custom_call" | custom-call | flops 1610612736 | bytes 6291456 | tf_op jit(solution)/shard_map/project/pallas_call | solution.py:346
  110.0 0.1 collective-permute-start.42
  110.1 1.5 collective-permute-done.10.refs_1_
  111.6 3.1 %collective-permute-start.14 = (f32[16,32,512]{2,1,0:T(8,128)S(1)}, f32[16,32,512]{2,1,0:T(8,128)S(1)}, u32[]{:S(2)}, u32[]{:S(2)}) collective-permute-start(f32[16,32,512]{2,1,0:T(8,128)S(1)} %collective-permute-done.10.refs_1_), channel_id=1, source_target_pairs={{0,4},{1,13},{4,8},{5,1},{8,12},{9,5},{12,0},{13,9},{2,6},{3,15},{... | collective-permute-start | bytes 3145736 | tf_op jit(solution)/shard_map/ppermute | solution.py:28
  114.8 0.1 collective-permute-start.43
  114.9 7.9 %collective-permute-done.12 = f32[16,32,512]{2,1,0:T(8,128)S(1)} collective-permute-done((f32[16,32,512]{2,1,0:T(8,128)S(1)}, f32[16,32,512]{2,1,0:T(8,128)S(1)}, u32[]{:S(2)}, u32[]{:S(2)}) %collective-permute-start.12) | collective-permute-done | bytes 1048608 | tf_op jit(solution)/shard_map/ppermute | solution.py:28
  122.8 1.3 collective-permute-start.13
  124.1 3.3 %collective-permute-done.43 = f32[512,256]{1,0:T(8,128)S(1)} collective-permute-done((f32[512,256]{1,0:T(8,128)S(1)}, f32[512,256]{1,0:T(8,128)S(1)}, u32[]{:S(2)}, u32[]{:S(2)}) %collective-permute-start.43) | collective-permute-done | bytes 524320 | tf_op jit(solution)/shard_map/ppermute | solution.py:20
  127.6 7.5 %scatter.1.refs_7_ = f32[2,2048,256]{2,1,0:T(8,128)S(1)} custom-call(s32[2]{0:T(128)S(1)} %copy-done.5, s32[1024]{0:T(1024)S(1)} %bitcast.16, f32[2,2048,256]{2,1,0:T(8,128)S(1)} %copy-done.1, f32[1024,512]{1,0:T(8,128)S(1)} %get-tuple-element.34.update_ref, f32[2,512,256]{2,1,0:T(8,128)S(1)} %solve.1.refs_5_.refs_3_.solved_ref), custom_call_target="tpu_custom_call" | custom-call | flops 1048576 | bytes 25165824 | tf_op jit(solution)/shard_map/scatter/pallas_call | solution.py:422
  135.1 13.4 %finish.1 = f32[2,2048,256]{2,1,0:T(8,128)} custom-call(s32[2]{0:T(128)S(1)} %copy-done.5, s32[1024]{0:T(1024)S(1)} %bitcast.17, f32[16,32,512]{2,1,0:T(8,128)S(1)} %pad_maximum_fusion.refs_0_, f32[16,32,512]{2,1,0:T(8,128)S(1)} %collective-permute-done.10.refs_1_, f32[16,32,512]{2,1,0:T(8,128)S(1)} %collective-permute-done.13.refs_2_, ...), custom_call_target="tpu_custom_call" | custom-call | flops 4831838208 | bytes 13631488 | tf_op jit(solution)/shard_map/finish/pallas_call | solution.py:483
  (65 shorter events, 0.9 us)
Async XLA Ops:
  0.0 0.9 copy-start.2
  0.9 0.8 copy-start.3
  1.8 4.2 %collective-permute-start = (f32[1,48,512]{2,1,0:T(8,128)S(1)}, f32[1,48,512]{2,1,0:T(8,128)S(1)}, u32[]{:S(2)}, u32[]{:S(2)}) collective-permute-start(f32[1,48,512]{2,1,0:T(8,128)S(1)} %get-tuple-element.20), channel_id=1, source_target_pairs={{0,1},{1,0},{2,3},{3,2},{4,5},{5,4},{6,7},{7,6},{8,9},{9,8},{10,11... | collective-permute-start | bytes 294920 | tf_op jit(solution)/shard_map/ppermute | solution.py:20
  6.0 8.1 %collective-permute-start.3 = (f32[2,48,512]{2,1,0:T(8,128)S(1)}, f32[2,48,512]{2,1,0:T(8,128)S(1)}, u32[]{:S(2)}, u32[]{:S(2)}) collective-permute-start(f32[2,48,512]{2,1,0:T(8,128)S(1)} %constant_dynamic-update-slice_fusion.own_ref), channel_id=1, source_target_pairs={{0,32},{1,97},{16,48},{17,113},{32,64},{33,1},{48,80},{49,17},{64,... | collective-permute-start | bytes 589832 | tf_op jit(solution)/shard_map/ppermute | solution.py:28
  10.4 7.8 %collective-permute-start.23 = (f32[1,32,512]{2,1,0:T(8,128)S(1)}, f32[1,32,512]{2,1,0:T(8,128)S(1)}, u32[]{:S(2)}, u32[]{:S(2)}) collective-permute-start(f32[1,32,512]{2,1,0:T(8,128)S(1)} %get-tuple-element.26), channel_id=1, source_target_pairs={{0,128},{128,0},{1,129},{129,1},{2,130},{130,2},{3,131},{131,3},{4... | collective-permute-start | bytes 196616 | tf_op jit(solution)/shard_map/ppermute | solution.py:20
  13.3 10.6 %collective-permute-start.1 = (f32[2,48,512]{2,1,0:T(8,128)S(1)}, f32[2,48,512]{2,1,0:T(8,128)S(1)}, u32[]{:S(2)}, u32[]{:S(2)}) collective-permute-start(f32[2,48,512]{2,1,0:T(8,128)S(1)} %constant_dynamic-update-slice_fusion.own_ref), channel_id=1, source_target_pairs={{0,16},{1,113},{16,32},{17,1},{32,48},{33,17},{48,64},{49,33},{64,... | collective-permute-start | bytes 589832 | tf_op jit(solution)/shard_map/ppermute | solution.py:28
  14.1 15.6 %collective-permute-start.5 = (f32[2,48,512]{2,1,0:T(8,128)S(1)}, f32[2,48,512]{2,1,0:T(8,128)S(1)}, u32[]{:S(2)}, u32[]{:S(2)}) collective-permute-start(f32[2,48,512]{2,1,0:T(8,128)S(1)} %collective-permute-done.3.refs_2_), channel_id=1, source_target_pairs={{0,16},{1,113},{16,32},{17,1},{32,48},{33,17},{48,64},{49,33},{64,... | collective-permute-start | bytes 589832 | tf_op jit(solution)/shard_map/ppermute | solution.py:28
  18.2 5.7 %collective-permute-start.24 = (f32[2,32,512]{2,1,0:T(8,128)S(1)}, f32[2,32,512]{2,1,0:T(8,128)S(1)}, u32[]{:S(2)}, u32[]{:S(2)}) collective-permute-start(f32[2,32,512]{2,1,0:T(8,128)S(1)} %get-tuple-element.35), channel_id=1, source_target_pairs={{0,1},{1,0},{2,3},{3,2},{4,5},{5,4},{6,7},{7,6},{8,9},{9,8},{10,11... | collective-permute-start | bytes 393224 | tf_op jit(solution)/shard_map/ppermute | solution.py:20
  18.3 2.2 %copy-start = (f32[2,2048,256]{2,1,0:T(8,128)S(1)}, f32[2,2048,256]{2,1,0:T(8,128)}, u32[]{:S(2)}) copy-start(f32[2,2048,256]{2,1,0:T(8,128)} %front_ref.3) | copy-start | bytes 12582916
  20.5 0.7 copy-start.4
  21.8 16.8 %collective-permute-start.37 = (f32[512,256]{1,0:T(8,128)S(1)}, f32[512,256]{1,0:T(8,128)S(1)}, u32[]{:S(2)}, u32[]{:S(2)}) collective-permute-start(f32[512,256]{1,0:T(8,128)S(1)} %get-tuple-element.31), channel_id=1, source_target_pairs={{0,1},{1,0},{2,3},{3,2},{4,5},{5,4},{6,7},{7,6},{8,9},{9,8},{10,11... | collective-permute-start | bytes 1572872 | tf_op jit(solution)/shard_map/ppermute | solution.py:20
  22.4 4.5 %collective-permute-start.7 = (f32[1,48,512]{2,1,0:T(8,128)S(1)}, f32[1,48,512]{2,1,0:T(8,128)S(1)}, u32[]{:S(2)}, u32[]{:S(2)}) collective-permute-start(f32[1,48,512]{2,1,0:T(8,128)S(1)} %slice.14), channel_id=1, source_target_pairs={{0,32},{1,97},{16,48},{17,113},{32,64},{33,1},{48,80},{49,17},{64,... | collective-permute-start | bytes 294920 | tf_op jit(solution)/shard_map/ppermute | solution.py:28
  23.9 9.1 %collective-permute-start.4 = (f32[2,48,512]{2,1,0:T(8,128)S(1)}, f32[2,48,512]{2,1,0:T(8,128)S(1)}, u32[]{:S(2)}, u32[]{:S(2)}) collective-permute-start(f32[2,48,512]{2,1,0:T(8,128)S(1)} %collective-permute-done.3.refs_2_), channel_id=1, source_target_pairs={{0,1},{1,0},{2,3},{3,2},{4,5},{5,4},{6,7},{7,6},{8,9},{9,8},{10,11... | collective-permute-start | bytes 589832 | tf_op jit(solution)/shard_map/ppermute | solution.py:20
  23.9 9.1 %collective-permute-start.2 = (f32[2,48,512]{2,1,0:T(8,128)S(1)}, f32[2,48,512]{2,1,0:T(8,128)S(1)}, u32[]{:S(2)}, u32[]{:S(2)}) collective-permute-start(f32[2,48,512]{2,1,0:T(8,128)S(1)} %collective-permute-done.1.refs_0_), channel_id=1, source_target_pairs={{0,1},{1,0},{2,3},{3,2},{4,5},{5,4},{6,7},{7,6},{8,9},{9,8},{10,11... | collective-permute-start | bytes 589832 | tf_op jit(solution)/shard_map/ppermute | solution.py:20
  26.9 3.8 %collective-permute-start.8 = (f32[1,48,512]{2,1,0:T(8,128)S(1)}, f32[1,48,512]{2,1,0:T(8,128)S(1)}, u32[]{:S(2)}, u32[]{:S(2)}) collective-permute-start(f32[1,48,512]{2,1,0:T(8,128)S(1)} %collective-permute-done.7.refs_6_), channel_id=1, source_target_pairs={{0,1},{1,0},{2,3},{3,2},{4,5},{5,4},{6,7},{7,6},{8,9},{9,8},{10,11... | collective-permute-start | bytes 294920 | tf_op jit(solution)/shard_map/ppermute | solution.py:20
  29.7 3.3 %collective-permute-start.6 = (f32[2,48,512]{2,1,0:T(8,128)S(1)}, f32[2,48,512]{2,1,0:T(8,128)S(1)}, u32[]{:S(2)}, u32[]{:S(2)}) collective-permute-start(f32[2,48,512]{2,1,0:T(8,128)S(1)} %collective-permute-done.5.refs_4_), channel_id=1, source_target_pairs={{0,1},{1,0},{2,3},{3,2},{4,5},{5,4},{6,7},{7,6},{8,9},{9,8},{10,11... | collective-permute-start | bytes 589832 | tf_op jit(solution)/shard_map/ppermute | solution.py:20
  30.7 6.1 %collective-permute-start.25 = (f32[4,32,512]{2,1,0:T(8,128)S(1)}, f32[4,32,512]{2,1,0:T(8,128)S(1)}, u32[]{:S(2)}, u32[]{:S(2)}) collective-permute-start(f32[4,32,512]{2,1,0:T(8,128)S(1)} %constant_dynamic-update-slice_fusion.4.own_ref), channel_id=1, source_target_pairs={{0,4},{1,13},{4,8},{5,1},{8,12},{9,5},{12,0},{13,9},{2,6},{3,15},{... | collective-permute-start | bytes 786440 | tf_op jit(solution)/shard_map/ppermute | solution.py:28
  33.2 11.2 %collective-permute-start.15 = (f32[8,16,512]{2,1,0:T(8,128)S(1)}, f32[8,16,512]{2,1,0:T(8,128)S(1)}, u32[]{:S(2)}, u32[]{:S(2)}) collective-permute-start(f32[8,16,512]{2,1,0:T(8,128)S(1)} %bitcast.12), channel_id=1, source_target_pairs={{0,128},{128,0},{1,129},{129,1},{2,130},{130,2},{3,131},{131,3},{4... | collective-permute-start | bytes 786440 | tf_op jit(solution)/shard_map/ppermute | solution.py:20
  36.1 7.2 %collective-permute-start.27 = (f32[2,32,512]{2,1,0:T(8,128)S(1)}, f32[2,32,512]{2,1,0:T(8,128)S(1)}, u32[]{:S(2)}, u32[]{:S(2)}) collective-permute-start(f32[2,32,512]{2,1,0:T(8,128)S(1)} %get-tuple-element.35), channel_id=1, source_target_pairs={{0,8},{1,9},{4,12},{5,13},{8,0},{9,1},{12,4},{13,5},{2,10},{3,11},... | collective-permute-start | bytes 393224 | tf_op jit(solution)/shard_map/ppermute | solution.py:28
  36.8 8.5 %collective-permute-start.26 = (f32[4,32,512]{2,1,0:T(8,128)S(1)}, f32[4,32,512]{2,1,0:T(8,128)S(1)}, u32[]{:S(2)}, u32[]{:S(2)}) collective-permute-start(f32[4,32,512]{2,1,0:T(8,128)S(1)} %collective-permute-done.25.refs_0_), channel_id=1, source_target_pairs={{0,1},{1,0},{2,3},{3,2},{4,5},{5,4},{6,7},{7,6},{8,9},{9,8},{10,11... | collective-permute-start | bytes 786440 | tf_op jit(solution)/shard_map/ppermute | solution.py:20
  38.7 15.9 %collective-permute-start.38 = (f32[512,256]{1,0:T(8,128)S(1)}, f32[512,256]{1,0:T(8,128)S(1)}, u32[]{:S(2)}, u32[]{:S(2)}) collective-permute-start(f32[512,256]{1,0:T(8,128)S(1)} %add.12), channel_id=1, source_target_pairs={{0,2},{2,0},{1,3},{3,1},{4,6},{6,4},{5,7},{7,5},{8,10},{10,8},{9,1... | collective-permute-start | bytes 1572872 | tf_op jit(solution)/shard_map/ppermute | solution.py:20
  39.9 26.0 %collective-permute-start.9 = (f32[8,32,512]{2,1,0:T(8,128)S(1)}, f32[8,32,512]{2,1,0:T(8,128)S(1)}, u32[]{:S(2)}, u32[]{:S(2)}) collective-permute-start(f32[8,32,512]{2,1,0:T(8,128)S(1)} %bitcast.9), channel_id=1, source_target_pairs={{0,128},{128,0},{1,129},{129,1},{2,130},{130,2},{3,131},{131,3},{4... | collective-permute-start | bytes 1572872 | tf_op jit(solution)/shard_map/ppermute | solution.py:20
  43.2 2.1 %collective-permute-start.28 = (f32[2,32,512]{2,1,0:T(8,128)S(1)}, f32[2,32,512]{2,1,0:T(8,128)S(1)}, u32[]{:S(2)}, u32[]{:S(2)}) collective-permute-start(f32[2,32,512]{2,1,0:T(8,128)S(1)} %collective-permute-done.27.refs_2_), channel_id=1, source_target_pairs={{0,1},{1,0},{2,3},{3,2},{4,5},{5,4},{6,7},{7,6},{8,9},{9,8},{10,11... | collective-permute-start | bytes 393224 | tf_op jit(solution)/shard_map/ppermute | solution.py:20
  44.3 2.9 %collective-permute-start.16 = (f32[8,16,512]{2,1,0:T(8,128)S(1)}, f32[8,16,512]{2,1,0:T(8,128)S(1)}, u32[]{:S(2)}, u32[]{:S(2)}) collective-permute-start(f32[8,16,512]{2,1,0:T(8,128)S(1)} %collective-permute-done.15), channel_id=1, source_target_pairs={{0,1},{1,0},{2,3},{3,2},{4,5},{5,4},{6,7},{7,6},{8,9},{9,8},{10,11... | collective-permute-start | bytes 786440 | tf_op jit(solution)/shard_map/ppermute | solution.py:20
  45.4 38.7 %copy-start.6 = (s32[2,1024]{1,0:T(2,128)S(1)}, s32[2,1024]{1,0:T(2,128)}, u32[]{:S(2)}) copy-start(s32[2,1024]{1,0:T(2,128)} %param.8) | copy-start | bytes 24580
  45.4 22.0 %collective-permute-start.32 = (f32[8,32,512]{2,1,0:T(8,128)S(1)}, f32[8,32,512]{2,1,0:T(8,128)S(1)}, u32[]{:S(2)}, u32[]{:S(2)}) collective-permute-start(f32[8,32,512]{2,1,0:T(8,128)S(1)} %bitcast.20), channel_id=1, source_target_pairs={{0,16},{1,113},{16,32},{17,1},{32,48},{33,17},{48,64},{49,33},{64,... | collective-permute-start | bytes 1572872 | tf_op jit(solution)/shard_map/ppermute | solution.py:28
  46.3 21.9 %collective-permute-start.29 = (f32[8,32,512]{2,1,0:T(8,128)S(1)}, f32[8,32,512]{2,1,0:T(8,128)S(1)}, u32[]{:S(2)}, u32[]{:S(2)}) collective-permute-start(f32[8,32,512]{2,1,0:T(8,128)S(1)} %bitcast.18), channel_id=1, source_target_pairs={{0,16},{1,113},{16,32},{17,1},{32,48},{33,17},{48,64},{49,33},{64,... | collective-permute-start | bytes 1572872 | tf_op jit(solution)/shard_map/ppermute | solution.py:28
  47.2 21.8 %collective-permute-start.17 = (f32[16,16,512]{2,1,0:T(8,128)S(1)}, f32[16,16,512]{2,1,0:T(8,128)S(1)}, u32[]{:S(2)}, u32[]{:S(2)}) collective-permute-start(f32[16,16,512]{2,1,0:T(8,128)S(1)} %pad_maximum_fusion.2.refs_0_), channel_id=1, source_target_pairs={{0,4},{1,13},{4,8},{5,1},{8,12},{9,5},{12,0},{13,9},{2,6},{3,15},{... | collective-permute-start | bytes 1572872 | tf_op jit(solution)/shard_map/ppermute | solution.py:28
  54.6 17.8 %collective-permute-start.18 = (f32[16,16,512]{2,1,0:T(8,128)S(1)}, f32[16,16,512]{2,1,0:T(8,128)S(1)}, u32[]{:S(2)}, u32[]{:S(2)}) collective-permute-start(f32[16,16,512]{2,1,0:T(8,128)S(1)} %pad_maximum_fusion.3.refs_1_), channel_id=1, source_target_pairs={{0,4},{1,13},{4,8},{5,1},{8,12},{9,5},{12,0},{13,9},{2,6},{3,15},{... | collective-permute-start | bytes 1572872 | tf_op jit(solution)/shard_map/ppermute | solution.py:28
  66.0 6.5 %collective-permute-start.11 = (f32[8,32,512]{2,1,0:T(8,128)S(1)}, f32[8,32,512]{2,1,0:T(8,128)S(1)}, u32[]{:S(2)}, u32[]{:S(2)}) collective-permute-start(f32[8,32,512]{2,1,0:T(8,128)S(1)} %collective-permute-done.9), channel_id=1, source_target_pairs={{0,1},{1,0},{2,3},{3,2},{4,5},{5,4},{6,7},{7,6},{8,9},{9,8},{10,11... | collective-permute-start | bytes 1572872 | tf_op jit(solution)/shard_map/ppermute | solution.py:20
  67.3 8.3 %collective-permute-start.33 = (f32[8,32,512]{2,1,0:T(8,128)S(1)}, f32[8,32,512]{2,1,0:T(8,128)S(1)}, u32[]{:S(2)}, u32[]{:S(2)}) collective-permute-start(f32[8,32,512]{2,1,0:T(8,128)S(1)} %collective-permute-done.32), channel_id=1, source_target_pairs={{0,16},{1,113},{16,32},{17,1},{32,48},{33,17},{48,64},{49,33},{64,... | collective-permute-start | bytes 1572872 | tf_op jit(solution)/shard_map/ppermute | solution.py:28
  68.2 13.1 %collective-permute-start.30 = (f32[8,32,512]{2,1,0:T(8,128)S(1)}, f32[8,32,512]{2,1,0:T(8,128)S(1)}, u32[]{:S(2)}, u32[]{:S(2)}) collective-permute-start(f32[8,32,512]{2,1,0:T(8,128)S(1)} %collective-permute-done.29.refs_1_), channel_id=1, source_target_pairs={{0,16},{1,113},{16,32},{17,1},{32,48},{33,17},{48,64},{49,33},{64,... | collective-permute-start | bytes 1572872 | tf_op jit(solution)/shard_map/ppermute | solution.py:28
  69.0 14.0 %collective-permute-start.21 = (f32[16,16,512]{2,1,0:T(8,128)S(1)}, f32[16,16,512]{2,1,0:T(8,128)S(1)}, u32[]{:S(2)}, u32[]{:S(2)}) collective-permute-start(f32[16,16,512]{2,1,0:T(8,128)S(1)} %collective-permute-done.17.refs_2_), channel_id=1, source_target_pairs={{0,4},{1,13},{4,8},{5,1},{8,12},{9,5},{12,0},{13,9},{2,6},{3,15},{... | collective-permute-start | bytes 1572872 | tf_op jit(solution)/shard_map/ppermute | solution.py:28
  72.4 11.0 %collective-permute-start.20 = (f32[16,16,512]{2,1,0:T(8,128)S(1)}, f32[16,16,512]{2,1,0:T(8,128)S(1)}, u32[]{:S(2)}, u32[]{:S(2)}) collective-permute-start(f32[16,16,512]{2,1,0:T(8,128)S(1)} %collective-permute-done.17.refs_2_), channel_id=1, source_target_pairs={{0,1},{1,0},{2,3},{3,2},{4,5},{5,4},{6,7},{7,6},{8,9},{9,8},{10,11... | collective-permute-start | bytes 1572872 | tf_op jit(solution)/shard_map/ppermute | solution.py:20
  72.5 11.3 %collective-permute-start.19 = (f32[16,16,512]{2,1,0:T(8,128)S(1)}, f32[16,16,512]{2,1,0:T(8,128)S(1)}, u32[]{:S(2)}, u32[]{:S(2)}) collective-permute-start(f32[16,16,512]{2,1,0:T(8,128)S(1)} %collective-permute-done.18.refs_3_), channel_id=1, source_target_pairs={{0,1},{1,0},{2,3},{3,2},{4,5},{5,4},{6,7},{7,6},{8,9},{9,8},{10,11... | collective-permute-start | bytes 1572872 | tf_op jit(solution)/shard_map/ppermute | solution.py:20
  75.7 11.2 %collective-permute-start.34 = (f32[8,32,512]{2,1,0:T(8,128)S(1)}, f32[8,32,512]{2,1,0:T(8,128)S(1)}, u32[]{:S(2)}, u32[]{:S(2)}) collective-permute-start(f32[8,32,512]{2,1,0:T(8,128)S(1)} %collective-permute-done.33), channel_id=1, source_target_pairs={{0,16},{1,113},{16,32},{17,1},{32,48},{33,17},{48,64},{49,33},{64,... | collective-permute-start | bytes 1572872 | tf_op jit(solution)/shard_map/ppermute | solution.py:28
  81.3 11.2 %collective-permute-start.31 = (f32[8,32,512]{2,1,0:T(8,128)S(1)}, f32[8,32,512]{2,1,0:T(8,128)S(1)}, u32[]{:S(2)}, u32[]{:S(2)}) collective-permute-start(f32[8,32,512]{2,1,0:T(8,128)S(1)} %collective-permute-done.30.refs_3_), channel_id=1, source_target_pairs={{0,16},{1,113},{16,32},{17,1},{32,48},{33,17},{48,64},{49,33},{64,... | collective-permute-start | bytes 1572872 | tf_op jit(solution)/shard_map/ppermute | solution.py:28
  83.0 11.6 %collective-permute-start.22 = (f32[16,16,512]{2,1,0:T(8,128)S(1)}, f32[16,16,512]{2,1,0:T(8,128)S(1)}, u32[]{:S(2)}, u32[]{:S(2)}) collective-permute-start(f32[16,16,512]{2,1,0:T(8,128)S(1)} %collective-permute-done.21.refs_6_), channel_id=1, source_target_pairs={{0,1},{1,0},{2,3},{3,2},{4,5},{5,4},{6,7},{7,6},{8,9},{9,8},{10,11... | collective-permute-start | bytes 1572872 | tf_op jit(solution)/shard_map/ppermute | solution.py:20
  83.4 12.9 %collective-permute-start.39 = (f32[512,256]{1,0:T(8,128)S(1)}, f32[512,256]{1,0:T(8,128)S(1)}, u32[]{:S(2)}, u32[]{:S(2)}) collective-permute-start(f32[512,256]{1,0:T(8,128)S(1)} %add.13.mine_ref), channel_id=1, source_target_pairs={{0,1},{1,0},{2,3},{3,2},{4,5},{5,4},{6,7},{7,6},{8,9},{9,8},{10,11... | collective-permute-start | bytes 1572872 | tf_op jit(solution)/shard_map/ppermute | solution.py:20
  83.7 16.1 %collective-permute-start.40 = (f32[8,32,512]{2,1,0:T(8,128)S(1)}, f32[8,32,512]{2,1,0:T(8,128)S(1)}, u32[]{:S(2)}, u32[]{:S(2)}) collective-permute-start(f32[8,32,512]{2,1,0:T(8,128)S(1)} %collective-permute-done.32), channel_id=1, source_target_pairs={{0,1},{1,0},{2,3},{3,2},{4,5},{5,4},{6,7},{7,6},{8,9},{9,8},{10,11... | collective-permute-start | bytes 1572872 | tf_op jit(solution)/shard_map/ppermute | solution.py:20
  86.9 15.3 %collective-permute-start.41 = (f32[8,32,512]{2,1,0:T(8,128)S(1)}, f32[8,32,512]{2,1,0:T(8,128)S(1)}, u32[]{:S(2)}, u32[]{:S(2)}) collective-permute-start(f32[8,32,512]{2,1,0:T(8,128)S(1)} %collective-permute-done.33), channel_id=1, source_target_pairs={{0,1},{1,0},{2,3},{3,2},{4,5},{5,4},{6,7},{7,6},{8,9},{9,8},{10,11... | collective-permute-start | bytes 1572872 | tf_op jit(solution)/shard_map/ppermute | solution.py:20
  92.5 13.7 %collective-permute-start.35 = (f32[8,32,512]{2,1,0:T(8,128)S(1)}, f32[8,32,512]{2,1,0:T(8,128)S(1)}, u32[]{:S(2)}, u32[]{:S(2)}) collective-permute-start(f32[8,32,512]{2,1,0:T(8,128)S(1)} %collective-permute-done.34), channel_id=1, source_target_pairs={{0,1},{1,0},{2,3},{3,2},{4,5},{5,4},{6,7},{7,6},{8,9},{9,8},{10,11... | collective-permute-start | bytes 1572872 | tf_op jit(solution)/shard_map/ppermute | solution.py:20
  94.6 11.6 %collective-permute-start.36 = (f32[8,32,512]{2,1,0:T(8,128)S(1)}, f32[8,32,512]{2,1,0:T(8,128)S(1)}, u32[]{:S(2)}, u32[]{:S(2)}) collective-permute-start(f32[8,32,512]{2,1,0:T(8,128)S(1)} %collective-permute-done.31.refs_0_), channel_id=1, source_target_pairs={{0,16},{1,113},{16,32},{17,1},{32,48},{33,17},{48,64},{49,33},{64,... | collective-permute-start | bytes 1572872 | tf_op jit(solution)/shard_map/ppermute | solution.py:28
  96.3 15.2 %collective-permute-start.10 = (f32[16,32,512]{2,1,0:T(8,128)S(1)}, f32[16,32,512]{2,1,0:T(8,128)S(1)}, u32[]{:S(2)}, u32[]{:S(2)}) collective-permute-start(f32[16,32,512]{2,1,0:T(8,128)S(1)} %pad_maximum_fusion.refs_0_), channel_id=1, source_target_pairs={{0,4},{1,13},{4,8},{5,1},{8,12},{9,5},{12,0},{13,9},{2,6},{3,15},{... | collective-permute-start | bytes 3145736 | tf_op jit(solution)/shard_map/ppermute | solution.py:28
  99.8 23.0 %collective-permute-start.12 = (f32[16,32,512]{2,1,0:T(8,128)S(1)}, f32[16,32,512]{2,1,0:T(8,128)S(1)}, u32[]{:S(2)}, u32[]{:S(2)}) collective-permute-start(f32[16,32,512]{2,1,0:T(8,128)S(1)} %pad_maximum_fusion.1), channel_id=1, source_target_pairs={{0,4},{1,13},{4,8},{5,1},{8,12},{9,5},{12,0},{13,9},{2,6},{3,15},{... | collective-permute-start | bytes 3145736 | tf_op jit(solution)/shard_map/ppermute | solution.py:28
  99.9 2.3 %copy-start.5 = (s32[2]{0:T(128)S(1)}, s32[2]{0:T(128)}, u32[]{:S(2)}) copy-start(s32[2]{0:T(128)} %block_ref.9) | copy-start | bytes 28
  102.2 4.0 %copy-start.1 = (f32[2,2048,256]{2,1,0:T(8,128)S(1)}, f32[2,2048,256]{2,1,0:T(8,128)}, u32[]{:S(2)}) copy-start(f32[2,2048,256]{2,1,0:T(8,128)} %front_ref.3) | copy-start | bytes 12582916
  110.0 4.7 %collective-permute-start.42 = (f32[512,256]{1,0:T(8,128)S(1)}, f32[512,256]{1,0:T(8,128)S(1)}, u32[]{:S(2)}, u32[]{:S(2)}) collective-permute-start(f32[512,256]{1,0:T(8,128)S(1)} %get-tuple-element.33), channel_id=1, source_target_pairs={{0,1},{1,0},{2,3},{3,2},{4,5},{5,4},{6,7},{7,6},{8,9},{9,8},{10,11... | collective-permute-start | bytes 1572872 | tf_op jit(solution)/shard_map/ppermute | solution.py:20
  111.6 23.5 %collective-permute-start.14 = (f32[16,32,512]{2,1,0:T(8,128)S(1)}, f32[16,32,512]{2,1,0:T(8,128)S(1)}, u32[]{:S(2)}, u32[]{:S(2)}) collective-permute-start(f32[16,32,512]{2,1,0:T(8,128)S(1)} %collective-permute-done.10.refs_1_), channel_id=1, source_target_pairs={{0,4},{1,13},{4,8},{5,1},{8,12},{9,5},{12,0},{13,9},{2,6},{3,15},{... | collective-permute-start | bytes 3145736 | tf_op jit(solution)/shard_map/ppermute | solution.py:28
  114.8 12.7 %collective-permute-start.43 = (f32[512,256]{1,0:T(8,128)S(1)}, f32[512,256]{1,0:T(8,128)S(1)}, u32[]{:S(2)}, u32[]{:S(2)}) collective-permute-start(f32[512,256]{1,0:T(8,128)S(1)} %add.14), channel_id=1, source_target_pairs={{0,2},{2,0},{1,3},{3,1},{4,6},{6,4},{5,7},{7,5},{8,10},{10,8},{9,1... | collective-permute-start | bytes 1572872 | tf_op jit(solution)/shard_map/ppermute | solution.py:20
  122.8 12.3 %collective-permute-start.13 = (f32[16,32,512]{2,1,0:T(8,128)S(1)}, f32[16,32,512]{2,1,0:T(8,128)S(1)}, u32[]{:S(2)}, u32[]{:S(2)}) collective-permute-start(f32[16,32,512]{2,1,0:T(8,128)S(1)} %collective-permute-done.12), channel_id=1, source_target_pairs={{0,1},{1,0},{2,3},{3,2},{4,5},{5,4},{6,7},{7,6},{8,9},{9,8},{10,11... | collective-permute-start | bytes 3145736 | tf_op jit(solution)/shard_map/ppermute | solution.py:20
  127.5 7.6 %collective-permute-start.44 = (f32[512,256]{1,0:T(8,128)S(1)}, f32[512,256]{1,0:T(8,128)S(1)}, u32[]{:S(2)}, u32[]{:S(2)}) collective-permute-start(f32[512,256]{1,0:T(8,128)S(1)} %add.15.refs_5_), channel_id=1, source_target_pairs={{0,1},{1,0},{2,3},{3,2},{4,5},{5,4},{6,7},{7,6},{8,9},{9,8},{10,11... | collective-permute-start | bytes 1572872 | tf_op jit(solution)/shard_map/ppermute | solution.py:20

commit v2 on v1

--- a/solution.py
+++ b/solution.py
@@ -95,13 +95,13 @@
         grid_spec=pltpu.PrefetchScalarGridSpec(
             num_scalar_prefetch=1,
             grid=(1,),
-            in_specs=[ANYWHERE],
+            in_specs=[OUTSIDE],
             out_specs=[whole(s) for s in shapes],
             scratch_shapes=[pltpu.VMEM((2, depth, width), jnp.float32), pltpu.SemaphoreType.DMA],
         ),
         out_shape=shapes,
         cost_estimate=pl.CostEstimate(flops=0, bytes_accessed=2 * MIB, transcendentals=0),
-        compiler_params=pltpu.CompilerParams(vmem_limit_bytes=8 * MIB),
+        compiler_params=pltpu.CompilerParams(vmem_limit_bytes=50 * MIB),
         name="take",
     )(blocks, front)
 
@@ -152,6 +152,9 @@
 
 
 ANYWHERE = pl.BlockSpec(memory_space=pl.ANY)
+OUTSIDE = pl.BlockSpec(memory_space=pltpu.HBM)
+INSIDE = pl.BlockSpec(memory_space=pltpu.VMEM)
+SCALARS = pl.BlockSpec(memory_space=pltpu.SMEM)
 
 
 def order_kernel(*refs):
@@ -228,9 +231,8 @@
     shape = jax.ShapeDtypeStruct((2, depth, width), jnp.float32)
     return pl.pallas_call(
         solve_into,
-        grid=(1,),
-        in_specs=[whole(inverse), whole(mine), whole(other)],
-        out_specs=whole(shape),
+        in_specs=[INSIDE] * 3,
+        out_specs=INSIDE,
         scratch_shapes=[pltpu.VMEM((2 * depth, 2 * width), jnp.bfloat16)] * 2,
         out_shape=shape,
         cost_estimate=pl.CostEstimate(flops=6 * 2 * depth * 2 * depth * 2 * width, bytes_accessed=6 * MIB, transcendentals=0),
@@ -275,12 +277,14 @@
     if first:
         solved_ref, out_ref = refs[pieces : pieces + 2]
     else:
-        solved_ref, so_far_ref, front_ref, out_ref, mine_ref, other_ref, sums_ref, pivot_ref, pivot_sem = refs[pieces:-4]
+        solved_ref, so_far_ref, front_ref, out_ref, mine_ref, other_ref, sums_ref, pivot_ref, more_sem = refs[pieces:-4]
         depth, width = mine_ref.shape
-        pivot = pltpu.make_async_copy(front_ref.at[:, pl.ds(first_row, depth), :], pivot_ref, pivot_sem)
-        pivot.start()
-        sums_ref[:1024, :] = so_far_ref[...]
-    target_ref = out_ref if first else sums_ref
+        more = [
+            pltpu.make_async_copy(so_far_ref, sums_ref.at[pl.ds(0, 1024)], more_sem.at[0]),
+            pltpu.make_async_copy(front_ref.at[:, pl.ds(first_row, depth), :], pivot_ref, more_sem.at[1]),
+        ]
+        for copy in more:
+            copy.start()
     put_operand(solved_ref[0], solved_ref[1], high_ref, low_ref)
     for copy in copies:
         copy.wait()
@@ -288,13 +292,22 @@
     @pl.loop(0, panel_ref.shape[0] // 8)
     def _(m):
         result = multiply_panel(panel_ref[pl.ds(m * 8, 8)], high_ref, low_ref)
+        if not first:
+            out_ref[pl.ds(pl.multiple_of(m * 128, 128), 128), :] = result
+            return
         for j in range(8):
             row = pl.multiple_of(source(done + m * 8 + j, False) * 16, 16)
-            target_ref[pl.ds(row, 16), :] = result[j * 16 : (j + 1) * 16]
+            out_ref[pl.ds(row, 16), :] = result[j * 16 : (j + 1) * 16]
 
     if not first:
-        out_ref[...] = sums_ref[:1024, :]
-        pivot.wait()
+        for copy in more:
+            copy.wait()
+
+        @pl.loop(0, panel_ref.shape[0], unroll=4)
+        def _(piece):
+            row = pl.multiple_of(source(done + piece, False) * 16, 16)
+            sums_ref[pl.ds(row, 16), :] = out_ref[pl.ds(pl.multiple_of(piece * 16, 16), 16), :]
+
 
         @pl.when(owned)
         def _():
@@ -304,7 +317,7 @@
             in_first = lax.broadcasted_iota(jnp.int32, (8, 2 * width), 0) < 8 - past
             core_first = lax.axis_index("c") == 0
 
-            @pl.loop(0, depth // 8)
+            @pl.loop(0, depth // 8, unroll=4)
             def _(m):
                 rows = pl.ds(pl.multiple_of(m * 8, 8), 8)
                 base = pl.multiple_of(start - past + m * 8, 8)
@@ -325,38 +338,33 @@
 def project(blocks, slots, panels, done, solved, so_far=None, front=None):
     _, depth, width = solved.shape
     first = so_far is None
-    inputs = [solved] if first else [solved, so_far]
-    shapes = [jax.ShapeDtypeStruct((1024, 2 * width), jnp.float32)]
-    in_specs = [ANYWHERE] * len(panels) + [whole(a) for a in inputs]
+    count = sum(a.shape[0] for a in panels)
+    rows = 1024 if first else count * 16
+    inputs = [*panels, solved] if first else [*panels, solved, so_far, front]
+    shapes = [jax.ShapeDtypeStruct((rows, 2 * width), jnp.float32)]
     scratch = [
-        pltpu.VMEM((sum(a.shape[0] for a in panels), 32, depth), jnp.float32),
+        pltpu.VMEM((count, 32, depth), jnp.float32),
         pltpu.VMEM((2 * depth, 2 * width), jnp.bfloat16),
         pltpu.VMEM((2 * depth, 2 * width), jnp.bfloat16),
         pltpu.SemaphoreType.DMA((len(panels),)),
     ]
     if not first:
-        inputs.append(front)
-        in_specs.append(ANYWHERE)
         shapes += [jax.ShapeDtypeStruct((depth, width), jnp.float32)] * 2
         scratch = [
             pltpu.VMEM((1032, 2 * width), jnp.float32),
             pltpu.VMEM(solved.shape, jnp.float32),
-            pltpu.SemaphoreType.DMA,
+            pltpu.SemaphoreType.DMA((2,)),
         ] + scratch
     return pl.pallas_call(
         functools.partial(project_kernel, len(panels), done, first),
-        grid_spec=pltpu.PrefetchScalarGridSpec(
-            num_scalar_prefetch=2,
-            grid=(1,),
-            in_specs=in_specs,
-            out_specs=[whole(s) for s in shapes],
-            scratch_shapes=scratch,
-        ),
+        in_specs=[SCALARS] * 2 + [ANYWHERE] * len(panels) + ([INSIDE] if first else [INSIDE, ANYWHERE, OUTSIDE]),
+        out_specs=[INSIDE] * len(shapes),
+        scratch_shapes=scratch,
         out_shape=shapes,
         cost_estimate=pl.CostEstimate(flops=3 * 2 * 1024 * depth * 2 * width, bytes_accessed=6 * MIB, transcendentals=0),
         compiler_params=pltpu.CompilerParams(vmem_limit_bytes=24 * MIB),
         name="project",
-    )(blocks, slots, *panels, *inputs)
+    )(blocks, slots, *inputs)
 
 
 def subtract_rows(front_ref, update_ref, first, targets):
@@ -392,7 +400,7 @@
     ]
 
 
-def scatter_kernel(block_ref, slot_ref, front_ref, update_ref, solved_ref, out_ref, held_ref, sem):
+def scatter_kernel(block_ref, slot_ref, front_ref, early_ref, late_ref, solved_ref, out_ref, held_ref, sem):
     rows, depth = front_ref.shape[1], solved_ref.shape[1]
     copies = load_front(front_ref, held_ref, sem)
     for copy in copies:
@@ -406,9 +414,16 @@
     def _():
         held_ref[:, pl.ds(first_row, depth), :] = solved_ref[...]
 
-    @pl.loop(0, 64)
-    def _(g):
-        subtract_rows(held_ref, update_ref, g * 16, slot_targets(slot_ref, g * 16, 16, rows))
+    late = late_ref.shape[0] // 16
+    for first, count, update_ref in ((0, 64 - late, early_ref), (64 - late, late, late_ref)):
+
+        @pl.loop(0, count)
+        def _(piece, first=first, update_ref=update_ref):
+            slot = source(first + piece, False) * 16
+            place = piece if first else source(piece, False)
+            targets = slot_targets(slot_ref, slot, 16, rows)
+            for i in range(0, 16, 4):
+                subtract_rows(held_ref, update_ref, place * 16 + i, targets[i : i + 4])
 
     copies = store_front(held_ref, out_ref, sem)
     for copy in copies:
@@ -417,22 +432,22 @@
         copy.wait()
 
 
-def scatter(blocks, slots, front, update, solved):
+def scatter(blocks, slots, front, early, late, solved):
     _, rows, width = front.shape
     return pl.pallas_call(
         scatter_kernel,
         grid_spec=pltpu.PrefetchScalarGridSpec(
             num_scalar_prefetch=2,
             grid=(1,),
-            in_specs=[ANYWHERE, whole(update), whole(solved)],
-            out_specs=ANYWHERE,
+            in_specs=[OUTSIDE, whole(early), whole(late), whole(solved)],
+            out_specs=OUTSIDE,
             scratch_shapes=[pltpu.VMEM((2, rows + 8, width), jnp.float32), pltpu.SemaphoreType.DMA((2,))],
         ),
         out_shape=jax.ShapeDtypeStruct(front.shape, jnp.float32),
         cost_estimate=pl.CostEstimate(flops=MIB, bytes_accessed=24 * MIB, transcendentals=0),
         compiler_params=pltpu.CompilerParams(vmem_limit_bytes=24 * MIB),
         name="scatter",
-    )(blocks, slots, front, update, solved)
+    )(blocks, slots, front, early, late, solved)
 
 
 def finish_kernel(pieces, block_ref, slot_ref, *refs):
@@ -460,7 +475,8 @@
             targets = slot_targets(slot_ref, base, 16, rows)
             if skip is not None:
                 targets = [jnp.where(skip, rows + i % 8, t) for i, t in enumerate(targets)]
-            subtract_rows(held_ref, update_ref, j * 16, targets)
+            for i in range(0, 16, 4):
+                subtract_rows(held_ref, update_ref, j * 16 + i, targets[i : i + 4])
 
     @pl.loop(0, 4)
     def _(m):
@@ -482,23 +498,19 @@
     depth = mine.shape[0]
     return pl.pallas_call(
         functools.partial(finish_kernel, len(panels)),
-        grid_spec=pltpu.PrefetchScalarGridSpec(
-            num_scalar_prefetch=2,
-            grid=(1,),
-            in_specs=[ANYWHERE] * len(panels) + [whole(a) for a in (inverse, mine, other)] + [ANYWHERE],
-            out_specs=ANYWHERE,
-            scratch_shapes=[
-                pltpu.VMEM((2, rows + 8, width), jnp.float32),
-                pltpu.VMEM((2, depth, width), jnp.float32),
-                pltpu.VMEM((64, 32, depth), jnp.float32),
-                pltpu.VMEM((128, 2 * width), jnp.float32),
-                pltpu.VMEM((128, 2 * width), jnp.float32),
-                pltpu.VMEM((2 * depth, 2 * width), jnp.bfloat16),
-                pltpu.VMEM((2 * depth, 2 * width), jnp.bfloat16),
-                pltpu.SemaphoreType.DMA((2,)),
-                pltpu.SemaphoreType.DMA((len(panels),)),
-            ],
-        ),
+        in_specs=[SCALARS] * 2 + [ANYWHERE] * len(panels) + [INSIDE] * 3 + [OUTSIDE],
+        out_specs=OUTSIDE,
+        scratch_shapes=[
+            pltpu.VMEM((2, rows + 8, width), jnp.float32),
+            pltpu.VMEM((2, depth, width), jnp.float32),
+            pltpu.VMEM((64, 32, depth), jnp.float32),
+            pltpu.VMEM((128, 2 * width), jnp.float32),
+            pltpu.VMEM((128, 2 * width), jnp.float32),
+            pltpu.VMEM((2 * depth, 2 * width), jnp.bfloat16),
+            pltpu.VMEM((2 * depth, 2 * width), jnp.bfloat16),
+            pltpu.SemaphoreType.DMA((2,)),
+            pltpu.SemaphoreType.DMA((len(panels),)),
+        ],
         out_shape=jax.ShapeDtypeStruct(front.shape, jnp.float32),
         cost_estimate=pl.CostEstimate(flops=9 * 2 * 1024 * depth * 2 * width, bytes_accessed=13 * MIB, transcendentals=0),
         compiler_params=pltpu.CompilerParams(vmem_limit_bytes=32 * MIB),
@@ -549,8 +561,8 @@
 
     solved0 = solve(inverse0, mine0, other0)
     (early,) = project(pivot_block, ancestors[0], early_a, 0, solved0)
-    sums, mine1, other1 = project(pivot_block, ancestors[0], late_a, 40, solved0, early, right_side)
-    front = scatter(pivot_block, ancestors[0], right_side, sums, solved0)
+    late, mine1, other1 = project(pivot_block, ancestors[0], late_a, 40, solved0, early, right_side)
+    front = scatter(pivot_block, ancestors[0], right_side, early, late, solved0)
     mine1, other1 = from_owner(mine1, other1)
     return finish(pivot_block, ancestors[1], panels_b, inverse1, mine1, other1, front)
 

time: 149 us -> 147 us (0.987)
  local copies, waits for them, and re-layouts: 4.66 us -> 2.46 us
    unnamed x16 -> x12, local copies, waits for them, and re-layouts: 4.61 us -> 2.42 us
  transfers between devices with their start and end apart: 45 -> 45, of which waited for: 13 -> 13; matrix products, arithmetic and copies ran while one was open for 0% -> 0% of each run, Pallas kernels for 13% -> 14%
where the time goes in v2:
time: 147 us
  starting transfers between devices  65.2 us (44%)
  waiting for transfers between devices  45.8 us (31%)
  Pallas kernels  32.6 us (22%)
  local copies, waits for them, and re-layouts  2.46 us (2%)
    ppermute x19, starting transfers between devices, send_apart(): return lax.ppermute(value, (axis, 'c'), pairs)  34.7 us
    ppermute x26, starting transfers between devices, send(): lax.ppermute(value, axis, [(i, (i + shift) % size) for i in range(size)])  30.5 us
    ppermute x19, waiting for transfers between devices, send_apart(): return lax.ppermute(value, (axis, 'c'), pairs)  24.6 us
    ppermute x26, waiting for transfers between devices, send(): lax.ppermute(value, axis, [(i, (i + shift) % size) for i in range(size)])  21.2 us
    pallas_call x1, Pallas kernels, finish(): pl.pallas_call(functools.partial(finish_kernel, len(panels)), in_specs=[S...  12.7 us
    pallas_call x2, Pallas kernels, project(): pl.pallas_call(functools.partial(project_kernel, len(panels), done, first...  7.68 us
    pallas_call x1, Pallas kernels, scatter(): pl.pallas_call(scatter_kernel, grid_spec=pltpu.PrefetchScalarGridSpec(num...  7.47 us
  transfers between devices with their start and end apart: 45, of which 13 were waited for; matrix products, arithmetic and copies ran while one was open for 0% of the time, Pallas kernels for 14%

profile of v2, /device:TPU:1, one launch (start us, length us, event | category | flops | bytes accessed | tf_op | source)
XLA Modules:
  0.0 147.0 jit_solution(7021156018203471060)
XLA Ops:
  0.0 0.9 copy-done.1
  0.9 0.8 copy-done.2
  1.8 3.3 %collective-permute-start = (f32[1,48,512]{2,1,0:T(8,128)S(1)}, f32[1,48,512]{2,1,0:T(8,128)S(1)}, u32[]{:S(2)}, u32[]{:S(2)}) collective-permute-start(f32[1,48,512]{2,1,0:T(8,128)S(1)} %get-tuple-element.20), channel_id=1, source_target_pairs={{0,1},{1,0},{2,3},{3,2},{4,5},{5,4},{6,7},{7,6},{8,9},{9,8},{10,11... | collective-permute-start | bytes 294920 | tf_op jit(solution)/shard_map/ppermute | solution.py:20
  5.1 0.9 collective-permute-done
  6.0 4.4 %collective-permute-start.3 = (f32[2,48,512]{2,1,0:T(8,128)S(1)}, f32[2,48,512]{2,1,0:T(8,128)S(1)}, u32[]{:S(2)}, u32[]{:S(2)}) collective-permute-start(f32[2,48,512]{2,1,0:T(8,128)S(1)} %constant_dynamic-update-slice_fusion.own_ref), channel_id=1, source_target_pairs={{0,32},{1,97},{16,48},{17,113},{32,64},{33,1},{48,80},{49,17},{64,... | collective-permute-start | bytes 589832 | tf_op jit(solution)/shard_map/ppermute | solution.py:28
  10.4 2.9 %collective-permute-start.23 = (f32[1,32,512]{2,1,0:T(8,128)S(1)}, f32[1,32,512]{2,1,0:T(8,128)S(1)}, u32[]{:S(2)}, u32[]{:S(2)}) collective-permute-start(f32[1,32,512]{2,1,0:T(8,128)S(1)} %get-tuple-element.26), channel_id=1, source_target_pairs={{0,128},{128,0},{1,129},{129,1},{2,130},{130,2},{3,131},{131,3},{4... | collective-permute-start | bytes 196616 | tf_op jit(solution)/shard_map/ppermute | solution.py:20
  13.3 0.8 collective-permute-start.1
  14.1 4.1 %collective-permute-start.5 = (f32[2,48,512]{2,1,0:T(8,128)S(1)}, f32[2,48,512]{2,1,0:T(8,128)S(1)}, u32[]{:S(2)}, u32[]{:S(2)}) collective-permute-start(f32[2,48,512]{2,1,0:T(8,128)S(1)} %collective-permute-done.3.refs_2_), channel_id=1, source_target_pairs={{0,16},{1,113},{16,32},{17,1},{32,48},{33,17},{48,64},{49,33},{64,... | collective-permute-start | bytes 589832 | tf_op jit(solution)/shard_map/ppermute | solution.py:28
  18.2 0.1 collective-permute-start.24
  18.3 0.6 copy-done.3
  19.0 0.6 take.1
  19.6 0.6 collective-permute-start.37
  20.2 1.5 %collective-permute-start.7 = (f32[1,48,512]{2,1,0:T(8,128)S(1)}, f32[1,48,512]{2,1,0:T(8,128)S(1)}, u32[]{:S(2)}, u32[]{:S(2)}) collective-permute-start(f32[1,48,512]{2,1,0:T(8,128)S(1)} %slice.14), channel_id=1, source_target_pairs={{0,32},{1,97},{16,48},{17,113},{32,64},{33,1},{48,80},{49,17},{64,... | collective-permute-start | bytes 294920 | tf_op jit(solution)/shard_map/ppermute | solution.py:28
  21.8 0.5 collective-permute-start.2
  22.3 2.5 %collective-permute-done.7.refs_6_ = f32[1,48,512]{2,1,0:T(8,128)S(1)} collective-permute-done((f32[1,48,512]{2,1,0:T(8,128)S(1)}, f32[1,48,512]{2,1,0:T(8,128)S(1)}, u32[]{:S(2)}, u32[]{:S(2)}) %collective-permute-start.7) | collective-permute-done | bytes 98336 | tf_op jit(solution)/shard_map/ppermute | solution.py:28
  24.8 2.8 %collective-permute-start.8 = (f32[1,48,512]{2,1,0:T(8,128)S(1)}, f32[1,48,512]{2,1,0:T(8,128)S(1)}, u32[]{:S(2)}, u32[]{:S(2)}) collective-permute-start(f32[1,48,512]{2,1,0:T(8,128)S(1)} %collective-permute-done.7.refs_6_), channel_id=1, source_target_pairs={{0,1},{1,0},{2,3},{3,2},{4,5},{5,4},{6,7},{7,6},{8,9},{9,8},{10,11... | collective-permute-start | bytes 294920 | tf_op jit(solution)/shard_map/ppermute | solution.py:20
  27.6 0.9 collective-permute-done.8.refs_7_
  28.5 2.3 %collective-permute-start.25 = (f32[4,32,512]{2,1,0:T(8,128)S(1)}, f32[4,32,512]{2,1,0:T(8,128)S(1)}, u32[]{:S(2)}, u32[]{:S(2)}) collective-permute-start(f32[4,32,512]{2,1,0:T(8,128)S(1)} %constant_dynamic-update-slice_fusion.4.own_ref), channel_id=1, source_target_pairs={{0,4},{1,13},{4,8},{5,1},{8,12},{9,5},{12,0},{13,9},{2,6},{3,15},{... | collective-permute-start | bytes 786440 | tf_op jit(solution)/shard_map/ppermute | solution.py:28
  30.9 0.1 pack.2
  31.0 2.9 %collective-permute-start.15 = (f32[8,16,512]{2,1,0:T(8,128)S(1)}, f32[8,16,512]{2,1,0:T(8,128)S(1)}, u32[]{:S(2)}, u32[]{:S(2)}) collective-permute-start(f32[8,16,512]{2,1,0:T(8,128)S(1)} %bitcast.12), channel_id=1, source_target_pairs={{0,128},{128,0},{1,129},{129,1},{2,130},{130,2},{3,131},{131,3},{4... | collective-permute-start | bytes 786440 | tf_op jit(solution)/shard_map/ppermute | solution.py:20
  33.9 0.7 collective-permute-start.27
  34.6 1.8 %collective-permute-start.26 = (f32[4,32,512]{2,1,0:T(8,128)S(1)}, f32[4,32,512]{2,1,0:T(8,128)S(1)}, u32[]{:S(2)}, u32[]{:S(2)}) collective-permute-start(f32[4,32,512]{2,1,0:T(8,128)S(1)} %collective-permute-done.25.refs_0_), channel_id=1, source_target_pairs={{0,1},{1,0},{2,3},{3,2},{4,5},{5,4},{6,7},{7,6},{8,9},{9,8},{10,11... | collective-permute-start | bytes 786440 | tf_op jit(solution)/shard_map/ppermute | solution.py:20
  36.5 2.4 %collective-permute-start.38 = (f32[512,256]{1,0:T(8,128)S(1)}, f32[512,256]{1,0:T(8,128)S(1)}, u32[]{:S(2)}, u32[]{:S(2)}) collective-permute-start(f32[512,256]{1,0:T(8,128)S(1)} %add.12), channel_id=1, source_target_pairs={{0,2},{2,0},{1,3},{3,1},{4,6},{6,4},{5,7},{7,5},{8,10},{10,8},{9,1... | collective-permute-start | bytes 1572872 | tf_op jit(solution)/shard_map/ppermute | solution.py:20
  38.9 3.3 %collective-permute-start.9 = (f32[8,32,512]{2,1,0:T(8,128)S(1)}, f32[8,32,512]{2,1,0:T(8,128)S(1)}, u32[]{:S(2)}, u32[]{:S(2)}) collective-permute-start(f32[8,32,512]{2,1,0:T(8,128)S(1)} %bitcast.9), channel_id=1, source_target_pairs={{0,128},{128,0},{1,129},{129,1},{2,130},{130,2},{3,131},{131,3},{4... | collective-permute-start | bytes 1572872 | tf_op jit(solution)/shard_map/ppermute | solution.py:20
  42.2 1.1 collective-permute-start.28
  43.3 0.3 collective-permute-start.16
  43.6 0.7 collective-permute-done.28.refs_3_
  44.3 0.9 collective-permute-start.32
  45.3 0.8 collective-permute-start.29
  46.1 3.5 %collective-permute-start.17 = (f32[16,16,512]{2,1,0:T(8,128)S(1)}, f32[16,16,512]{2,1,0:T(8,128)S(1)}, u32[]{:S(2)}, u32[]{:S(2)}) collective-permute-start(f32[16,16,512]{2,1,0:T(8,128)S(1)} %pad_maximum_fusion.2.refs_0_), channel_id=1, source_target_pairs={{0,4},{1,13},{4,8},{5,1},{8,12},{9,5},{12,0},{13,9},{2,6},{3,15},{... | collective-permute-start | bytes 1572872 | tf_op jit(solution)/shard_map/ppermute | solution.py:28
  49.7 3.9 %collective-permute-done.38 = f32[512,256]{1,0:T(8,128)S(1)} collective-permute-done((f32[512,256]{1,0:T(8,128)S(1)}, f32[512,256]{1,0:T(8,128)S(1)}, u32[]{:S(2)}, u32[]{:S(2)}) %collective-permute-start.38) | collective-permute-done | bytes 524320 | tf_op jit(solution)/shard_map/ppermute | solution.py:20
  53.6 11.3 %collective-permute-done.9 = f32[8,32,512]{2,1,0:T(8,128)S(1)} collective-permute-done((f32[8,32,512]{2,1,0:T(8,128)S(1)}, f32[8,32,512]{2,1,0:T(8,128)S(1)}, u32[]{:S(2)}, u32[]{:S(2)}) %collective-permute-start.9) | collective-permute-done | bytes 524320 | tf_op jit(solution)/shard_map/ppermute | solution.py:20
  64.9 1.4 collective-permute-start.11
  66.3 0.8 collective-permute-start.33
  67.2 0.8 collective-permute-start.30
  68.0 3.4 %collective-permute-start.21 = (f32[16,16,512]{2,1,0:T(8,128)S(1)}, f32[16,16,512]{2,1,0:T(8,128)S(1)}, u32[]{:S(2)}, u32[]{:S(2)}) collective-permute-start(f32[16,16,512]{2,1,0:T(8,128)S(1)} %collective-permute-done.17.refs_2_), channel_id=1, source_target_pairs={{0,4},{1,13},{4,8},{5,1},{8,12},{9,5},{12,0},{13,9},{2,6},{3,15},{... | collective-permute-start | bytes 1572872 | tf_op jit(solution)/shard_map/ppermute | solution.py:28
  71.4 0.5 collective-permute-start.19
  71.9 2.7 %collective-permute-done.33 = f32[8,32,512]{2,1,0:T(8,128)S(1)} collective-permute-done((f32[8,32,512]{2,1,0:T(8,128)S(1)}, f32[8,32,512]{2,1,0:T(8,128)S(1)}, u32[]{:S(2)}, u32[]{:S(2)}) %collective-permute-start.33) | collective-permute-done | bytes 524320 | tf_op jit(solution)/shard_map/ppermute | solution.py:28
  74.6 2.0 %collective-permute-start.34 = (f32[8,32,512]{2,1,0:T(8,128)S(1)}, f32[8,32,512]{2,1,0:T(8,128)S(1)}, u32[]{:S(2)}, u32[]{:S(2)}) collective-permute-start(f32[8,32,512]{2,1,0:T(8,128)S(1)} %collective-permute-done.33), channel_id=1, source_target_pairs={{0,16},{1,113},{16,32},{17,1},{32,48},{33,17},{48,64},{49,33},{64,... | collective-permute-start | bytes 1572872 | tf_op jit(solution)/shard_map/ppermute | solution.py:28
  76.7 3.6 %collective-permute-done.30.refs_3_ = f32[8,32,512]{2,1,0:T(8,128)S(1)} collective-permute-done((f32[8,32,512]{2,1,0:T(8,128)S(1)}, f32[8,32,512]{2,1,0:T(8,128)S(1)}, u32[]{:S(2)}, u32[]{:S(2)}) %collective-permute-start.30) | collective-permute-done | bytes 524320 | tf_op jit(solution)/shard_map/ppermute | solution.py:28
  80.3 1.7 %collective-permute-start.31 = (f32[8,32,512]{2,1,0:T(8,128)S(1)}, f32[8,32,512]{2,1,0:T(8,128)S(1)}, u32[]{:S(2)}, u32[]{:S(2)}) collective-permute-start(f32[8,32,512]{2,1,0:T(8,128)S(1)} %collective-permute-done.30.refs_3_), channel_id=1, source_target_pairs={{0,16},{1,113},{16,32},{17,1},{32,48},{33,17},{48,64},{49,33},{64,... | collective-permute-start | bytes 1572872 | tf_op jit(solution)/shard_map/ppermute | solution.py:28
  82.0 0.3 collective-permute-start.22
  82.4 0.3 collective-permute-start.39
  82.7 0.3 collective-permute-start.40
  83.0 2.8 %collective-permute-done.34 = f32[8,32,512]{2,1,0:T(8,128)S(1)} collective-permute-done((f32[8,32,512]{2,1,0:T(8,128)S(1)}, f32[8,32,512]{2,1,0:T(8,128)S(1)}, u32[]{:S(2)}, u32[]{:S(2)}) %collective-permute-start.34) | collective-permute-done | bytes 524320 | tf_op jit(solution)/shard_map/ppermute | solution.py:28
  85.9 2.1 %collective-permute-start.41 = (f32[8,32,512]{2,1,0:T(8,128)S(1)}, f32[8,32,512]{2,1,0:T(8,128)S(1)}, u32[]{:S(2)}, u32[]{:S(2)}) collective-permute-start(f32[8,32,512]{2,1,0:T(8,128)S(1)} %collective-permute-done.33), channel_id=1, source_target_pairs={{0,1},{1,0},{2,3},{3,2},{4,5},{5,4},{6,7},{7,6},{8,9},{9,8},{10,11... | collective-permute-start | bytes 1572872 | tf_op jit(solution)/shard_map/ppermute | solution.py:20
  88.0 3.5 %collective-permute-done.31.refs_0_ = f32[8,32,512]{2,1,0:T(8,128)S(1)} collective-permute-done((f32[8,32,512]{2,1,0:T(8,128)S(1)}, f32[8,32,512]{2,1,0:T(8,128)S(1)}, u32[]{:S(2)}, u32[]{:S(2)}) %collective-permute-start.31) | collective-permute-done | bytes 524320 | tf_op jit(solution)/shard_map/ppermute | solution.py:28
  91.5 2.1 %collective-permute-start.35 = (f32[8,32,512]{2,1,0:T(8,128)S(1)}, f32[8,32,512]{2,1,0:T(8,128)S(1)}, u32[]{:S(2)}, u32[]{:S(2)}) collective-permute-start(f32[8,32,512]{2,1,0:T(8,128)S(1)} %collective-permute-done.34), channel_id=1, source_target_pairs={{0,1},{1,0},{2,3},{3,2},{4,5},{5,4},{6,7},{7,6},{8,9},{9,8},{10,11... | collective-permute-start | bytes 1572872 | tf_op jit(solution)/shard_map/ppermute | solution.py:20
  93.7 1.6 %order.1 = (f32[2,512,512]{2,1,0:T(8,128)S(1)}, f32[2,512,512]{2,1,0:T(8,128)S(1)}) custom-call(f32[16,16,512]{2,1,0:T(8,128)S(1)} %pad_maximum_fusion.2.refs_0_, f32[16,16,512]{2,1,0:T(8,128)S(1)} %pad_maximum_fusion.3.refs_1_, f32[16,16,512]{2,1,0:T(8,128)S(1)} %collective-permute-done.17.refs_2_, f32[16,16,512]{2,1,0:T(8,128)S(1)} %collective-permute-done.18.refs_3_, ...), custom_call_target="tpu_custom_call" | custom-call | bytes 8388608 | tf_op jit(solution)/shard_map/order/pallas_call | solution.py:179
  95.3 3.5 %collective-permute-start.10 = (f32[16,32,512]{2,1,0:T(8,128)S(1)}, f32[16,32,512]{2,1,0:T(8,128)S(1)}, u32[]{:S(2)}, u32[]{:S(2)}) collective-permute-start(f32[16,32,512]{2,1,0:T(8,128)S(1)} %pad_maximum_fusion.refs_0_), channel_id=1, source_target_pairs={{0,4},{1,13},{4,8},{5,1},{8,12},{9,5},{12,0},{13,9},{2,6},{3,15},{... | collective-permute-start | bytes 3145736 | tf_op jit(solution)/shard_map/ppermute | solution.py:28
  98.8 0.1 collective-permute-start.12
  98.9 2.3 %solve.1.refs_5_.refs_3_.solved_ref = f32[2,512,256]{2,1,0:T(8,128)S(1)} custom-call(f32[2,512,512]{2,1,0:T(8,128)S(1)} %get-tuple-element.29.inverse_ref, f32[512,256]{1,0:T(8,128)S(1)} %add.13.mine_ref, f32[512,256]{1,0:T(8,128)S(1)} %collective-permute-done.39.other_ref), custom_call_target="tpu_custom_call" | custom-call | flops 3221225472 | bytes 6291456 | tf_op jit(solution)/shard_map/solve/pallas_call | solution.py:232
  101.2 4.0 %project.2.refs_4_.early_ref = f32[1024,512]{1,0:T(8,128)S(1)} custom-call(s32[2]{0:T(128)S(1)} %copy-done.3, s32[1024]{0:T(1024)S(1)} %bitcast.14, f32[8,32,512]{2,1,0:T(8,128)S(1)} %bitcast.19, f32[8,32,512]{2,1,0:T(8,128)S(1)} %collective-permute-done.29.refs_1_, f32[8,32,512]{2,1,0:T(8,128)S(1)} %collective-permute-done.40.refs_2_, ...), custom_call_target="tpu_custom_call" | custom-call | flops 1610612736 | bytes 6291456 | tf_op jit(solution)/shard_map/project/pallas_call | solution.py:358
  105.2 3.7 %project.3 = (f32[384,512]{1,0:T(8,128)S(1)}, f32[512,256]{1,0:T(8,128)S(1)}, f32[512,256]{1,0:T(8,128)S(1)}) custom-call(s32[2]{0:T(128)S(1)} %copy-done.3, s32[1024]{0:T(1024)S(1)} %bitcast.15, f32[8,32,512]{2,1,0:T(8,128)S(1)} %collective-permute-done.31.refs_0_, f32[8,32,512]{2,1,0:T(8,128)S(1)} %collective-permute-done.35.refs_1_, ...), custom_call_target="tpu_custom_call" | custom-call | flops 1610612736 | bytes 6291456 | tf_op jit(solution)/shard_map/project/pallas_call | solution.py:358
  108.9 0.1 collective-permute-start.42
  109.0 1.5 %collective-permute-done.10.refs_1_ = f32[16,32,512]{2,1,0:T(8,128)S(1)} collective-permute-done((f32[16,32,512]{2,1,0:T(8,128)S(1)}, f32[16,32,512]{2,1,0:T(8,128)S(1)}, u32[]{:S(2)}, u32[]{:S(2)}) %collective-permute-start.10) | collective-permute-done | bytes 1048608 | tf_op jit(solution)/shard_map/ppermute | solution.py:28
  110.5 3.1 %collective-permute-start.14 = (f32[16,32,512]{2,1,0:T(8,128)S(1)}, f32[16,32,512]{2,1,0:T(8,128)S(1)}, u32[]{:S(2)}, u32[]{:S(2)}) collective-permute-start(f32[16,32,512]{2,1,0:T(8,128)S(1)} %collective-permute-done.10.refs_1_), channel_id=1, source_target_pairs={{0,4},{1,13},{4,8},{5,1},{8,12},{9,5},{12,0},{13,9},{2,6},{3,15},{... | collective-permute-start | bytes 3145736 | tf_op jit(solution)/shard_map/ppermute | solution.py:28
  113.7 0.1 collective-permute-start.43
  113.8 7.9 %collective-permute-done.12 = f32[16,32,512]{2,1,0:T(8,128)S(1)} collective-permute-done((f32[16,32,512]{2,1,0:T(8,128)S(1)}, f32[16,32,512]{2,1,0:T(8,128)S(1)}, u32[]{:S(2)}, u32[]{:S(2)}) %collective-permute-start.12) | collective-permute-done | bytes 1048608 | tf_op jit(solution)/shard_map/ppermute | solution.py:28
  121.8 1.3 collective-permute-start.13
  123.1 3.3 %collective-permute-done.43 = f32[512,256]{1,0:T(8,128)S(1)} collective-permute-done((f32[512,256]{1,0:T(8,128)S(1)}, f32[512,256]{1,0:T(8,128)S(1)}, u32[]{:S(2)}, u32[]{:S(2)}) %collective-permute-start.43) | collective-permute-done | bytes 524320 | tf_op jit(solution)/shard_map/ppermute | solution.py:20
  126.5 0.1 collective-permute-start.44
  126.6 7.5 %scatter.1.refs_7_ = f32[2,2048,256]{2,1,0:T(8,128)S(1)} custom-call(s32[2]{0:T(128)S(1)} %copy-done.3, s32[1024]{0:T(1024)S(1)} %bitcast.16, f32[2,2048,256]{2,1,0:T(8,128)S(1)} %copy-done, f32[1024,512]{1,0:T(8,128)S(1)} %project.2.refs_4_.early_ref, f32[384,512]{1,0:T(8,128)S(1)} %get-tuple-element.34.late_ref, ...), custom_call_target="tpu_custom_call" | custom-call | flops 1048576 | bytes 25165824 | tf_op jit(solution)/shard_map/scatter/pallas_call | solution.py:437
  134.1 12.7 %finish.1 = f32[2,2048,256]{2,1,0:T(8,128)} custom-call(s32[2]{0:T(128)S(1)} %copy-done.3, s32[1024]{0:T(1024)S(1)} %bitcast.17, f32[16,32,512]{2,1,0:T(8,128)S(1)} %pad_maximum_fusion.refs_0_, f32[16,32,512]{2,1,0:T(8,128)S(1)} %collective-permute-done.10.refs_1_, f32[16,32,512]{2,1,0:T(8,128)S(1)} %collective-permute-done.13.refs_2_, ...), custom_call_target="tpu_custom_call" | custom-call | flops 4831838208 | bytes 13631488 | tf_op jit(solution)/shard_map/finish/pallas_call | solution.py:499
  (61 shorter events, 0.8 us)
Async XLA Ops:
  0.0 0.9 copy-start.1
  0.9 0.8 copy-start.2
  1.8 4.2 %collective-permute-start = (f32[1,48,512]{2,1,0:T(8,128)S(1)}, f32[1,48,512]{2,1,0:T(8,128)S(1)}, u32[]{:S(2)}, u32[]{:S(2)}) collective-permute-start(f32[1,48,512]{2,1,0:T(8,128)S(1)} %get-tuple-element.20), channel_id=1, source_target_pairs={{0,1},{1,0},{2,3},{3,2},{4,5},{5,4},{6,7},{7,6},{8,9},{9,8},{10,11... | collective-permute-start | bytes 294920 | tf_op jit(solution)/shard_map/ppermute | solution.py:20
  6.0 8.1 %collective-permute-start.3 = (f32[2,48,512]{2,1,0:T(8,128)S(1)}, f32[2,48,512]{2,1,0:T(8,128)S(1)}, u32[]{:S(2)}, u32[]{:S(2)}) collective-permute-start(f32[2,48,512]{2,1,0:T(8,128)S(1)} %constant_dynamic-update-slice_fusion.own_ref), channel_id=1, source_target_pairs={{0,32},{1,97},{16,48},{17,113},{32,64},{33,1},{48,80},{49,17},{64,... | collective-permute-start | bytes 589832 | tf_op jit(solution)/shard_map/ppermute | solution.py:28
  10.4 7.8 %collective-permute-start.23 = (f32[1,32,512]{2,1,0:T(8,128)S(1)}, f32[1,32,512]{2,1,0:T(8,128)S(1)}, u32[]{:S(2)}, u32[]{:S(2)}) collective-permute-start(f32[1,32,512]{2,1,0:T(8,128)S(1)} %get-tuple-element.26), channel_id=1, source_target_pairs={{0,128},{128,0},{1,129},{129,1},{2,130},{130,2},{3,131},{131,3},{4... | collective-permute-start | bytes 196616 | tf_op jit(solution)/shard_map/ppermute | solution.py:20
  13.3 8.4 %collective-permute-start.1 = (f32[2,48,512]{2,1,0:T(8,128)S(1)}, f32[2,48,512]{2,1,0:T(8,128)S(1)}, u32[]{:S(2)}, u32[]{:S(2)}) collective-permute-start(f32[2,48,512]{2,1,0:T(8,128)S(1)} %constant_dynamic-update-slice_fusion.own_ref), channel_id=1, source_target_pairs={{0,16},{1,113},{16,32},{17,1},{32,48},{33,17},{48,64},{49,33},{64,... | collective-permute-start | bytes 589832 | tf_op jit(solution)/shard_map/ppermute | solution.py:28
  14.1 13.4 %collective-permute-start.5 = (f32[2,48,512]{2,1,0:T(8,128)S(1)}, f32[2,48,512]{2,1,0:T(8,128)S(1)}, u32[]{:S(2)}, u32[]{:S(2)}) collective-permute-start(f32[2,48,512]{2,1,0:T(8,128)S(1)} %collective-permute-done.3.refs_2_), channel_id=1, source_target_pairs={{0,16},{1,113},{16,32},{17,1},{32,48},{33,17},{48,64},{49,33},{64,... | collective-permute-start | bytes 589832 | tf_op jit(solution)/shard_map/ppermute | solution.py:28
  18.2 3.5 %collective-permute-start.24 = (f32[2,32,512]{2,1,0:T(8,128)S(1)}, f32[2,32,512]{2,1,0:T(8,128)S(1)}, u32[]{:S(2)}, u32[]{:S(2)}) collective-permute-start(f32[2,32,512]{2,1,0:T(8,128)S(1)} %get-tuple-element.35), channel_id=1, source_target_pairs={{0,1},{1,0},{2,3},{3,2},{4,5},{5,4},{6,7},{7,6},{8,9},{9,8},{10,11... | collective-permute-start | bytes 393224 | tf_op jit(solution)/shard_map/ppermute | solution.py:20
  18.3 0.7 copy-start.3
  19.6 63.4 %copy-start.4 = (s32[2,1024]{1,0:T(2,128)S(1)}, s32[2,1024]{1,0:T(2,128)}, u32[]{:S(2)}) copy-start(s32[2,1024]{1,0:T(2,128)} %param.8) | copy-start | bytes 24580
  19.6 16.8 %collective-permute-start.37 = (f32[512,256]{1,0:T(8,128)S(1)}, f32[512,256]{1,0:T(8,128)S(1)}, u32[]{:S(2)}, u32[]{:S(2)}) collective-permute-start(f32[512,256]{1,0:T(8,128)S(1)} %get-tuple-element.31), channel_id=1, source_target_pairs={{0,1},{1,0},{2,3},{3,2},{4,5},{5,4},{6,7},{7,6},{8,9},{9,8},{10,11... | collective-permute-start | bytes 1572872 | tf_op jit(solution)/shard_map/ppermute | solution.py:20
  20.2 4.5 %collective-permute-start.7 = (f32[1,48,512]{2,1,0:T(8,128)S(1)}, f32[1,48,512]{2,1,0:T(8,128)S(1)}, u32[]{:S(2)}, u32[]{:S(2)}) collective-permute-start(f32[1,48,512]{2,1,0:T(8,128)S(1)} %slice.14), channel_id=1, source_target_pairs={{0,32},{1,97},{16,48},{17,113},{32,64},{33,1},{48,80},{49,17},{64,... | collective-permute-start | bytes 294920 | tf_op jit(solution)/shard_map/ppermute | solution.py:28
  21.8 9.1 %collective-permute-start.4 = (f32[2,48,512]{2,1,0:T(8,128)S(1)}, f32[2,48,512]{2,1,0:T(8,128)S(1)}, u32[]{:S(2)}, u32[]{:S(2)}) collective-permute-start(f32[2,48,512]{2,1,0:T(8,128)S(1)} %collective-permute-done.3.refs_2_), channel_id=1, source_target_pairs={{0,1},{1,0},{2,3},{3,2},{4,5},{5,4},{6,7},{7,6},{8,9},{9,8},{10,11... | collective-permute-start | bytes 589832 | tf_op jit(solution)/shard_map/ppermute | solution.py:20
  21.8 9.1 %collective-permute-start.2 = (f32[2,48,512]{2,1,0:T(8,128)S(1)}, f32[2,48,512]{2,1,0:T(8,128)S(1)}, u32[]{:S(2)}, u32[]{:S(2)}) collective-permute-start(f32[2,48,512]{2,1,0:T(8,128)S(1)} %collective-permute-done.1.refs_0_), channel_id=1, source_target_pairs={{0,1},{1,0},{2,3},{3,2},{4,5},{5,4},{6,7},{7,6},{8,9},{9,8},{10,11... | collective-permute-start | bytes 589832 | tf_op jit(solution)/shard_map/ppermute | solution.py:20
  24.8 3.8 %collective-permute-start.8 = (f32[1,48,512]{2,1,0:T(8,128)S(1)}, f32[1,48,512]{2,1,0:T(8,128)S(1)}, u32[]{:S(2)}, u32[]{:S(2)}) collective-permute-start(f32[1,48,512]{2,1,0:T(8,128)S(1)} %collective-permute-done.7.refs_6_), channel_id=1, source_target_pairs={{0,1},{1,0},{2,3},{3,2},{4,5},{5,4},{6,7},{7,6},{8,9},{9,8},{10,11... | collective-permute-start | bytes 294920 | tf_op jit(solution)/shard_map/ppermute | solution.py:20
  27.6 3.3 %collective-permute-start.6 = (f32[2,48,512]{2,1,0:T(8,128)S(1)}, f32[2,48,512]{2,1,0:T(8,128)S(1)}, u32[]{:S(2)}, u32[]{:S(2)}) collective-permute-start(f32[2,48,512]{2,1,0:T(8,128)S(1)} %collective-permute-done.5.refs_4_), channel_id=1, source_target_pairs={{0,1},{1,0},{2,3},{3,2},{4,5},{5,4},{6,7},{7,6},{8,9},{9,8},{10,11... | collective-permute-start | bytes 589832 | tf_op jit(solution)/shard_map/ppermute | solution.py:20
  28.5 6.1 %collective-permute-start.25 = (f32[4,32,512]{2,1,0:T(8,128)S(1)}, f32[4,32,512]{2,1,0:T(8,128)S(1)}, u32[]{:S(2)}, u32[]{:S(2)}) collective-permute-start(f32[4,32,512]{2,1,0:T(8,128)S(1)} %constant_dynamic-update-slice_fusion.4.own_ref), channel_id=1, source_target_pairs={{0,4},{1,13},{4,8},{5,1},{8,12},{9,5},{12,0},{13,9},{2,6},{3,15},{... | collective-permute-start | bytes 786440 | tf_op jit(solution)/shard_map/ppermute | solution.py:28
  31.0 12.3 %collective-permute-start.15 = (f32[8,16,512]{2,1,0:T(8,128)S(1)}, f32[8,16,512]{2,1,0:T(8,128)S(1)}, u32[]{:S(2)}, u32[]{:S(2)}) collective-permute-start(f32[8,16,512]{2,1,0:T(8,128)S(1)} %bitcast.12), channel_id=1, source_target_pairs={{0,128},{128,0},{1,129},{129,1},{2,130},{130,2},{3,131},{131,3},{4... | collective-permute-start | bytes 786440 | tf_op jit(solution)/shard_map/ppermute | solution.py:20
  33.9 8.3 %collective-permute-start.27 = (f32[2,32,512]{2,1,0:T(8,128)S(1)}, f32[2,32,512]{2,1,0:T(8,128)S(1)}, u32[]{:S(2)}, u32[]{:S(2)}) collective-permute-start(f32[2,32,512]{2,1,0:T(8,128)S(1)} %get-tuple-element.35), channel_id=1, source_target_pairs={{0,8},{1,9},{4,12},{5,13},{8,0},{9,1},{12,4},{13,5},{2,10},{3,11},... | collective-permute-start | bytes 393224 | tf_op jit(solution)/shard_map/ppermute | solution.py:28
  34.6 9.6 %collective-permute-start.26 = (f32[4,32,512]{2,1,0:T(8,128)S(1)}, f32[4,32,512]{2,1,0:T(8,128)S(1)}, u32[]{:S(2)}, u32[]{:S(2)}) collective-permute-start(f32[4,32,512]{2,1,0:T(8,128)S(1)} %collective-permute-done.25.refs_0_), channel_id=1, source_target_pairs={{0,1},{1,0},{2,3},{3,2},{4,5},{5,4},{6,7},{7,6},{8,9},{9,8},{10,11... | collective-permute-start | bytes 786440 | tf_op jit(solution)/shard_map/ppermute | solution.py:20
  36.5 17.1 %collective-permute-start.38 = (f32[512,256]{1,0:T(8,128)S(1)}, f32[512,256]{1,0:T(8,128)S(1)}, u32[]{:S(2)}, u32[]{:S(2)}) collective-permute-start(f32[512,256]{1,0:T(8,128)S(1)} %add.12), channel_id=1, source_target_pairs={{0,2},{2,0},{1,3},{3,1},{4,6},{6,4},{5,7},{7,5},{8,10},{10,8},{9,1... | collective-permute-start | bytes 1572872 | tf_op jit(solution)/shard_map/ppermute | solution.py:20
  38.9 26.0 %collective-permute-start.9 = (f32[8,32,512]{2,1,0:T(8,128)S(1)}, f32[8,32,512]{2,1,0:T(8,128)S(1)}, u32[]{:S(2)}, u32[]{:S(2)}) collective-permute-start(f32[8,32,512]{2,1,0:T(8,128)S(1)} %bitcast.9), channel_id=1, source_target_pairs={{0,128},{128,0},{1,129},{129,1},{2,130},{130,2},{3,131},{131,3},{4... | collective-permute-start | bytes 1572872 | tf_op jit(solution)/shard_map/ppermute | solution.py:20
  42.2 2.1 %collective-permute-start.28 = (f32[2,32,512]{2,1,0:T(8,128)S(1)}, f32[2,32,512]{2,1,0:T(8,128)S(1)}, u32[]{:S(2)}, u32[]{:S(2)}) collective-permute-start(f32[2,32,512]{2,1,0:T(8,128)S(1)} %collective-permute-done.27.refs_2_), channel_id=1, source_target_pairs={{0,1},{1,0},{2,3},{3,2},{4,5},{5,4},{6,7},{7,6},{8,9},{9,8},{10,11... | collective-permute-start | bytes 393224 | tf_op jit(solution)/shard_map/ppermute | solution.py:20
  43.3 2.9 %collective-permute-start.16 = (f32[8,16,512]{2,1,0:T(8,128)S(1)}, f32[8,16,512]{2,1,0:T(8,128)S(1)}, u32[]{:S(2)}, u32[]{:S(2)}) collective-permute-start(f32[8,16,512]{2,1,0:T(8,128)S(1)} %collective-permute-done.15), channel_id=1, source_target_pairs={{0,1},{1,0},{2,3},{3,2},{4,5},{5,4},{6,7},{7,6},{8,9},{9,8},{10,11... | collective-permute-start | bytes 786440 | tf_op jit(solution)/shard_map/ppermute | solution.py:20
  44.3 22.0 %collective-permute-start.32 = (f32[8,32,512]{2,1,0:T(8,128)S(1)}, f32[8,32,512]{2,1,0:T(8,128)S(1)}, u32[]{:S(2)}, u32[]{:S(2)}) collective-permute-start(f32[8,32,512]{2,1,0:T(8,128)S(1)} %bitcast.20), channel_id=1, source_target_pairs={{0,16},{1,113},{16,32},{17,1},{32,48},{33,17},{48,64},{49,33},{64,... | collective-permute-start | bytes 1572872 | tf_op jit(solution)/shard_map/ppermute | solution.py:28
  45.3 21.9 %collective-permute-start.29 = (f32[8,32,512]{2,1,0:T(8,128)S(1)}, f32[8,32,512]{2,1,0:T(8,128)S(1)}, u32[]{:S(2)}, u32[]{:S(2)}) collective-permute-start(f32[8,32,512]{2,1,0:T(8,128)S(1)} %bitcast.18), channel_id=1, source_target_pairs={{0,16},{1,113},{16,32},{17,1},{32,48},{33,17},{48,64},{49,33},{64,... | collective-permute-start | bytes 1572872 | tf_op jit(solution)/shard_map/ppermute | solution.py:28
  46.1 21.8 %collective-permute-start.17 = (f32[16,16,512]{2,1,0:T(8,128)S(1)}, f32[16,16,512]{2,1,0:T(8,128)S(1)}, u32[]{:S(2)}, u32[]{:S(2)}) collective-permute-start(f32[16,16,512]{2,1,0:T(8,128)S(1)} %pad_maximum_fusion.2.refs_0_), channel_id=1, source_target_pairs={{0,4},{1,13},{4,8},{5,1},{8,12},{9,5},{12,0},{13,9},{2,6},{3,15},{... | collective-permute-start | bytes 1572872 | tf_op jit(solution)/shard_map/ppermute | solution.py:28
  53.6 17.8 %collective-permute-start.18 = (f32[16,16,512]{2,1,0:T(8,128)S(1)}, f32[16,16,512]{2,1,0:T(8,128)S(1)}, u32[]{:S(2)}, u32[]{:S(2)}) collective-permute-start(f32[16,16,512]{2,1,0:T(8,128)S(1)} %pad_maximum_fusion.3.refs_1_), channel_id=1, source_target_pairs={{0,4},{1,13},{4,8},{5,1},{8,12},{9,5},{12,0},{13,9},{2,6},{3,15},{... | collective-permute-start | bytes 1572872 | tf_op jit(solution)/shard_map/ppermute | solution.py:28
  64.9 6.5 %collective-permute-start.11 = (f32[8,32,512]{2,1,0:T(8,128)S(1)}, f32[8,32,512]{2,1,0:T(8,128)S(1)}, u32[]{:S(2)}, u32[]{:S(2)}) collective-permute-start(f32[8,32,512]{2,1,0:T(8,128)S(1)} %collective-permute-done.9), channel_id=1, source_target_pairs={{0,1},{1,0},{2,3},{3,2},{4,5},{5,4},{6,7},{7,6},{8,9},{9,8},{10,11... | collective-permute-start | bytes 1572872 | tf_op jit(solution)/shard_map/ppermute | solution.py:20
  66.3 8.3 %collective-permute-start.33 = (f32[8,32,512]{2,1,0:T(8,128)S(1)}, f32[8,32,512]{2,1,0:T(8,128)S(1)}, u32[]{:S(2)}, u32[]{:S(2)}) collective-permute-start(f32[8,32,512]{2,1,0:T(8,128)S(1)} %collective-permute-done.32), channel_id=1, source_target_pairs={{0,16},{1,113},{16,32},{17,1},{32,48},{33,17},{48,64},{49,33},{64,... | collective-permute-start | bytes 1572872 | tf_op jit(solution)/shard_map/ppermute | solution.py:28
  67.2 13.1 %collective-permute-start.30 = (f32[8,32,512]{2,1,0:T(8,128)S(1)}, f32[8,32,512]{2,1,0:T(8,128)S(1)}, u32[]{:S(2)}, u32[]{:S(2)}) collective-permute-start(f32[8,32,512]{2,1,0:T(8,128)S(1)} %collective-permute-done.29.refs_1_), channel_id=1, source_target_pairs={{0,16},{1,113},{16,32},{17,1},{32,48},{33,17},{48,64},{49,33},{64,... | collective-permute-start | bytes 1572872 | tf_op jit(solution)/shard_map/ppermute | solution.py:28
  68.0 14.0 %collective-permute-start.21 = (f32[16,16,512]{2,1,0:T(8,128)S(1)}, f32[16,16,512]{2,1,0:T(8,128)S(1)}, u32[]{:S(2)}, u32[]{:S(2)}) collective-permute-start(f32[16,16,512]{2,1,0:T(8,128)S(1)} %collective-permute-done.17.refs_2_), channel_id=1, source_target_pairs={{0,4},{1,13},{4,8},{5,1},{8,12},{9,5},{12,0},{13,9},{2,6},{3,15},{... | collective-permute-start | bytes 1572872 | tf_op jit(solution)/shard_map/ppermute | solution.py:28
  71.4 11.0 %collective-permute-start.20 = (f32[16,16,512]{2,1,0:T(8,128)S(1)}, f32[16,16,512]{2,1,0:T(8,128)S(1)}, u32[]{:S(2)}, u32[]{:S(2)}) collective-permute-start(f32[16,16,512]{2,1,0:T(8,128)S(1)} %collective-permute-done.17.refs_2_), channel_id=1, source_target_pairs={{0,1},{1,0},{2,3},{3,2},{4,5},{5,4},{6,7},{7,6},{8,9},{9,8},{10,11... | collective-permute-start | bytes 1572872 | tf_op jit(solution)/shard_map/ppermute | solution.py:20
  71.4 11.3 %collective-permute-start.19 = (f32[16,16,512]{2,1,0:T(8,128)S(1)}, f32[16,16,512]{2,1,0:T(8,128)S(1)}, u32[]{:S(2)}, u32[]{:S(2)}) collective-permute-start(f32[16,16,512]{2,1,0:T(8,128)S(1)} %collective-permute-done.18.refs_3_), channel_id=1, source_target_pairs={{0,1},{1,0},{2,3},{3,2},{4,5},{5,4},{6,7},{7,6},{8,9},{9,8},{10,11... | collective-permute-start | bytes 1572872 | tf_op jit(solution)/shard_map/ppermute | solution.py:20
  74.6 11.2 %collective-permute-start.34 = (f32[8,32,512]{2,1,0:T(8,128)S(1)}, f32[8,32,512]{2,1,0:T(8,128)S(1)}, u32[]{:S(2)}, u32[]{:S(2)}) collective-permute-start(f32[8,32,512]{2,1,0:T(8,128)S(1)} %collective-permute-done.33), channel_id=1, source_target_pairs={{0,16},{1,113},{16,32},{17,1},{32,48},{33,17},{48,64},{49,33},{64,... | collective-permute-start | bytes 1572872 | tf_op jit(solution)/shard_map/ppermute | solution.py:28
  80.3 11.2 %collective-permute-start.31 = (f32[8,32,512]{2,1,0:T(8,128)S(1)}, f32[8,32,512]{2,1,0:T(8,128)S(1)}, u32[]{:S(2)}, u32[]{:S(2)}) collective-permute-start(f32[8,32,512]{2,1,0:T(8,128)S(1)} %collective-permute-done.30.refs_3_), channel_id=1, source_target_pairs={{0,16},{1,113},{16,32},{17,1},{32,48},{33,17},{48,64},{49,33},{64,... | collective-permute-start | bytes 1572872 | tf_op jit(solution)/shard_map/ppermute | solution.py:28
  82.0 11.6 %collective-permute-start.22 = (f32[16,16,512]{2,1,0:T(8,128)S(1)}, f32[16,16,512]{2,1,0:T(8,128)S(1)}, u32[]{:S(2)}, u32[]{:S(2)}) collective-permute-start(f32[16,16,512]{2,1,0:T(8,128)S(1)} %collective-permute-done.21.refs_6_), channel_id=1, source_target_pairs={{0,1},{1,0},{2,3},{3,2},{4,5},{5,4},{6,7},{7,6},{8,9},{9,8},{10,11... | collective-permute-start | bytes 1572872 | tf_op jit(solution)/shard_map/ppermute | solution.py:20
  82.4 12.9 %collective-permute-start.39 = (f32[512,256]{1,0:T(8,128)S(1)}, f32[512,256]{1,0:T(8,128)S(1)}, u32[]{:S(2)}, u32[]{:S(2)}) collective-permute-start(f32[512,256]{1,0:T(8,128)S(1)} %add.13.mine_ref), channel_id=1, source_target_pairs={{0,1},{1,0},{2,3},{3,2},{4,5},{5,4},{6,7},{7,6},{8,9},{9,8},{10,11... | collective-permute-start | bytes 1572872 | tf_op jit(solution)/shard_map/ppermute | solution.py:20
  82.7 16.1 %collective-permute-start.40 = (f32[8,32,512]{2,1,0:T(8,128)S(1)}, f32[8,32,512]{2,1,0:T(8,128)S(1)}, u32[]{:S(2)}, u32[]{:S(2)}) collective-permute-start(f32[8,32,512]{2,1,0:T(8,128)S(1)} %collective-permute-done.32), channel_id=1, source_target_pairs={{0,1},{1,0},{2,3},{3,2},{4,5},{5,4},{6,7},{7,6},{8,9},{9,8},{10,11... | collective-permute-start | bytes 1572872 | tf_op jit(solution)/shard_map/ppermute | solution.py:20
  85.9 15.3 %collective-permute-start.41 = (f32[8,32,512]{2,1,0:T(8,128)S(1)}, f32[8,32,512]{2,1,0:T(8,128)S(1)}, u32[]{:S(2)}, u32[]{:S(2)}) collective-permute-start(f32[8,32,512]{2,1,0:T(8,128)S(1)} %collective-permute-done.33), channel_id=1, source_target_pairs={{0,1},{1,0},{2,3},{3,2},{4,5},{5,4},{6,7},{7,6},{8,9},{9,8},{10,11... | collective-permute-start | bytes 1572872 | tf_op jit(solution)/shard_map/ppermute | solution.py:20
  91.5 13.7 %collective-permute-start.35 = (f32[8,32,512]{2,1,0:T(8,128)S(1)}, f32[8,32,512]{2,1,0:T(8,128)S(1)}, u32[]{:S(2)}, u32[]{:S(2)}) collective-permute-start(f32[8,32,512]{2,1,0:T(8,128)S(1)} %collective-permute-done.34), channel_id=1, source_target_pairs={{0,1},{1,0},{2,3},{3,2},{4,5},{5,4},{6,7},{7,6},{8,9},{9,8},{10,11... | collective-permute-start | bytes 1572872 | tf_op jit(solution)/shard_map/ppermute | solution.py:20
  93.6 11.6 %collective-permute-start.36 = (f32[8,32,512]{2,1,0:T(8,128)S(1)}, f32[8,32,512]{2,1,0:T(8,128)S(1)}, u32[]{:S(2)}, u32[]{:S(2)}) collective-permute-start(f32[8,32,512]{2,1,0:T(8,128)S(1)} %collective-permute-done.31.refs_0_), channel_id=1, source_target_pairs={{0,16},{1,113},{16,32},{17,1},{32,48},{33,17},{48,64},{49,33},{64,... | collective-permute-start | bytes 1572872 | tf_op jit(solution)/shard_map/ppermute | solution.py:28
  95.3 15.2 %collective-permute-start.10 = (f32[16,32,512]{2,1,0:T(8,128)S(1)}, f32[16,32,512]{2,1,0:T(8,128)S(1)}, u32[]{:S(2)}, u32[]{:S(2)}) collective-permute-start(f32[16,32,512]{2,1,0:T(8,128)S(1)} %pad_maximum_fusion.refs_0_), channel_id=1, source_target_pairs={{0,4},{1,13},{4,8},{5,1},{8,12},{9,5},{12,0},{13,9},{2,6},{3,15},{... | collective-permute-start | bytes 3145736 | tf_op jit(solution)/shard_map/ppermute | solution.py:28
  98.8 23.0 %collective-permute-start.12 = (f32[16,32,512]{2,1,0:T(8,128)S(1)}, f32[16,32,512]{2,1,0:T(8,128)S(1)}, u32[]{:S(2)}, u32[]{:S(2)}) collective-permute-start(f32[16,32,512]{2,1,0:T(8,128)S(1)} %pad_maximum_fusion.1), channel_id=1, source_target_pairs={{0,4},{1,13},{4,8},{5,1},{8,12},{9,5},{12,0},{13,9},{2,6},{3,15},{... | collective-permute-start | bytes 3145736 | tf_op jit(solution)/shard_map/ppermute | solution.py:28
  101.2 4.0 %copy-start = (f32[2,2048,256]{2,1,0:T(8,128)S(1)}, f32[2,2048,256]{2,1,0:T(8,128)}, u32[]{:S(2)}) copy-start(f32[2,2048,256]{2,1,0:T(8,128)} %front_ref.3) | copy-start | bytes 12582916
  108.9 4.7 %collective-permute-start.42 = (f32[512,256]{1,0:T(8,128)S(1)}, f32[512,256]{1,0:T(8,128)S(1)}, u32[]{:S(2)}, u32[]{:S(2)}) collective-permute-start(f32[512,256]{1,0:T(8,128)S(1)} %get-tuple-element.33), channel_id=1, source_target_pairs={{0,1},{1,0},{2,3},{3,2},{4,5},{5,4},{6,7},{7,6},{8,9},{9,8},{10,11... | collective-permute-start | bytes 1572872 | tf_op jit(solution)/shard_map/ppermute | solution.py:20
  110.5 23.6 %collective-permute-start.14 = (f32[16,32,512]{2,1,0:T(8,128)S(1)}, f32[16,32,512]{2,1,0:T(8,128)S(1)}, u32[]{:S(2)}, u32[]{:S(2)}) collective-permute-start(f32[16,32,512]{2,1,0:T(8,128)S(1)} %collective-permute-done.10.refs_1_), channel_id=1, source_target_pairs={{0,4},{1,13},{4,8},{5,1},{8,12},{9,5},{12,0},{13,9},{2,6},{3,15},{... | collective-permute-start | bytes 3145736 | tf_op jit(solution)/shard_map/ppermute | solution.py:28
  113.7 12.7 %collective-permute-start.43 = (f32[512,256]{1,0:T(8,128)S(1)}, f32[512,256]{1,0:T(8,128)S(1)}, u32[]{:S(2)}, u32[]{:S(2)}) collective-permute-start(f32[512,256]{1,0:T(8,128)S(1)} %add.14), channel_id=1, source_target_pairs={{0,2},{2,0},{1,3},{3,1},{4,6},{6,4},{5,7},{7,5},{8,10},{10,8},{9,1... | collective-permute-start | bytes 1572872 | tf_op jit(solution)/shard_map/ppermute | solution.py:20
  121.8 12.3 %collective-permute-start.13 = (f32[16,32,512]{2,1,0:T(8,128)S(1)}, f32[16,32,512]{2,1,0:T(8,128)S(1)}, u32[]{:S(2)}, u32[]{:S(2)}) collective-permute-start(f32[16,32,512]{2,1,0:T(8,128)S(1)} %collective-permute-done.12), channel_id=1, source_target_pairs={{0,1},{1,0},{2,3},{3,2},{4,5},{5,4},{6,7},{7,6},{8,9},{9,8},{10,11... | collective-permute-start | bytes 3145736 | tf_op jit(solution)/shard_map/ppermute | solution.py:20
  126.5 7.6 %collective-permute-start.44 = (f32[512,256]{1,0:T(8,128)S(1)}, f32[512,256]{1,0:T(8,128)S(1)}, u32[]{:S(2)}, u32[]{:S(2)}) collective-permute-start(f32[512,256]{1,0:T(8,128)S(1)} %add.15.refs_5_), channel_id=1, source_target_pairs={{0,1},{1,0},{2,3},{3,2},{4,5},{5,4},{6,7},{7,6},{8,9},{9,8},{10,11... | collective-permute-start | bytes 1572872 | tf_op jit(solution)/shard_map/ppermute | solution.py:20

commit v3 on v2

--- a/solution.py
+++ b/solution.py
@@ -422,8 +422,8 @@
             slot = source(first + piece, False) * 16
             place = piece if first else source(piece, False)
             targets = slot_targets(slot_ref, slot, 16, rows)
-            for i in range(0, 16, 4):
-                subtract_rows(held_ref, update_ref, place * 16 + i, targets[i : i + 4])
+            for i in range(0, 16, 2):
+                subtract_rows(held_ref, update_ref, place * 16 + i, targets[i : i + 2])
 
     copies = store_front(held_ref, out_ref, sem)
     for copy in copies:
@@ -475,8 +475,8 @@
             targets = slot_targets(slot_ref, base, 16, rows)
             if skip is not None:
                 targets = [jnp.where(skip, rows + i % 8, t) for i, t in enumerate(targets)]
-            for i in range(0, 16, 4):
-                subtract_rows(held_ref, update_ref, j * 16 + i, targets[i : i + 4])
+            for i in range(0, 16, 2):
+                subtract_rows(held_ref, update_ref, j * 16 + i, targets[i : i + 2])
 
     @pl.loop(0, 4)
     def _(m):

time: 147 us -> 146 us (level)
  no operation moved by 1% of the time
where the time goes in v3:
time: 146 us
  starting transfers between devices  65.2 us (45%)
  waiting for transfers between devices  45.8 us (31%)
  Pallas kernels  31.7 us (22%)
  local copies, waits for them, and re-layouts  2.46 us (2%)
    ppermute x19, starting transfers between devices, send_apart(): return lax.ppermute(value, (axis, 'c'), pairs)  34.7 us
    ppermute x26, starting transfers between devices, send(): lax.ppermute(value, axis, [(i, (i + shift) % size) for i in range(size)])  30.5 us
    ppermute x19, waiting for transfers between devices, send_apart(): return lax.ppermute(value, (axis, 'c'), pairs)  24.6 us
    ppermute x26, waiting for transfers between devices, send(): lax.ppermute(value, axis, [(i, (i + shift) % size) for i in range(size)])  21.2 us
    pallas_call x1, Pallas kernels, finish(): pl.pallas_call(functools.partial(finish_kernel, len(panels)), in_specs=[S...  11.6 us
    pallas_call x2, Pallas kernels, project(): pl.pallas_call(functools.partial(project_kernel, len(panels), done, first...  7.68 us
    pallas_call x1, Pallas kernels, scatter(): pl.pallas_call(scatter_kernel, grid_spec=pltpu.PrefetchScalarGridSpec(num...  7.66 us
  transfers between devices with their start and end apart: 45, of which 13 were waited for; matrix products, arithmetic and copies ran while one was open for 0% of the time, Pallas kernels for 14%

profile of v3, /device:TPU:1, one launch (start us, length us, event | category | flops | bytes accessed | tf_op | source)
XLA Modules:
  0.0 146.1 jit_solution(18134283288110282895)
XLA Ops:
  0.0 0.9 copy-done.1
  0.9 0.8 copy-done.2
  1.8 3.3 %collective-permute-start = (f32[1,48,512]{2,1,0:T(8,128)S(1)}, f32[1,48,512]{2,1,0:T(8,128)S(1)}, u32[]{:S(2)}, u32[]{:S(2)}) collective-permute-start(f32[1,48,512]{2,1,0:T(8,128)S(1)} %get-tuple-element.20), channel_id=1, source_target_pairs={{0,1},{1,0},{2,3},{3,2},{4,5},{5,4},{6,7},{7,6},{8,9},{9,8},{10,11... | collective-permute-start | bytes 294920 | tf_op jit(solution)/shard_map/ppermute | solution.py:20
  5.1 0.9 collective-permute-done
  6.0 4.4 %collective-permute-start.3 = (f32[2,48,512]{2,1,0:T(8,128)S(1)}, f32[2,48,512]{2,1,0:T(8,128)S(1)}, u32[]{:S(2)}, u32[]{:S(2)}) collective-permute-start(f32[2,48,512]{2,1,0:T(8,128)S(1)} %constant_dynamic-update-slice_fusion.own_ref), channel_id=1, source_target_pairs={{0,32},{1,97},{16,48},{17,113},{32,64},{33,1},{48,80},{49,17},{64,... | collective-permute-start | bytes 589832 | tf_op jit(solution)/shard_map/ppermute | solution.py:28
  10.4 2.9 %collective-permute-start.23 = (f32[1,32,512]{2,1,0:T(8,128)S(1)}, f32[1,32,512]{2,1,0:T(8,128)S(1)}, u32[]{:S(2)}, u32[]{:S(2)}) collective-permute-start(f32[1,32,512]{2,1,0:T(8,128)S(1)} %get-tuple-element.26), channel_id=1, source_target_pairs={{0,128},{128,0},{1,129},{129,1},{2,130},{130,2},{3,131},{131,3},{4... | collective-permute-start | bytes 196616 | tf_op jit(solution)/shard_map/ppermute | solution.py:20
  13.3 0.8 collective-permute-start.1
  14.1 4.1 %collective-permute-start.5 = (f32[2,48,512]{2,1,0:T(8,128)S(1)}, f32[2,48,512]{2,1,0:T(8,128)S(1)}, u32[]{:S(2)}, u32[]{:S(2)}) collective-permute-start(f32[2,48,512]{2,1,0:T(8,128)S(1)} %collective-permute-done.3.refs_2_), channel_id=1, source_target_pairs={{0,16},{1,113},{16,32},{17,1},{32,48},{33,17},{48,64},{49,33},{64,... | collective-permute-start | bytes 589832 | tf_op jit(solution)/shard_map/ppermute | solution.py:28
  18.2 0.1 collective-permute-start.24
  18.3 0.6 copy-done.3
  19.0 0.6 take.1
  19.6 0.6 collective-permute-start.37
  20.2 1.5 %collective-permute-start.7 = (f32[1,48,512]{2,1,0:T(8,128)S(1)}, f32[1,48,512]{2,1,0:T(8,128)S(1)}, u32[]{:S(2)}, u32[]{:S(2)}) collective-permute-start(f32[1,48,512]{2,1,0:T(8,128)S(1)} %slice.14), channel_id=1, source_target_pairs={{0,32},{1,97},{16,48},{17,113},{32,64},{33,1},{48,80},{49,17},{64,... | collective-permute-start | bytes 294920 | tf_op jit(solution)/shard_map/ppermute | solution.py:28
  21.8 0.5 collective-permute-start.2
  22.3 2.5 %collective-permute-done.7.refs_6_ = f32[1,48,512]{2,1,0:T(8,128)S(1)} collective-permute-done((f32[1,48,512]{2,1,0:T(8,128)S(1)}, f32[1,48,512]{2,1,0:T(8,128)S(1)}, u32[]{:S(2)}, u32[]{:S(2)}) %collective-permute-start.7) | collective-permute-done | bytes 98336 | tf_op jit(solution)/shard_map/ppermute | solution.py:28
  24.8 2.8 %collective-permute-start.8 = (f32[1,48,512]{2,1,0:T(8,128)S(1)}, f32[1,48,512]{2,1,0:T(8,128)S(1)}, u32[]{:S(2)}, u32[]{:S(2)}) collective-permute-start(f32[1,48,512]{2,1,0:T(8,128)S(1)} %collective-permute-done.7.refs_6_), channel_id=1, source_target_pairs={{0,1},{1,0},{2,3},{3,2},{4,5},{5,4},{6,7},{7,6},{8,9},{9,8},{10,11... | collective-permute-start | bytes 294920 | tf_op jit(solution)/shard_map/ppermute | solution.py:20
  27.6 0.9 collective-permute-done.8.refs_7_
  28.5 2.3 %collective-permute-start.25 = (f32[4,32,512]{2,1,0:T(8,128)S(1)}, f32[4,32,512]{2,1,0:T(8,128)S(1)}, u32[]{:S(2)}, u32[]{:S(2)}) collective-permute-start(f32[4,32,512]{2,1,0:T(8,128)S(1)} %constant_dynamic-update-slice_fusion.4.own_ref), channel_id=1, source_target_pairs={{0,4},{1,13},{4,8},{5,1},{8,12},{9,5},{12,0},{13,9},{2,6},{3,15},{... | collective-permute-start | bytes 786440 | tf_op jit(solution)/shard_map/ppermute | solution.py:28
  30.9 0.1 pack.2
  31.0 2.9 %collective-permute-start.15 = (f32[8,16,512]{2,1,0:T(8,128)S(1)}, f32[8,16,512]{2,1,0:T(8,128)S(1)}, u32[]{:S(2)}, u32[]{:S(2)}) collective-permute-start(f32[8,16,512]{2,1,0:T(8,128)S(1)} %bitcast.12), channel_id=1, source_target_pairs={{0,128},{128,0},{1,129},{129,1},{2,130},{130,2},{3,131},{131,3},{4... | collective-permute-start | bytes 786440 | tf_op jit(solution)/shard_map/ppermute | solution.py:20
  33.9 0.7 collective-permute-start.27
  34.6 1.8 %collective-permute-start.26 = (f32[4,32,512]{2,1,0:T(8,128)S(1)}, f32[4,32,512]{2,1,0:T(8,128)S(1)}, u32[]{:S(2)}, u32[]{:S(2)}) collective-permute-start(f32[4,32,512]{2,1,0:T(8,128)S(1)} %collective-permute-done.25.refs_0_), channel_id=1, source_target_pairs={{0,1},{1,0},{2,3},{3,2},{4,5},{5,4},{6,7},{7,6},{8,9},{9,8},{10,11... | collective-permute-start | bytes 786440 | tf_op jit(solution)/shard_map/ppermute | solution.py:20
  36.5 2.4 %collective-permute-start.38 = (f32[512,256]{1,0:T(8,128)S(1)}, f32[512,256]{1,0:T(8,128)S(1)}, u32[]{:S(2)}, u32[]{:S(2)}) collective-permute-start(f32[512,256]{1,0:T(8,128)S(1)} %add.12), channel_id=1, source_target_pairs={{0,2},{2,0},{1,3},{3,1},{4,6},{6,4},{5,7},{7,5},{8,10},{10,8},{9,1... | collective-permute-start | bytes 1572872 | tf_op jit(solution)/shard_map/ppermute | solution.py:20
  38.9 3.3 %collective-permute-start.9 = (f32[8,32,512]{2,1,0:T(8,128)S(1)}, f32[8,32,512]{2,1,0:T(8,128)S(1)}, u32[]{:S(2)}, u32[]{:S(2)}) collective-permute-start(f32[8,32,512]{2,1,0:T(8,128)S(1)} %bitcast.9), channel_id=1, source_target_pairs={{0,128},{128,0},{1,129},{129,1},{2,130},{130,2},{3,131},{131,3},{4... | collective-permute-start | bytes 1572872 | tf_op jit(solution)/shard_map/ppermute | solution.py:20
  42.2 1.1 collective-permute-start.28
  43.3 0.3 collective-permute-start.16
  43.6 0.7 collective-permute-done.28.refs_3_
  44.3 0.9 collective-permute-start.32
  45.3 0.8 collective-permute-start.29
  46.1 3.5 %collective-permute-start.17 = (f32[16,16,512]{2,1,0:T(8,128)S(1)}, f32[16,16,512]{2,1,0:T(8,128)S(1)}, u32[]{:S(2)}, u32[]{:S(2)}) collective-permute-start(f32[16,16,512]{2,1,0:T(8,128)S(1)} %pad_maximum_fusion.2.refs_0_), channel_id=1, source_target_pairs={{0,4},{1,13},{4,8},{5,1},{8,12},{9,5},{12,0},{13,9},{2,6},{3,15},{... | collective-permute-start | bytes 1572872 | tf_op jit(solution)/shard_map/ppermute | solution.py:28
  49.7 3.9 %collective-permute-done.38 = f32[512,256]{1,0:T(8,128)S(1)} collective-permute-done((f32[512,256]{1,0:T(8,128)S(1)}, f32[512,256]{1,0:T(8,128)S(1)}, u32[]{:S(2)}, u32[]{:S(2)}) %collective-permute-start.38) | collective-permute-done | bytes 524320 | tf_op jit(solution)/shard_map/ppermute | solution.py:20
  53.6 11.3 %collective-permute-done.9 = f32[8,32,512]{2,1,0:T(8,128)S(1)} collective-permute-done((f32[8,32,512]{2,1,0:T(8,128)S(1)}, f32[8,32,512]{2,1,0:T(8,128)S(1)}, u32[]{:S(2)}, u32[]{:S(2)}) %collective-permute-start.9) | collective-permute-done | bytes 524320 | tf_op jit(solution)/shard_map/ppermute | solution.py:20
  64.9 1.4 collective-permute-start.11
  66.3 0.8 collective-permute-start.33
  67.2 0.8 collective-permute-start.30
  68.0 3.4 %collective-permute-start.21 = (f32[16,16,512]{2,1,0:T(8,128)S(1)}, f32[16,16,512]{2,1,0:T(8,128)S(1)}, u32[]{:S(2)}, u32[]{:S(2)}) collective-permute-start(f32[16,16,512]{2,1,0:T(8,128)S(1)} %collective-permute-done.17.refs_2_), channel_id=1, source_target_pairs={{0,4},{1,13},{4,8},{5,1},{8,12},{9,5},{12,0},{13,9},{2,6},{3,15},{... | collective-permute-start | bytes 1572872 | tf_op jit(solution)/shard_map/ppermute | solution.py:28
  71.4 0.5 collective-permute-start.19
  71.9 2.7 %collective-permute-done.33 = f32[8,32,512]{2,1,0:T(8,128)S(1)} collective-permute-done((f32[8,32,512]{2,1,0:T(8,128)S(1)}, f32[8,32,512]{2,1,0:T(8,128)S(1)}, u32[]{:S(2)}, u32[]{:S(2)}) %collective-permute-start.33) | collective-permute-done | bytes 524320 | tf_op jit(solution)/shard_map/ppermute | solution.py:28
  74.6 2.0 %collective-permute-start.34 = (f32[8,32,512]{2,1,0:T(8,128)S(1)}, f32[8,32,512]{2,1,0:T(8,128)S(1)}, u32[]{:S(2)}, u32[]{:S(2)}) collective-permute-start(f32[8,32,512]{2,1,0:T(8,128)S(1)} %collective-permute-done.33), channel_id=1, source_target_pairs={{0,16},{1,113},{16,32},{17,1},{32,48},{33,17},{48,64},{49,33},{64,... | collective-permute-start | bytes 1572872 | tf_op jit(solution)/shard_map/ppermute | solution.py:28
  76.7 3.6 %collective-permute-done.30.refs_3_ = f32[8,32,512]{2,1,0:T(8,128)S(1)} collective-permute-done((f32[8,32,512]{2,1,0:T(8,128)S(1)}, f32[8,32,512]{2,1,0:T(8,128)S(1)}, u32[]{:S(2)}, u32[]{:S(2)}) %collective-permute-start.30) | collective-permute-done | bytes 524320 | tf_op jit(solution)/shard_map/ppermute | solution.py:28
  80.3 1.7 %collective-permute-start.31 = (f32[8,32,512]{2,1,0:T(8,128)S(1)}, f32[8,32,512]{2,1,0:T(8,128)S(1)}, u32[]{:S(2)}, u32[]{:S(2)}) collective-permute-start(f32[8,32,512]{2,1,0:T(8,128)S(1)} %collective-permute-done.30.refs_3_), channel_id=1, source_target_pairs={{0,16},{1,113},{16,32},{17,1},{32,48},{33,17},{48,64},{49,33},{64,... | collective-permute-start | bytes 1572872 | tf_op jit(solution)/shard_map/ppermute | solution.py:28
  82.0 0.3 collective-permute-start.22
  82.4 0.3 collective-permute-start.39
  82.7 0.3 collective-permute-start.40
  83.0 2.8 %collective-permute-done.34 = f32[8,32,512]{2,1,0:T(8,128)S(1)} collective-permute-done((f32[8,32,512]{2,1,0:T(8,128)S(1)}, f32[8,32,512]{2,1,0:T(8,128)S(1)}, u32[]{:S(2)}, u32[]{:S(2)}) %collective-permute-start.34) | collective-permute-done | bytes 524320 | tf_op jit(solution)/shard_map/ppermute | solution.py:28
  85.9 2.1 %collective-permute-start.41 = (f32[8,32,512]{2,1,0:T(8,128)S(1)}, f32[8,32,512]{2,1,0:T(8,128)S(1)}, u32[]{:S(2)}, u32[]{:S(2)}) collective-permute-start(f32[8,32,512]{2,1,0:T(8,128)S(1)} %collective-permute-done.33), channel_id=1, source_target_pairs={{0,1},{1,0},{2,3},{3,2},{4,5},{5,4},{6,7},{7,6},{8,9},{9,8},{10,11... | collective-permute-start | bytes 1572872 | tf_op jit(solution)/shard_map/ppermute | solution.py:20
  88.0 3.5 %collective-permute-done.31.refs_0_ = f32[8,32,512]{2,1,0:T(8,128)S(1)} collective-permute-done((f32[8,32,512]{2,1,0:T(8,128)S(1)}, f32[8,32,512]{2,1,0:T(8,128)S(1)}, u32[]{:S(2)}, u32[]{:S(2)}) %collective-permute-start.31) | collective-permute-done | bytes 524320 | tf_op jit(solution)/shard_map/ppermute | solution.py:28
  91.5 2.1 %collective-permute-start.35 = (f32[8,32,512]{2,1,0:T(8,128)S(1)}, f32[8,32,512]{2,1,0:T(8,128)S(1)}, u32[]{:S(2)}, u32[]{:S(2)}) collective-permute-start(f32[8,32,512]{2,1,0:T(8,128)S(1)} %collective-permute-done.34), channel_id=1, source_target_pairs={{0,1},{1,0},{2,3},{3,2},{4,5},{5,4},{6,7},{7,6},{8,9},{9,8},{10,11... | collective-permute-start | bytes 1572872 | tf_op jit(solution)/shard_map/ppermute | solution.py:20
  93.7 1.6 %order.1 = (f32[2,512,512]{2,1,0:T(8,128)S(1)}, f32[2,512,512]{2,1,0:T(8,128)S(1)}) custom-call(f32[16,16,512]{2,1,0:T(8,128)S(1)} %pad_maximum_fusion.2.refs_0_, f32[16,16,512]{2,1,0:T(8,128)S(1)} %pad_maximum_fusion.3.refs_1_, f32[16,16,512]{2,1,0:T(8,128)S(1)} %collective-permute-done.17.refs_2_, f32[16,16,512]{2,1,0:T(8,128)S(1)} %collective-permute-done.18.refs_3_, ...), custom_call_target="tpu_custom_call" | custom-call | bytes 8388608 | tf_op jit(solution)/shard_map/order/pallas_call | solution.py:179
  95.3 3.5 %collective-permute-start.10 = (f32[16,32,512]{2,1,0:T(8,128)S(1)}, f32[16,32,512]{2,1,0:T(8,128)S(1)}, u32[]{:S(2)}, u32[]{:S(2)}) collective-permute-start(f32[16,32,512]{2,1,0:T(8,128)S(1)} %pad_maximum_fusion.refs_0_), channel_id=1, source_target_pairs={{0,4},{1,13},{4,8},{5,1},{8,12},{9,5},{12,0},{13,9},{2,6},{3,15},{... | collective-permute-start | bytes 3145736 | tf_op jit(solution)/shard_map/ppermute | solution.py:28
  98.8 0.1 collective-permute-start.12
  98.9 2.3 %solve.1.refs_5_.refs_3_.solved_ref = f32[2,512,256]{2,1,0:T(8,128)S(1)} custom-call(f32[2,512,512]{2,1,0:T(8,128)S(1)} %get-tuple-element.29.inverse_ref, f32[512,256]{1,0:T(8,128)S(1)} %add.13.mine_ref, f32[512,256]{1,0:T(8,128)S(1)} %collective-permute-done.39.other_ref), custom_call_target="tpu_custom_call" | custom-call | flops 3221225472 | bytes 6291456 | tf_op jit(solution)/shard_map/solve/pallas_call | solution.py:232
  101.2 4.0 %project.2.refs_4_.early_ref = f32[1024,512]{1,0:T(8,128)S(1)} custom-call(s32[2]{0:T(128)S(1)} %copy-done.3, s32[1024]{0:T(1024)S(1)} %bitcast.14, f32[8,32,512]{2,1,0:T(8,128)S(1)} %bitcast.19, f32[8,32,512]{2,1,0:T(8,128)S(1)} %collective-permute-done.29.refs_1_, f32[8,32,512]{2,1,0:T(8,128)S(1)} %collective-permute-done.40.refs_2_, ...), custom_call_target="tpu_custom_call" | custom-call | flops 1610612736 | bytes 6291456 | tf_op jit(solution)/shard_map/project/pallas_call | solution.py:358
  105.2 3.7 %project.3 = (f32[384,512]{1,0:T(8,128)S(1)}, f32[512,256]{1,0:T(8,128)S(1)}, f32[512,256]{1,0:T(8,128)S(1)}) custom-call(s32[2]{0:T(128)S(1)} %copy-done.3, s32[1024]{0:T(1024)S(1)} %bitcast.15, f32[8,32,512]{2,1,0:T(8,128)S(1)} %collective-permute-done.31.refs_0_, f32[8,32,512]{2,1,0:T(8,128)S(1)} %collective-permute-done.35.refs_1_, ...), custom_call_target="tpu_custom_call" | custom-call | flops 1610612736 | bytes 6291456 | tf_op jit(solution)/shard_map/project/pallas_call | solution.py:358
  108.9 0.1 collective-permute-start.42
  109.0 1.5 %collective-permute-done.10.refs_1_ = f32[16,32,512]{2,1,0:T(8,128)S(1)} collective-permute-done((f32[16,32,512]{2,1,0:T(8,128)S(1)}, f32[16,32,512]{2,1,0:T(8,128)S(1)}, u32[]{:S(2)}, u32[]{:S(2)}) %collective-permute-start.10) | collective-permute-done | bytes 1048608 | tf_op jit(solution)/shard_map/ppermute | solution.py:28
  110.5 3.1 %collective-permute-start.14 = (f32[16,32,512]{2,1,0:T(8,128)S(1)}, f32[16,32,512]{2,1,0:T(8,128)S(1)}, u32[]{:S(2)}, u32[]{:S(2)}) collective-permute-start(f32[16,32,512]{2,1,0:T(8,128)S(1)} %collective-permute-done.10.refs_1_), channel_id=1, source_target_pairs={{0,4},{1,13},{4,8},{5,1},{8,12},{9,5},{12,0},{13,9},{2,6},{3,15},{... | collective-permute-start | bytes 3145736 | tf_op jit(solution)/shard_map/ppermute | solution.py:28
  113.7 0.1 collective-permute-start.43
  113.8 7.9 %collective-permute-done.12 = f32[16,32,512]{2,1,0:T(8,128)S(1)} collective-permute-done((f32[16,32,512]{2,1,0:T(8,128)S(1)}, f32[16,32,512]{2,1,0:T(8,128)S(1)}, u32[]{:S(2)}, u32[]{:S(2)}) %collective-permute-start.12) | collective-permute-done | bytes 1048608 | tf_op jit(solution)/shard_map/ppermute | solution.py:28
  121.8 1.3 collective-permute-start.13
  123.1 3.3 %collective-permute-done.43 = f32[512,256]{1,0:T(8,128)S(1)} collective-permute-done((f32[512,256]{1,0:T(8,128)S(1)}, f32[512,256]{1,0:T(8,128)S(1)}, u32[]{:S(2)}, u32[]{:S(2)}) %collective-permute-start.43) | collective-permute-done | bytes 524320 | tf_op jit(solution)/shard_map/ppermute | solution.py:20
  126.5 0.1 collective-permute-start.44
  126.6 7.7 %scatter.1.refs_7_ = f32[2,2048,256]{2,1,0:T(8,128)S(1)} custom-call(s32[2]{0:T(128)S(1)} %copy-done.3, s32[1024]{0:T(1024)S(1)} %bitcast.16, f32[2,2048,256]{2,1,0:T(8,128)S(1)} %copy-done, f32[1024,512]{1,0:T(8,128)S(1)} %project.2.refs_4_.early_ref, f32[384,512]{1,0:T(8,128)S(1)} %get-tuple-element.34.late_ref, ...), custom_call_target="tpu_custom_call" | custom-call | flops 1048576 | bytes 25165824 | tf_op jit(solution)/shard_map/scatter/pallas_call | solution.py:437
  134.3 11.6 %finish.1 = f32[2,2048,256]{2,1,0:T(8,128)} custom-call(s32[2]{0:T(128)S(1)} %copy-done.3, s32[1024]{0:T(1024)S(1)} %bitcast.17, f32[16,32,512]{2,1,0:T(8,128)S(1)} %pad_maximum_fusion.refs_0_, f32[16,32,512]{2,1,0:T(8,128)S(1)} %collective-permute-done.10.refs_1_, f32[16,32,512]{2,1,0:T(8,128)S(1)} %collective-permute-done.13.refs_2_, ...), custom_call_target="tpu_custom_call" | custom-call | flops 4831838208 | bytes 13631488 | tf_op jit(solution)/shard_map/finish/pallas_call | solution.py:499
  (61 shorter events, 0.8 us)
Async XLA Ops:
  0.0 0.9 copy-start.1
  0.9 0.8 copy-start.2
  1.8 4.2 %collective-permute-start = (f32[1,48,512]{2,1,0:T(8,128)S(1)}, f32[1,48,512]{2,1,0:T(8,128)S(1)}, u32[]{:S(2)}, u32[]{:S(2)}) collective-permute-start(f32[1,48,512]{2,1,0:T(8,128)S(1)} %get-tuple-element.20), channel_id=1, source_target_pairs={{0,1},{1,0},{2,3},{3,2},{4,5},{5,4},{6,7},{7,6},{8,9},{9,8},{10,11... | collective-permute-start | bytes 294920 | tf_op jit(solution)/shard_map/ppermute | solution.py:20
  6.0 8.1 %collective-permute-start.3 = (f32[2,48,512]{2,1,0:T(8,128)S(1)}, f32[2,48,512]{2,1,0:T(8,128)S(1)}, u32[]{:S(2)}, u32[]{:S(2)}) collective-permute-start(f32[2,48,512]{2,1,0:T(8,128)S(1)} %constant_dynamic-update-slice_fusion.own_ref), channel_id=1, source_target_pairs={{0,32},{1,97},{16,48},{17,113},{32,64},{33,1},{48,80},{49,17},{64,... | collective-permute-start | bytes 589832 | tf_op jit(solution)/shard_map/ppermute | solution.py:28
  10.4 7.8 %collective-permute-start.23 = (f32[1,32,512]{2,1,0:T(8,128)S(1)}, f32[1,32,512]{2,1,0:T(8,128)S(1)}, u32[]{:S(2)}, u32[]{:S(2)}) collective-permute-start(f32[1,32,512]{2,1,0:T(8,128)S(1)} %get-tuple-element.26), channel_id=1, source_target_pairs={{0,128},{128,0},{1,129},{129,1},{2,130},{130,2},{3,131},{131,3},{4... | collective-permute-start | bytes 196616 | tf_op jit(solution)/shard_map/ppermute | solution.py:20
  13.3 8.4 %collective-permute-start.1 = (f32[2,48,512]{2,1,0:T(8,128)S(1)}, f32[2,48,512]{2,1,0:T(8,128)S(1)}, u32[]{:S(2)}, u32[]{:S(2)}) collective-permute-start(f32[2,48,512]{2,1,0:T(8,128)S(1)} %constant_dynamic-update-slice_fusion.own_ref), channel_id=1, source_target_pairs={{0,16},{1,113},{16,32},{17,1},{32,48},{33,17},{48,64},{49,33},{64,... | collective-permute-start | bytes 589832 | tf_op jit(solution)/shard_map/ppermute | solution.py:28
  14.1 13.4 %collective-permute-start.5 = (f32[2,48,512]{2,1,0:T(8,128)S(1)}, f32[2,48,512]{2,1,0:T(8,128)S(1)}, u32[]{:S(2)}, u32[]{:S(2)}) collective-permute-start(f32[2,48,512]{2,1,0:T(8,128)S(1)} %collective-permute-done.3.refs_2_), channel_id=1, source_target_pairs={{0,16},{1,113},{16,32},{17,1},{32,48},{33,17},{48,64},{49,33},{64,... | collective-permute-start | bytes 589832 | tf_op jit(solution)/shard_map/ppermute | solution.py:28
  18.2 3.5 %collective-permute-start.24 = (f32[2,32,512]{2,1,0:T(8,128)S(1)}, f32[2,32,512]{2,1,0:T(8,128)S(1)}, u32[]{:S(2)}, u32[]{:S(2)}) collective-permute-start(f32[2,32,512]{2,1,0:T(8,128)S(1)} %get-tuple-element.35), channel_id=1, source_target_pairs={{0,1},{1,0},{2,3},{3,2},{4,5},{5,4},{6,7},{7,6},{8,9},{9,8},{10,11... | collective-permute-start | bytes 393224 | tf_op jit(solution)/shard_map/ppermute | solution.py:20
  18.3 0.7 copy-start.3
  19.6 63.4 %copy-start.4 = (s32[2,1024]{1,0:T(2,128)S(1)}, s32[2,1024]{1,0:T(2,128)}, u32[]{:S(2)}) copy-start(s32[2,1024]{1,0:T(2,128)} %param.8) | copy-start | bytes 24580
  19.6 16.8 %collective-permute-start.37 = (f32[512,256]{1,0:T(8,128)S(1)}, f32[512,256]{1,0:T(8,128)S(1)}, u32[]{:S(2)}, u32[]{:S(2)}) collective-permute-start(f32[512,256]{1,0:T(8,128)S(1)} %get-tuple-element.31), channel_id=1, source_target_pairs={{0,1},{1,0},{2,3},{3,2},{4,5},{5,4},{6,7},{7,6},{8,9},{9,8},{10,11... | collective-permute-start | bytes 1572872 | tf_op jit(solution)/shard_map/ppermute | solution.py:20
  20.2 4.5 %collective-permute-start.7 = (f32[1,48,512]{2,1,0:T(8,128)S(1)}, f32[1,48,512]{2,1,0:T(8,128)S(1)}, u32[]{:S(2)}, u32[]{:S(2)}) collective-permute-start(f32[1,48,512]{2,1,0:T(8,128)S(1)} %slice.14), channel_id=1, source_target_pairs={{0,32},{1,97},{16,48},{17,113},{32,64},{33,1},{48,80},{49,17},{64,... | collective-permute-start | bytes 294920 | tf_op jit(solution)/shard_map/ppermute | solution.py:28
  21.8 9.1 %collective-permute-start.4 = (f32[2,48,512]{2,1,0:T(8,128)S(1)}, f32[2,48,512]{2,1,0:T(8,128)S(1)}, u32[]{:S(2)}, u32[]{:S(2)}) collective-permute-start(f32[2,48,512]{2,1,0:T(8,128)S(1)} %collective-permute-done.3.refs_2_), channel_id=1, source_target_pairs={{0,1},{1,0},{2,3},{3,2},{4,5},{5,4},{6,7},{7,6},{8,9},{9,8},{10,11... | collective-permute-start | bytes 589832 | tf_op jit(solution)/shard_map/ppermute | solution.py:20
  21.8 9.1 %collective-permute-start.2 = (f32[2,48,512]{2,1,0:T(8,128)S(1)}, f32[2,48,512]{2,1,0:T(8,128)S(1)}, u32[]{:S(2)}, u32[]{:S(2)}) collective-permute-start(f32[2,48,512]{2,1,0:T(8,128)S(1)} %collective-permute-done.1.refs_0_), channel_id=1, source_target_pairs={{0,1},{1,0},{2,3},{3,2},{4,5},{5,4},{6,7},{7,6},{8,9},{9,8},{10,11... | collective-permute-start | bytes 589832 | tf_op jit(solution)/shard_map/ppermute | solution.py:20
  24.8 3.8 %collective-permute-start.8 = (f32[1,48,512]{2,1,0:T(8,128)S(1)}, f32[1,48,512]{2,1,0:T(8,128)S(1)}, u32[]{:S(2)}, u32[]{:S(2)}) collective-permute-start(f32[1,48,512]{2,1,0:T(8,128)S(1)} %collective-permute-done.7.refs_6_), channel_id=1, source_target_pairs={{0,1},{1,0},{2,3},{3,2},{4,5},{5,4},{6,7},{7,6},{8,9},{9,8},{10,11... | collective-permute-start | bytes 294920 | tf_op jit(solution)/shard_map/ppermute | solution.py:20
  27.6 3.3 %collective-permute-start.6 = (f32[2,48,512]{2,1,0:T(8,128)S(1)}, f32[2,48,512]{2,1,0:T(8,128)S(1)}, u32[]{:S(2)}, u32[]{:S(2)}) collective-permute-start(f32[2,48,512]{2,1,0:T(8,128)S(1)} %collective-permute-done.5.refs_4_), channel_id=1, source_target_pairs={{0,1},{1,0},{2,3},{3,2},{4,5},{5,4},{6,7},{7,6},{8,9},{9,8},{10,11... | collective-permute-start | bytes 589832 | tf_op jit(solution)/shard_map/ppermute | solution.py:20
  28.5 6.1 %collective-permute-start.25 = (f32[4,32,512]{2,1,0:T(8,128)S(1)}, f32[4,32,512]{2,1,0:T(8,128)S(1)}, u32[]{:S(2)}, u32[]{:S(2)}) collective-permute-start(f32[4,32,512]{2,1,0:T(8,128)S(1)} %constant_dynamic-update-slice_fusion.4.own_ref), channel_id=1, source_target_pairs={{0,4},{1,13},{4,8},{5,1},{8,12},{9,5},{12,0},{13,9},{2,6},{3,15},{... | collective-permute-start | bytes 786440 | tf_op jit(solution)/shard_map/ppermute | solution.py:28
  31.0 12.3 %collective-permute-start.15 = (f32[8,16,512]{2,1,0:T(8,128)S(1)}, f32[8,16,512]{2,1,0:T(8,128)S(1)}, u32[]{:S(2)}, u32[]{:S(2)}) collective-permute-start(f32[8,16,512]{2,1,0:T(8,128)S(1)} %bitcast.12), channel_id=1, source_target_pairs={{0,128},{128,0},{1,129},{129,1},{2,130},{130,2},{3,131},{131,3},{4... | collective-permute-start | bytes 786440 | tf_op jit(solution)/shard_map/ppermute | solution.py:20
  33.9 8.3 %collective-permute-start.27 = (f32[2,32,512]{2,1,0:T(8,128)S(1)}, f32[2,32,512]{2,1,0:T(8,128)S(1)}, u32[]{:S(2)}, u32[]{:S(2)}) collective-permute-start(f32[2,32,512]{2,1,0:T(8,128)S(1)} %get-tuple-element.35), channel_id=1, source_target_pairs={{0,8},{1,9},{4,12},{5,13},{8,0},{9,1},{12,4},{13,5},{2,10},{3,11},... | collective-permute-start | bytes 393224 | tf_op jit(solution)/shard_map/ppermute | solution.py:28
  34.6 9.6 %collective-permute-start.26 = (f32[4,32,512]{2,1,0:T(8,128)S(1)}, f32[4,32,512]{2,1,0:T(8,128)S(1)}, u32[]{:S(2)}, u32[]{:S(2)}) collective-permute-start(f32[4,32,512]{2,1,0:T(8,128)S(1)} %collective-permute-done.25.refs_0_), channel_id=1, source_target_pairs={{0,1},{1,0},{2,3},{3,2},{4,5},{5,4},{6,7},{7,6},{8,9},{9,8},{10,11... | collective-permute-start | bytes 786440 | tf_op jit(solution)/shard_map/ppermute | solution.py:20
  36.5 17.1 %collective-permute-start.38 = (f32[512,256]{1,0:T(8,128)S(1)}, f32[512,256]{1,0:T(8,128)S(1)}, u32[]{:S(2)}, u32[]{:S(2)}) collective-permute-start(f32[512,256]{1,0:T(8,128)S(1)} %add.12), channel_id=1, source_target_pairs={{0,2},{2,0},{1,3},{3,1},{4,6},{6,4},{5,7},{7,5},{8,10},{10,8},{9,1... | collective-permute-start | bytes 1572872 | tf_op jit(solution)/shard_map/ppermute | solution.py:20
  38.9 26.0 %collective-permute-start.9 = (f32[8,32,512]{2,1,0:T(8,128)S(1)}, f32[8,32,512]{2,1,0:T(8,128)S(1)}, u32[]{:S(2)}, u32[]{:S(2)}) collective-permute-start(f32[8,32,512]{2,1,0:T(8,128)S(1)} %bitcast.9), channel_id=1, source_target_pairs={{0,128},{128,0},{1,129},{129,1},{2,130},{130,2},{3,131},{131,3},{4... | collective-permute-start | bytes 1572872 | tf_op jit(solution)/shard_map/ppermute | solution.py:20
  42.2 2.1 %collective-permute-start.28 = (f32[2,32,512]{2,1,0:T(8,128)S(1)}, f32[2,32,512]{2,1,0:T(8,128)S(1)}, u32[]{:S(2)}, u32[]{:S(2)}) collective-permute-start(f32[2,32,512]{2,1,0:T(8,128)S(1)} %collective-permute-done.27.refs_2_), channel_id=1, source_target_pairs={{0,1},{1,0},{2,3},{3,2},{4,5},{5,4},{6,7},{7,6},{8,9},{9,8},{10,11... | collective-permute-start | bytes 393224 | tf_op jit(solution)/shard_map/ppermute | solution.py:20
  43.3 2.9 %collective-permute-start.16 = (f32[8,16,512]{2,1,0:T(8,128)S(1)}, f32[8,16,512]{2,1,0:T(8,128)S(1)}, u32[]{:S(2)}, u32[]{:S(2)}) collective-permute-start(f32[8,16,512]{2,1,0:T(8,128)S(1)} %collective-permute-done.15), channel_id=1, source_target_pairs={{0,1},{1,0},{2,3},{3,2},{4,5},{5,4},{6,7},{7,6},{8,9},{9,8},{10,11... | collective-permute-start | bytes 786440 | tf_op jit(solution)/shard_map/ppermute | solution.py:20
  44.3 22.0 %collective-permute-start.32 = (f32[8,32,512]{2,1,0:T(8,128)S(1)}, f32[8,32,512]{2,1,0:T(8,128)S(1)}, u32[]{:S(2)}, u32[]{:S(2)}) collective-permute-start(f32[8,32,512]{2,1,0:T(8,128)S(1)} %bitcast.20), channel_id=1, source_target_pairs={{0,16},{1,113},{16,32},{17,1},{32,48},{33,17},{48,64},{49,33},{64,... | collective-permute-start | bytes 1572872 | tf_op jit(solution)/shard_map/ppermute | solution.py:28
  45.3 21.9 %collective-permute-start.29 = (f32[8,32,512]{2,1,0:T(8,128)S(1)}, f32[8,32,512]{2,1,0:T(8,128)S(1)}, u32[]{:S(2)}, u32[]{:S(2)}) collective-permute-start(f32[8,32,512]{2,1,0:T(8,128)S(1)} %bitcast.18), channel_id=1, source_target_pairs={{0,16},{1,113},{16,32},{17,1},{32,48},{33,17},{48,64},{49,33},{64,... | collective-permute-start | bytes 1572872 | tf_op jit(solution)/shard_map/ppermute | solution.py:28
  46.1 21.8 %collective-permute-start.17 = (f32[16,16,512]{2,1,0:T(8,128)S(1)}, f32[16,16,512]{2,1,0:T(8,128)S(1)}, u32[]{:S(2)}, u32[]{:S(2)}) collective-permute-start(f32[16,16,512]{2,1,0:T(8,128)S(1)} %pad_maximum_fusion.2.refs_0_), channel_id=1, source_target_pairs={{0,4},{1,13},{4,8},{5,1},{8,12},{9,5},{12,0},{13,9},{2,6},{3,15},{... | collective-permute-start | bytes 1572872 | tf_op jit(solution)/shard_map/ppermute | solution.py:28
  53.6 17.8 %collective-permute-start.18 = (f32[16,16,512]{2,1,0:T(8,128)S(1)}, f32[16,16,512]{2,1,0:T(8,128)S(1)}, u32[]{:S(2)}, u32[]{:S(2)}) collective-permute-start(f32[16,16,512]{2,1,0:T(8,128)S(1)} %pad_maximum_fusion.3.refs_1_), channel_id=1, source_target_pairs={{0,4},{1,13},{4,8},{5,1},{8,12},{9,5},{12,0},{13,9},{2,6},{3,15},{... | collective-permute-start | bytes 1572872 | tf_op jit(solution)/shard_map/ppermute | solution.py:28
  64.9 6.5 %collective-permute-start.11 = (f32[8,32,512]{2,1,0:T(8,128)S(1)}, f32[8,32,512]{2,1,0:T(8,128)S(1)}, u32[]{:S(2)}, u32[]{:S(2)}) collective-permute-start(f32[8,32,512]{2,1,0:T(8,128)S(1)} %collective-permute-done.9), channel_id=1, source_target_pairs={{0,1},{1,0},{2,3},{3,2},{4,5},{5,4},{6,7},{7,6},{8,9},{9,8},{10,11... | collective-permute-start | bytes 1572872 | tf_op jit(solution)/shard_map/ppermute | solution.py:20
  66.3 8.3 %collective-permute-start.33 = (f32[8,32,512]{2,1,0:T(8,128)S(1)}, f32[8,32,512]{2,1,0:T(8,128)S(1)}, u32[]{:S(2)}, u32[]{:S(2)}) collective-permute-start(f32[8,32,512]{2,1,0:T(8,128)S(1)} %collective-permute-done.32), channel_id=1, source_target_pairs={{0,16},{1,113},{16,32},{17,1},{32,48},{33,17},{48,64},{49,33},{64,... | collective-permute-start | bytes 1572872 | tf_op jit(solution)/shard_map/ppermute | solution.py:28
  67.2 13.1 %collective-permute-start.30 = (f32[8,32,512]{2,1,0:T(8,128)S(1)}, f32[8,32,512]{2,1,0:T(8,128)S(1)}, u32[]{:S(2)}, u32[]{:S(2)}) collective-permute-start(f32[8,32,512]{2,1,0:T(8,128)S(1)} %collective-permute-done.29.refs_1_), channel_id=1, source_target_pairs={{0,16},{1,113},{16,32},{17,1},{32,48},{33,17},{48,64},{49,33},{64,... | collective-permute-start | bytes 1572872 | tf_op jit(solution)/shard_map/ppermute | solution.py:28
  68.0 14.0 %collective-permute-start.21 = (f32[16,16,512]{2,1,0:T(8,128)S(1)}, f32[16,16,512]{2,1,0:T(8,128)S(1)}, u32[]{:S(2)}, u32[]{:S(2)}) collective-permute-start(f32[16,16,512]{2,1,0:T(8,128)S(1)} %collective-permute-done.17.refs_2_), channel_id=1, source_target_pairs={{0,4},{1,13},{4,8},{5,1},{8,12},{9,5},{12,0},{13,9},{2,6},{3,15},{... | collective-permute-start | bytes 1572872 | tf_op jit(solution)/shard_map/ppermute | solution.py:28
  71.4 11.0 %collective-permute-start.20 = (f32[16,16,512]{2,1,0:T(8,128)S(1)}, f32[16,16,512]{2,1,0:T(8,128)S(1)}, u32[]{:S(2)}, u32[]{:S(2)}) collective-permute-start(f32[16,16,512]{2,1,0:T(8,128)S(1)} %collective-permute-done.17.refs_2_), channel_id=1, source_target_pairs={{0,1},{1,0},{2,3},{3,2},{4,5},{5,4},{6,7},{7,6},{8,9},{9,8},{10,11... | collective-permute-start | bytes 1572872 | tf_op jit(solution)/shard_map/ppermute | solution.py:20
  71.4 11.3 %collective-permute-start.19 = (f32[16,16,512]{2,1,0:T(8,128)S(1)}, f32[16,16,512]{2,1,0:T(8,128)S(1)}, u32[]{:S(2)}, u32[]{:S(2)}) collective-permute-start(f32[16,16,512]{2,1,0:T(8,128)S(1)} %collective-permute-done.18.refs_3_), channel_id=1, source_target_pairs={{0,1},{1,0},{2,3},{3,2},{4,5},{5,4},{6,7},{7,6},{8,9},{9,8},{10,11... | collective-permute-start | bytes 1572872 | tf_op jit(solution)/shard_map/ppermute | solution.py:20
  74.6 11.2 %collective-permute-start.34 = (f32[8,32,512]{2,1,0:T(8,128)S(1)}, f32[8,32,512]{2,1,0:T(8,128)S(1)}, u32[]{:S(2)}, u32[]{:S(2)}) collective-permute-start(f32[8,32,512]{2,1,0:T(8,128)S(1)} %collective-permute-done.33), channel_id=1, source_target_pairs={{0,16},{1,113},{16,32},{17,1},{32,48},{33,17},{48,64},{49,33},{64,... | collective-permute-start | bytes 1572872 | tf_op jit(solution)/shard_map/ppermute | solution.py:28
  80.3 11.2 %collective-permute-start.31 = (f32[8,32,512]{2,1,0:T(8,128)S(1)}, f32[8,32,512]{2,1,0:T(8,128)S(1)}, u32[]{:S(2)}, u32[]{:S(2)}) collective-permute-start(f32[8,32,512]{2,1,0:T(8,128)S(1)} %collective-permute-done.30.refs_3_), channel_id=1, source_target_pairs={{0,16},{1,113},{16,32},{17,1},{32,48},{33,17},{48,64},{49,33},{64,... | collective-permute-start | bytes 1572872 | tf_op jit(solution)/shard_map/ppermute | solution.py:28
  82.0 11.6 %collective-permute-start.22 = (f32[16,16,512]{2,1,0:T(8,128)S(1)}, f32[16,16,512]{2,1,0:T(8,128)S(1)}, u32[]{:S(2)}, u32[]{:S(2)}) collective-permute-start(f32[16,16,512]{2,1,0:T(8,128)S(1)} %collective-permute-done.21.refs_6_), channel_id=1, source_target_pairs={{0,1},{1,0},{2,3},{3,2},{4,5},{5,4},{6,7},{7,6},{8,9},{9,8},{10,11... | collective-permute-start | bytes 1572872 | tf_op jit(solution)/shard_map/ppermute | solution.py:20
  82.4 12.9 %collective-permute-start.39 = (f32[512,256]{1,0:T(8,128)S(1)}, f32[512,256]{1,0:T(8,128)S(1)}, u32[]{:S(2)}, u32[]{:S(2)}) collective-permute-start(f32[512,256]{1,0:T(8,128)S(1)} %add.13.mine_ref), channel_id=1, source_target_pairs={{0,1},{1,0},{2,3},{3,2},{4,5},{5,4},{6,7},{7,6},{8,9},{9,8},{10,11... | collective-permute-start | bytes 1572872 | tf_op jit(solution)/shard_map/ppermute | solution.py:20
  82.7 16.1 %collective-permute-start.40 = (f32[8,32,512]{2,1,0:T(8,128)S(1)}, f32[8,32,512]{2,1,0:T(8,128)S(1)}, u32[]{:S(2)}, u32[]{:S(2)}) collective-permute-start(f32[8,32,512]{2,1,0:T(8,128)S(1)} %collective-permute-done.32), channel_id=1, source_target_pairs={{0,1},{1,0},{2,3},{3,2},{4,5},{5,4},{6,7},{7,6},{8,9},{9,8},{10,11... | collective-permute-start | bytes 1572872 | tf_op jit(solution)/shard_map/ppermute | solution.py:20
  85.9 15.3 %collective-permute-start.41 = (f32[8,32,512]{2,1,0:T(8,128)S(1)}, f32[8,32,512]{2,1,0:T(8,128)S(1)}, u32[]{:S(2)}, u32[]{:S(2)}) collective-permute-start(f32[8,32,512]{2,1,0:T(8,128)S(1)} %collective-permute-done.33), channel_id=1, source_target_pairs={{0,1},{1,0},{2,3},{3,2},{4,5},{5,4},{6,7},{7,6},{8,9},{9,8},{10,11... | collective-permute-start | bytes 1572872 | tf_op jit(solution)/shard_map/ppermute | solution.py:20
  91.5 13.7 %collective-permute-start.35 = (f32[8,32,512]{2,1,0:T(8,128)S(1)}, f32[8,32,512]{2,1,0:T(8,128)S(1)}, u32[]{:S(2)}, u32[]{:S(2)}) collective-permute-start(f32[8,32,512]{2,1,0:T(8,128)S(1)} %collective-permute-done.34), channel_id=1, source_target_pairs={{0,1},{1,0},{2,3},{3,2},{4,5},{5,4},{6,7},{7,6},{8,9},{9,8},{10,11... | collective-permute-start | bytes 1572872 | tf_op jit(solution)/shard_map/ppermute | solution.py:20
  93.6 11.6 %collective-permute-start.36 = (f32[8,32,512]{2,1,0:T(8,128)S(1)}, f32[8,32,512]{2,1,0:T(8,128)S(1)}, u32[]{:S(2)}, u32[]{:S(2)}) collective-permute-start(f32[8,32,512]{2,1,0:T(8,128)S(1)} %collective-permute-done.31.refs_0_), channel_id=1, source_target_pairs={{0,16},{1,113},{16,32},{17,1},{32,48},{33,17},{48,64},{49,33},{64,... | collective-permute-start | bytes 1572872 | tf_op jit(solution)/shard_map/ppermute | solution.py:28
  95.3 15.2 %collective-permute-start.10 = (f32[16,32,512]{2,1,0:T(8,128)S(1)}, f32[16,32,512]{2,1,0:T(8,128)S(1)}, u32[]{:S(2)}, u32[]{:S(2)}) collective-permute-start(f32[16,32,512]{2,1,0:T(8,128)S(1)} %pad_maximum_fusion.refs_0_), channel_id=1, source_target_pairs={{0,4},{1,13},{4,8},{5,1},{8,12},{9,5},{12,0},{13,9},{2,6},{3,15},{... | collective-permute-start | bytes 3145736 | tf_op jit(solution)/shard_map/ppermute | solution.py:28
  98.8 23.0 %collective-permute-start.12 = (f32[16,32,512]{2,1,0:T(8,128)S(1)}, f32[16,32,512]{2,1,0:T(8,128)S(1)}, u32[]{:S(2)}, u32[]{:S(2)}) collective-permute-start(f32[16,32,512]{2,1,0:T(8,128)S(1)} %pad_maximum_fusion.1), channel_id=1, source_target_pairs={{0,4},{1,13},{4,8},{5,1},{8,12},{9,5},{12,0},{13,9},{2,6},{3,15},{... | collective-permute-start | bytes 3145736 | tf_op jit(solution)/shard_map/ppermute | solution.py:28
  101.2 4.0 %copy-start = (f32[2,2048,256]{2,1,0:T(8,128)S(1)}, f32[2,2048,256]{2,1,0:T(8,128)}, u32[]{:S(2)}) copy-start(f32[2,2048,256]{2,1,0:T(8,128)} %front_ref.3) | copy-start | bytes 12582916
  108.9 4.7 %collective-permute-start.42 = (f32[512,256]{1,0:T(8,128)S(1)}, f32[512,256]{1,0:T(8,128)S(1)}, u32[]{:S(2)}, u32[]{:S(2)}) collective-permute-start(f32[512,256]{1,0:T(8,128)S(1)} %get-tuple-element.33), channel_id=1, source_target_pairs={{0,1},{1,0},{2,3},{3,2},{4,5},{5,4},{6,7},{7,6},{8,9},{9,8},{10,11... | collective-permute-start | bytes 1572872 | tf_op jit(solution)/shard_map/ppermute | solution.py:20
  110.5 23.7 %collective-permute-start.14 = (f32[16,32,512]{2,1,0:T(8,128)S(1)}, f32[16,32,512]{2,1,0:T(8,128)S(1)}, u32[]{:S(2)}, u32[]{:S(2)}) collective-permute-start(f32[16,32,512]{2,1,0:T(8,128)S(1)} %collective-permute-done.10.refs_1_), channel_id=1, source_target_pairs={{0,4},{1,13},{4,8},{5,1},{8,12},{9,5},{12,0},{13,9},{2,6},{3,15},{... | collective-permute-start | bytes 3145736 | tf_op jit(solution)/shard_map/ppermute | solution.py:28
  113.7 12.7 %collective-permute-start.43 = (f32[512,256]{1,0:T(8,128)S(1)}, f32[512,256]{1,0:T(8,128)S(1)}, u32[]{:S(2)}, u32[]{:S(2)}) collective-permute-start(f32[512,256]{1,0:T(8,128)S(1)} %add.14), channel_id=1, source_target_pairs={{0,2},{2,0},{1,3},{3,1},{4,6},{6,4},{5,7},{7,5},{8,10},{10,8},{9,1... | collective-permute-start | bytes 1572872 | tf_op jit(solution)/shard_map/ppermute | solution.py:20
  121.8 12.5 %collective-permute-start.13 = (f32[16,32,512]{2,1,0:T(8,128)S(1)}, f32[16,32,512]{2,1,0:T(8,128)S(1)}, u32[]{:S(2)}, u32[]{:S(2)}) collective-permute-start(f32[16,32,512]{2,1,0:T(8,128)S(1)} %collective-permute-done.12), channel_id=1, source_target_pairs={{0,1},{1,0},{2,3},{3,2},{4,5},{5,4},{6,7},{7,6},{8,9},{9,8},{10,11... | collective-permute-start | bytes 3145736 | tf_op jit(solution)/shard_map/ppermute | solution.py:20
  126.5 7.8 %collective-permute-start.44 = (f32[512,256]{1,0:T(8,128)S(1)}, f32[512,256]{1,0:T(8,128)S(1)}, u32[]{:S(2)}, u32[]{:S(2)}) collective-permute-start(f32[512,256]{1,0:T(8,128)S(1)} %add.15.refs_5_), channel_id=1, source_target_pairs={{0,1},{1,0},{2,3},{3,2},{4,5},{5,4},{6,7},{7,6},{8,9},{9,8},{10,11... | collective-permute-start | bytes 1572872 | tf_op jit(solution)/shard_map/ppermute | solution.py:20
